TPU v7x, 128 devices: a whole 4x4x4 slice. The times are simulated.
128 devices in a mesh: dp: 8 (over z, core), expert: 16 (over y, x).
Axes of the slice: x: 4, y: 4, z: 4, core: 2. Of those that a mesh axis runs over, the one named last changes fastest.
Arguments:
- tokens_in: bfloat16 [16384, 4096], P(('dp', 'expert')), may hold values from -6 to 6
- out_grad: bfloat16 [16384, 4096], P(('dp', 'expert')), may hold values from -3 to 3
- expert_ids: int32 [16384, 2], P(('dp', 'expert')), may hold values from 0 to 15, all different within a row; in each aligned block of 128 rows (0 to 127, 128 to 255, ...) at most 32 rows name the same one
- gate_probs: bfloat16 [16384, 2], P(('dp', 'expert')), may hold values from 0.099609375 to 1
- gate_up: bfloat16 [4096, 2, 16, 768], P(None, None, 'expert'), may hold values from -0.09375 to 0.09375
- down_proj: bfloat16 [4096, 16, 768], P(None, 'expert'), may hold values from -0.21875 to 0.21875
Outputs:
- input_grad: bfloat16 [16384, 4096], P(('dp', 'expert'))
- gate_grad: bfloat16 [16384, 2], P(('dp', 'expert'))
- gate_up_grad: bfloat16 [4096, 2, 16, 768], P('dp', None, 'expert')
- down_grad: bfloat16 [4096, 16, 768], P('dp', 'expert')
Inputs may be any that keep to these rules, and one draw needn't show every extreme that they name: `expert_ids`: each row names 2 different experts. The rows of one device name no expert more than 32 times, and in every draw some device's rows name some expert exactly 32 times.
All inputs are finite; a program needn't handle non-finite values.
Results may differ from a plain program's by a relative error of at most 0.017.
Values may be sent and summed in bfloat16 or wider, within the bound.
No kernel may reach another device: no remote copies, remote signals or barrier semaphores. Data moves between devices by JAX's collectives and lax.ppermute only.
A program may use at most 192 MiB of HBM per device.

v0:
```python
import jax
import jax.numpy as jnp
from jax import lax
from jax.sharding import PartitionSpec as P


def body(tokens_in, out_grad, expert_ids, gate_probs, gate_up, down_proj):
    tok_dev, top_win = expert_ids.shape
    width = tokens_in.shape[1]
    owners = lax.axis_size("expert")
    local_experts = gate_up.shape[2]
    experts = local_experts * owners
    capacity = max(2, 2 * tok_dev * top_win // experts)
    assign = tok_dev * top_win
    slots = experts * capacity
    flat_ids = expert_ids.reshape(assign)
    onehot = (flat_ids[:, None] == jnp.arange(experts, dtype=jnp.int32)[None, :]).astype(jnp.int32)
    placed = jnp.sum((jnp.cumsum(onehot, axis=0) - onehot) * onehot, axis=1)
    slot_of = flat_ids * capacity + placed
    filler = (
        jnp.full((slots,), assign, jnp.int32).at[slot_of].set(jnp.arange(assign, dtype=jnp.int32))
    )
    token_of = filler // top_win
    tokens_pad = jnp.concatenate([tokens_in, jnp.zeros((1, width), jnp.bfloat16)], axis=0)
    grads_pad = jnp.concatenate([out_grad, jnp.zeros((1, width), jnp.bfloat16)], axis=0)
    gates_pad = jnp.concatenate([gate_probs.reshape(assign), jnp.zeros((1,), jnp.bfloat16)], axis=0)
    send_rows = tokens_pad[token_of].reshape(owners, local_experts, capacity, width)
    send_grads = grads_pad[token_of].reshape(owners, local_experts, capacity, width)
    send_gates = gates_pad[filler].reshape(owners, local_experts, capacity)
    rowwise_rows_in = lax.all_to_all(send_rows, "expert", split_axis=0, concat_axis=0, tiled=True)
    grads_in = lax.all_to_all(send_grads, "expert", split_axis=0, concat_axis=0, tiled=True)
    gates_in = lax.all_to_all(send_gates, "expert", split_axis=0, concat_axis=0, tiled=True)
    both = jnp.einsum(
        "secd,dgef->secgf", rowwise_rows_in, gate_up, preferred_element_type=jnp.float32
    )
    pre_gate = both[:, :, :, 0, :]
    pre_up = both[:, :, :, 1, :]
    sigmoid_gate = jax.nn.sigmoid(pre_gate)
    activated = pre_gate * sigmoid_gate
    rowwise_product = (activated * pre_up).astype(jnp.bfloat16)
    output_rows = jnp.einsum(
        "secf,def->secd", rowwise_product, down_proj, preferred_element_type=jnp.float32
    )
    gate_rows = jnp.sum(grads_in.astype(jnp.float32) * output_rows, axis=-1).astype(jnp.bfloat16)
    rowwise_scaled = (
        gates_in.astype(jnp.float32)[..., None] * grads_in.astype(jnp.float32)
    ).astype(jnp.bfloat16)
    act_grad = jnp.einsum(
        "secd,def->secf", rowwise_scaled, down_proj, preferred_element_type=jnp.float32
    )
    rowwise_hidden_grads = jnp.stack(
        [
            act_grad * pre_up * sigmoid_gate * (1.0 + pre_gate * (1.0 - sigmoid_gate)),
            act_grad * activated,
        ],
        axis=3,
    ).astype(jnp.bfloat16)
    input_rows = jnp.einsum(
        "secgf,dgef->secd", rowwise_hidden_grads, gate_up, preferred_element_type=jnp.float32
    ).astype(jnp.bfloat16)
    back_rows = lax.all_to_all(input_rows, "expert", split_axis=0, concat_axis=0, tiled=True)
    back_gates = lax.all_to_all(gate_rows, "expert", split_axis=0, concat_axis=0, tiled=True)
    back_rows, back_gates, rows_in, scaled, hidden_grads, product = (
        back_rows,
        back_gates,
        rowwise_rows_in,
        rowwise_scaled,
        rowwise_hidden_grads,
        rowwise_product,
    )
    slot_rows = back_rows.reshape(slots, width)
    slot_gates = back_gates.reshape(slots)
    input_grad = jnp.sum(
        slot_rows[slot_of].reshape(tok_dev, top_win, width).astype(jnp.float32), axis=1
    ).astype(jnp.bfloat16)
    gate_grad = slot_gates[slot_of].reshape(tok_dev, top_win)
    both_part = jnp.einsum(
        "secd,secgf->dgef", rows_in, hidden_grads, preferred_element_type=jnp.float32
    )
    down_part = jnp.einsum("secd,secf->def", scaled, product, preferred_element_type=jnp.float32)
    summed = lax.psum_scatter(
        jnp.concatenate([both_part, down_part[:, None]], axis=1).astype(jnp.bfloat16),
        "dp",
        scatter_dimension=0,
        tiled=True,
    ).astype(jnp.float32)
    gate_up_grad = summed[:, :2].astype(jnp.bfloat16)
    down_grad = summed[:, 2].astype(jnp.bfloat16)
    return (input_grad, gate_grad, gate_up_grad, down_grad)


def solution(mesh):
    placed = (
        P(("dp", "expert"), None),
        P(("dp", "expert"), None),
        P(("dp", "expert"), None),
        P(("dp", "expert"), None),
        P(None, None, "expert", None),
        P(None, "expert", None),
    )
    return jax.shard_map(
        body,
        mesh=mesh,
        in_specs=placed,
        out_specs=(
            P(("dp", "expert"), None),
            P(("dp", "expert"), None),
            P("dp", None, "expert", None),
            P("dp", "expert", None),
        ),
        check_vma=False,
    )
```

profile of v0, /device:TPU:0, one launch (start us, length us, event | category | flops | bytes accessed | tf_op | source)
XLA Modules:
  0.0 312.0 jit_solution(13624418939787632740)
XLA Ops:
  7.2 0.7 broadcast_multiply_fusion
  7.8 0.8 copy.44
  8.6 0.1 eq.29
  8.8 0.1 eq.25
  8.9 0.8 copy.42
  9.7 0.1 reshape.263
  9.9 0.1 copy.43
  10.0 0.1 mul.88
  10.1 0.6 reduce-window.6
  10.7 0.2 slice_reduce_fusion
  10.9 0.1 fusion.45
  11.1 1.4 scatter_custom_fusion
  12.5 3.5 %gather_fusion = bf16[512]{0:T(512)(128)(2,1)S(1)} fusion(bf16[257]{0:T(512)(128)(2,1)S(1)} %pad_maximum_fusion.4, s32[1024]{0:T(1024)S(1)} %get-tuple-element.25), kind=kCustom, calls=%fused_computation | custom fusion | bytes 4096 | tf_op jit(solution)/shard_map/gather | solution.py:29
  16.0 0.7 reshape.335
  16.7 7.1 %all-to-all-start = ((bf16[16,1,32]{2,1,0:T(2,128)(2,1)}), bf16[16,1,32]{2,1,0:T(2,128)(2,1)S(1)}, u32[]{:S(2)}, u32[]{:S(2)}) async-start(bf16[16,1,32]{2,1,0:T(2,128)(2,1)} %reshape.335), calls=%async_computation | async-start | bytes 16384 | tf_op jit(solution)/shard_map/all_to_all | solution.py:32
  23.9 1.3 concatenate.30
  25.2 4.4 %gather_fusion.2 = bf16[512,4096]{1,0:T(8,128)(2,1)} fusion(bf16[129,4096]{1,0:T(8,128)(2,1)S(1)} %concatenate.30, s32[1024]{0:T(1024)S(1)} %get-tuple-element.24), kind=kCustom, calls=%fused_computation.2 | custom fusion | bytes 8390656 | tf_op jit(solution)/shard_map/gather | solution.py:27
  29.6 1.7 all-to-all-done
  31.3 5.7 %all-to-all-start.2 = ((bf16[16,1,32,4096]{3,2,1,0:T(8,128)(2,1)}), bf16[16,1,32,4096]{3,2,1,0:T(8,128)(2,1)}, u32[]{:S(2)}, u32[]{:S(2)}) async-start(bf16[16,1,32,4096]{3,2,1,0:T(8,128)(2,1)} %bitcast.185), calls=%async_computation.2 | async-start | bytes 8388608 | tf_op jit(solution)/shard_map/all_to_all | solution.py:30
  37.0 0.1 concatenate.29
  37.1 4.4 %gather_fusion.1 = bf16[512,4096]{1,0:T(8,128)(2,1)} fusion(bf16[129,4096]{1,0:T(8,128)(2,1)S(1)} %concatenate.29, s32[1024]{0:T(1024)S(1)} %get-tuple-element.24), kind=kCustom, calls=%fused_computation.1 | custom fusion | bytes 8390656 | tf_op jit(solution)/shard_map/gather | solution.py:28
  41.5 57.0 %all-to-all-done.2 = bf16[16,1,32,4096]{3,2,1,0:T(8,128)(2,1)} async-done(((bf16[16,1,32,4096]{3,2,1,0:T(8,128)(2,1)}), bf16[16,1,32,4096]{3,2,1,0:T(8,128)(2,1)}, u32[]{:S(2)}, u32[]{:S(2)}) %all-to-all-start.2) | async-done | bytes 4194336 | tf_op jit(solution)/shard_map/all_to_all | solution.py:30
  98.5 5.0 %all-to-all-start.1 = ((bf16[16,1,32,4096]{3,2,1,0:T(8,128)(2,1)}), bf16[16,1,32,4096]{3,2,1,0:T(8,128)(2,1)}, u32[]{:S(2)}, u32[]{:S(2)}) async-start(bf16[16,1,32,4096]{3,2,1,0:T(8,128)(2,1)} %bitcast.184), calls=%async_computation.1 | async-start | bytes 8388608 | tf_op jit(solution)/shard_map/all_to_all | solution.py:31
  103.5 0.2 reduce-scatter.2.cloned.1.call-start
  103.8 10.7 %fusion.21 = f32[16,1,32,2,768]{4,2,0,3,1:T(8,128)S(1)} fusion(bf16[4096,2,768,1]{2,1,0,3:T(2,128)(2,1)} %bitcast.192, bf16[16,1,32,4096]{3,2,1,0:T(8,128)(2,1)} %all-to-all-done.2), kind=kOutput, calls=%fused_computation.27 | convolution fusion | flops 6442450944 | bytes 19922944 | tf_op jit(solution)/shard_map/secd,dgef->secgf/dot_general | solution.py:33
  114.5 47.2 %all-to-all-done.1 = bf16[16,1,32,4096]{3,2,1,0:T(8,128)(2,1)} async-done(((bf16[16,1,32,4096]{3,2,1,0:T(8,128)(2,1)}), bf16[16,1,32,4096]{3,2,1,0:T(8,128)(2,1)}, u32[]{:S(2)}, u32[]{:S(2)}) %all-to-all-start.1) | async-done | bytes 4194336 | tf_op jit(solution)/shard_map/all_to_all | solution.py:31
  161.7 6.3 %fusion.12 = bf16[4096,1,1,768]{0,3,1,2:T(8,128)(2,1)S(1)} fusion(bf16[16,1,32,4096]{3,2,1,0:T(8,128)(2,1)} %all-to-all-done.1, f32[16,32]{1,0:T(8,128)S(1)} %bitcast.186, f32[16,1,32,2,768]{4,2,0,3,1:T(8,128)S(1)} %fusion.21), kind=kOutput, calls=%fused_computation.22 | convolution fusion | flops 3233021952 | bytes 13633536 | tf_op jit(solution)/shard_map/secd,secf->def/dot_general | solution.py:80
  168.1 7.9 %fusion.42 = (bf16[16,32,1,768]{3,1,0,2:T(8,128)(2,1)S(1)}, bf16[16,32,1,768]{3,1,0,2:T(8,128)(2,1)S(1)}) fusion(f32[16,1,32,2,768]{4,2,0,3,1:T(8,128)S(1)} %fusion.21, bf16[4096,1,768]{2,0,1:T(8,128)(2,1)} %param.11, bf16[16,1,32,4096]{3,2,1,0:T(8,128)(2,1)} %all-to-all-done.1, f32[16,32]{1,0:T(8,128)S(1)} %bitcast.187), kind=kOutput, calls=%fused_computation.54 | convolution fusion | flops 3232628736 | bytes 15206400 | tf_op jit(solution)/shard_map/secd,def->secf/dot_general | solution.py:48
  175.9 9.7 %fusion = bf16[4096,2,1,768]{0,3,1,2:T(8,128)(2,1)S(1)} fusion(bf16[16,1,32,4096]{3,2,1,0:T(8,128)(2,1)} %all-to-all-done.2, bf16[16,32,1,768]{3,1,0,2:T(8,128)(2,1)S(1)} %get-tuple-element.21, bf16[16,32,1,768]{3,1,0,2:T(8,128)(2,1)S(1)} %get-tuple-element.20), kind=kOutput, calls=%fused_computation.8 | convolution fusion | flops 6449528832 | bytes 18350080 | tf_op jit(solution)/shard_map/secd,secgf->dgef/dot_general | solution.py:77
  185.7 10.5 %pad_maximum_fusion = bf16[4096,3,1,768]{0,3,1,2:T(8,128)(2,1)} fusion(bf16[4096,1,1,768]{0,3,1,2:T(8,128)(2,1)S(1)} %fusion.12, bf16[4096,2,1,768]{0,3,1,2:T(8,128)(2,1)S(1)} %fusion), kind=kLoop, calls=%fused_computation.7 | loop fusion | flops 9437184 | bytes 37748736 | tf_op jit(solution)/shard_map/concatenate | solution.py:82
  196.3 0.0 reduce-scatter.2.cloned.1.call-update
  196.3 7.5 %fusion.6 = bf16[16,32]{1,0:T(8,128)(2,1)S(1)} fusion(bf16[4096,1,768]{2,0,1:T(8,128)(2,1)} %param.11, bf16[16,1,32,4096]{3,2,1,0:T(8,128)(2,1)} %all-to-all-done.1, f32[16,1,32,2,768]{4,2,0,3,1:T(8,128)S(1)} %fusion.21), kind=kOutput, calls=%fused_computation.17 | convolution fusion | flops 3229875712 | bytes 13632512 | tf_op jit(solution)/shard_map/secf,def->secd/dot_general | solution.py:41
  203.8 0.6 copy.54
  204.5 4.3 %all-to-all-start.4 = ((bf16[16,1,32]{2,1,0:T(2,128)(2,1)}), bf16[16,1,32]{2,1,0:T(2,128)(2,1)S(1)}, u32[]{:S(2)}, u32[]{:S(2)}) async-start(bf16[16,1,32]{2,1,0:T(2,128)(2,1)} %copy.54), calls=%async_computation.4 | async-start | bytes 16384 | tf_op jit(solution)/shard_map/all_to_all | solution.py:62
  208.7 12.6 %fusion.13 = bf16[16,1,32,4096]{3,2,1,0:T(8,128)(2,1)} fusion(bf16[4096,2,768,1]{2,1,0,3:T(2,128)(2,1)} %bitcast.193, bf16[16,32,1,768]{3,1,0,2:T(8,128)(2,1)} %copy-done.4, bf16[16,32,1,768]{3,1,0,2:T(8,128)(2,1)} %copy-done.3), kind=kOutput, calls=%fused_computation.23 | convolution fusion | flops 6445334528 | bytes 18350080 | tf_op jit(solution)/shard_map/secgf,dgef->secd/dot_general | solution.py:58
  221.3 7.3 %all-to-all-start.3 = ((bf16[16,1,32,4096]{3,2,1,0:T(8,128)(2,1)}), bf16[16,1,32,4096]{3,2,1,0:T(8,128)(2,1)}, u32[]{:S(2)}, u32[]{:S(2)}) async-start(bf16[16,1,32,4096]{3,2,1,0:T(8,128)(2,1)} %fusion.13), calls=%async_computation.3 | async-start | bytes 8388608 | tf_op jit(solution)/shard_map/all_to_all | solution.py:61
  228.6 0.1 reshape.274
  228.7 1.9 gather_fusion.4
  230.6 0.2 reshape.275
  230.8 0.6 copy.55
  231.4 50.1 %all-to-all-done.3 = bf16[16,1,32,4096]{3,2,1,0:T(8,128)(2,1)} async-done(((bf16[16,1,32,4096]{3,2,1,0:T(8,128)(2,1)}), bf16[16,1,32,4096]{3,2,1,0:T(8,128)(2,1)}, u32[]{:S(2)}, u32[]{:S(2)}) %all-to-all-start.3) | async-done | bytes 4194336 | tf_op jit(solution)/shard_map/all_to_all | solution.py:61
  281.5 6.7 %gather_fusion.3 = bf16[256,4096]{1,0:T(8,128)(2,1)S(1)} fusion(bf16[512,4096]{1,0:T(8,128)(2,1)} %bitcast.36, s32[1024]{0:T(1024)S(1)} %pad_clamp_fusion), kind=kCustom, calls=%fused_computation.3 | custom fusion | bytes 4195328 | tf_op jit(solution)/shard_map/gather | solution.py:74
  288.2 2.7 reshape.273
  290.8 7.7 %reduce_sum.34 = bf16[128,4096]{1,0:T(8,128)(2,1)} reduce(bf16[128,2,4096]{2,1,0:T(2,128)(2,1)} %reshape.273, bf16[]{:T(256)} %constant.34.clone.1), dimensions={1}, to_apply=%region_4.5 | reduce | flops 524288 | bytes 3145730 | tf_op jit(solution)/shard_map/reduce_sum | solution.py:73
  298.5 1.4 slice-done
  299.9 2.9 copy.56
  302.8 1.2 slice_bitcast_fusion
  304.0 1.2 copy.57
  (24 shorter events, 0.2 us)
Async XLA Ops:
  11.0 1.5 copy-start.1
  16.7 14.6 %all-to-all-start = ((bf16[16,1,32]{2,1,0:T(2,128)(2,1)}), bf16[16,1,32]{2,1,0:T(2,128)(2,1)S(1)}, u32[]{:S(2)}, u32[]{:S(2)}) async-start(bf16[16,1,32]{2,1,0:T(2,128)(2,1)} %reshape.335), calls=%async_computation | async-start | bytes 16384 | tf_op jit(solution)/shard_map/all_to_all | solution.py:32
  31.3 5.7 %copy-start = (bf16[128,4096]{1,0:T(8,128)(2,1)S(1)}, bf16[128,4096]{1,0:T(8,128)(2,1)}, u32[]{:S(2)}) copy-start(bf16[128,4096]{1,0:T(8,128)(2,1)} %param.7) | copy-start | bytes 3145732
  31.3 67.1 %all-to-all-start.2 = ((bf16[16,1,32,4096]{3,2,1,0:T(8,128)(2,1)}), bf16[16,1,32,4096]{3,2,1,0:T(8,128)(2,1)}, u32[]{:S(2)}, u32[]{:S(2)}) async-start(bf16[16,1,32,4096]{3,2,1,0:T(8,128)(2,1)} %bitcast.185), calls=%async_computation.2 | async-start | bytes 8388608 | tf_op jit(solution)/shard_map/all_to_all | solution.py:30
  98.5 63.2 %all-to-all-start.1 = ((bf16[16,1,32,4096]{3,2,1,0:T(8,128)(2,1)}), bf16[16,1,32,4096]{3,2,1,0:T(8,128)(2,1)}, u32[]{:S(2)}, u32[]{:S(2)}) async-start(bf16[16,1,32,4096]{3,2,1,0:T(8,128)(2,1)} %bitcast.184), calls=%async_computation.1 | async-start | bytes 8388608 | tf_op jit(solution)/shard_map/all_to_all | solution.py:31
  103.5 195.0 %reduce-scatter.2.cloned.1.call-start = ((), (), s32[]{:S(2)}) async-start(), calls=%async_computation.6 | async-start | bytes 21233664 | tf_op jit(solution)/shard_map/reduce_scatter | solution.py:81
  175.9 9.8 %copy-start.3 = (bf16[16,32,1,768]{3,1,0,2:T(8,128)(2,1)}, bf16[16,32,1,768]{3,1,0,2:T(8,128)(2,1)S(1)}, u32[]{:S(2)}) copy-start(bf16[16,32,1,768]{3,1,0,2:T(8,128)(2,1)S(1)} %get-tuple-element.20) | copy-start | bytes 2359300
  175.9 9.8 %copy-start.4 = (bf16[16,32,1,768]{3,1,0,2:T(8,128)(2,1)}, bf16[16,32,1,768]{3,1,0,2:T(8,128)(2,1)S(1)}, u32[]{:S(2)}) copy-start(bf16[16,32,1,768]{3,1,0,2:T(8,128)(2,1)S(1)} %get-tuple-element.21) | copy-start | bytes 2359300
  204.5 16.8 %all-to-all-start.4 = ((bf16[16,1,32]{2,1,0:T(2,128)(2,1)}), bf16[16,1,32]{2,1,0:T(2,128)(2,1)S(1)}, u32[]{:S(2)}, u32[]{:S(2)}) async-start(bf16[16,1,32]{2,1,0:T(2,128)(2,1)} %copy.54), calls=%async_computation.4 | async-start | bytes 16384 | tf_op jit(solution)/shard_map/all_to_all | solution.py:62
  221.3 7.3 %copy-start.2 = (s32[256,1]{0,1:T(1,128)S(1)}, s32[256,1]{0,1:T(1,128)}, u32[]{:S(2)}) copy-start(s32[256,1]{0,1:T(1,128)} %copy-done.1) | copy-start | bytes 3076
  221.3 60.2 %all-to-all-start.3 = ((bf16[16,1,32,4096]{3,2,1,0:T(8,128)(2,1)}), bf16[16,1,32,4096]{3,2,1,0:T(8,128)(2,1)}, u32[]{:S(2)}, u32[]{:S(2)}) async-start(bf16[16,1,32,4096]{3,2,1,0:T(8,128)(2,1)} %fusion.13), calls=%async_computation.3 | async-start | bytes 8388608 | tf_op jit(solution)/shard_map/all_to_all | solution.py:61
  298.5 1.4 slice-start
Sparse Core Ops, SparseCore 0:
  196.4 101.4 reduce-scatter.1
where the time goes:
time: 313 us; the launch traced here: 312 us
  waiting for transfers between devices  156 us (50%)
  matrix products  54.8 us (18%)
  local copies, waits for them, and re-layouts  37.6 us (12%)
  starting transfers between devices  29.5 us (9%)
  other arithmetic  19.7 us (6%)
  between operations  14.3 us (5%)
    all_to_all x1, waiting for transfers between devices, body(): lax.all_to_all(send_rows, 'expert', split_axis=0, concat_axis=0, tiled=True)  57 us
    all_to_all x1, waiting for transfers between devices, body(): lax.all_to_all(input_rows, 'expert', split_axis=0, concat_axis=0, tiled=T...  50.1 us
    all_to_all x1, waiting for transfers between devices, body(): lax.all_to_all(send_grads, 'expert', split_axis=0, concat_axis=0, tiled=T...  47.2 us
    dot_general x1, matrix products, body(): jnp.einsum('secgf,dgef->secd', rowwise_hidden_grads, gate_up, preferred_e...  12.6 us
    dot_general x1, matrix products, body(): jnp.einsum('secd,dgef->secgf', rowwise_rows_in, gate_up, preferred_elemen...  10.7 us
    concatenate x1, other arithmetic, body(): jnp.concatenate([both_part, down_part[:, None]], axis=1)  10.5 us
    dot_general x1, matrix products, body(): jnp.einsum('secd,secgf->dgef', rows_in, hidden_grads, preferred_element_t...  9.74 us
    dot_general x1, matrix products, body(): jnp.einsum('secd,def->secf', rowwise_scaled, down_proj, preferred_element...  7.86 us
  transfers between devices with their start and end apart: 6, of which 4 were waited for; matrix products, arithmetic and copies ran while one was open for 20% of the time, Pallas kernels for 0%

commit v1 on v0

v1 whole, which is shorter than its diff:
```python
import functools

import jax
import jax.numpy as jnp
from jax import lax
from jax.experimental import pallas as pl
from jax.experimental.pallas import tpu as pltpu
from jax.sharding import PartitionSpec as P

BF = jnp.bfloat16
F32 = jnp.float32
SLICE = 512
PART_A = 384
PART_B = SLICE - PART_A
GROUP = SLICE + PART_A
SLICES = 8
CAP = 32
LANES = 128
VMEM_LIMIT = 48 * 1024 * 1024


def params(**extra):
    return pltpu.CompilerParams(vmem_limit_bytes=VMEM_LIMIT, **extra)


def dot_nn(a, b):
    return lax.dot_general(a, b, (((1,), (0,)), ((), ())), preferred_element_type=F32)


def dot_nt(a, b):
    return lax.dot_general(a, b, (((1,), (1,)), ((), ())), preferred_element_type=F32)


def dot_tn(a, b):
    return lax.dot_general(a, b, (((0,), (0,)), ((), ())), preferred_element_type=F32)


def pack_kernel(ids_ref, gates_ref, tok_ref, dy_ref, first_ref, second_ref, hot_ref, *, step_experts):
    tokens = ids_ref.shape[1]
    base = pl.program_id(0) * step_experts
    expert = lax.broadcasted_iota(jnp.int32, (8, tokens), 0) + base
    zero = jnp.zeros((8, tokens), F32)
    is_0 = ids_ref[0:1, :] == expert
    is_1 = ids_ref[1:2, :] == expert
    named = is_0 | is_1
    member = jnp.where(named, 1.0, 0.0).astype(BF)
    row = lax.broadcasted_iota(jnp.int32, (tokens, tokens), 0)
    col = lax.broadcasted_iota(jnp.int32, (tokens, tokens), 1)
    earlier = jnp.where(row < col, 1.0, 0.0).astype(BF)
    place = jnp.where(named, dot_nn(member, earlier), -1.0)
    gates = gates_ref[...].astype(F32)
    weight = jnp.where(is_0, gates[0:1, :], zero) + jnp.where(is_1, gates[1:2, :], zero)
    rows = step_experts * CAP
    place_all = jnp.broadcast_to(place[:step_experts, None, :], (step_experts, CAP, tokens)).reshape(rows, tokens)
    weight_all = jnp.broadcast_to(weight[:step_experts, None, :], (step_experts, CAP, tokens)).reshape(rows, tokens)
    slot = (lax.broadcasted_iota(jnp.int32, (rows, tokens), 0) % CAP).astype(F32)
    hot = jnp.where(place_all == slot, 1.0, 0.0)
    slot_gate = jnp.sum(hot * weight_all, axis=1, keepdims=True)
    first_ref[:, SLICES * GROUP :] = jnp.broadcast_to(slot_gate, (rows, LANES)).astype(BF)
    hot = hot.astype(BF)
    hot_ref[...] = hot
    for q in range(SLICES):
        cols = slice(q * SLICE, (q + 1) * SLICE)
        first_ref[:, q * GROUP : q * GROUP + SLICE] = dot_nn(hot, tok_ref[:, cols]).astype(BF)
        grads = dot_nn(hot, dy_ref[:, cols]).astype(BF)
        first_ref[:, q * GROUP + SLICE : (q + 1) * GROUP] = grads[:, :PART_A]
        second_ref[:, q * PART_B : (q + 1) * PART_B] = grads[:, PART_A:]


def pack(ids, gates, tokens_in, out_grad, slots):
    steps = 4
    tok_dev, width = tokens_in.shape
    rows = slots // steps
    wide = SLICES * GROUP + LANES
    whole = lambda shape: pl.BlockSpec(shape, lambda i: (0, 0))
    return pl.pallas_call(
        functools.partial(pack_kernel, step_experts=rows // CAP),
        grid=(steps,),
        in_specs=[whole((2, tok_dev)), whole((2, tok_dev)), whole((tok_dev, width)), whole((tok_dev, width))],
        out_specs=[
            pl.BlockSpec((rows, wide), lambda i: (i, 0)),
            pl.BlockSpec((rows, SLICES * PART_B), lambda i: (i, 0)),
            pl.BlockSpec((rows, tok_dev), lambda i: (i, 0)),
        ],
        out_shape=[
            jax.ShapeDtypeStruct((slots, wide), BF),
            jax.ShapeDtypeStruct((slots, SLICES * PART_B), BF),
            jax.ShapeDtypeStruct((slots, tok_dev), BF),
        ],
        compiler_params=params(),
        name="pack",
    )(ids, gates, tokens_in, out_grad)


def pick_kernel(index_ref, src_ref, out_ref):
    del index_ref
    out_ref[...] = src_ref[...]


def pick(src, index, width):
    rows = src.shape[0]
    return pl.pallas_call(
        pick_kernel,
        grid_spec=pltpu.PrefetchScalarGridSpec(
            num_scalar_prefetch=1,
            grid=(4,),
            in_specs=[pl.BlockSpec((rows, width), lambda i, index: (0, index[i]))],
            out_specs=pl.BlockSpec((rows, width), lambda i, index: (0, i)),
        ),
        out_shape=jax.ShapeDtypeStruct((rows, 4 * width), BF),
        compiler_params=params(),
        name="pick",
    )(index, src)


def pre_kernel(rows_ref, gate_ref, wg_ref, wu_ref, wd_ref, u_ref, c1_ref, c2_ref, p_ref, gp_ref, pg_acc, pu_acc, *, per):
    step = pl.program_id(0)

    @pl.when(step == 0)
    def _():
        pg_acc[...] = jnp.zeros_like(pg_acc)
        pu_acc[...] = jnp.zeros_like(pu_acc)
        u_ref[...] = jnp.zeros_like(u_ref)

    x = jnp.concatenate([rows_ref[:, k * GROUP : k * GROUP + SLICE] for k in range(per)], axis=1)
    pg_acc[...] += dot_nn(x, wg_ref[...])
    pu_acc[...] += dot_nn(x, wu_ref[...])
    dy = jnp.concatenate([rows_ref[:, k * GROUP + SLICE : (k + 1) * GROUP] for k in range(per)], axis=1)
    wd = jnp.concatenate([wd_ref[k * SLICE : k * SLICE + PART_A, :] for k in range(per)], axis=0)
    u_ref[...] += dot_nn(dy, wd)

    @pl.when(step == pl.num_programs(0) - 1)
    def _():
        chunk = 32

        def one(i, carry):
            at = pl.ds(pl.multiple_of(i * chunk, chunk), chunk)
            pg = pg_acc[at, :]
            pu = pu_acc[at, :]
            g = gate_ref[at, :].astype(F32)[:, :1]
            s = jax.nn.sigmoid(pg)
            a = pg * s
            product = a * pu
            p_ref[at, :] = product.astype(BF)
            gp_ref[at, :] = (g * product).astype(BF)
            c1_ref[at, :] = g * (pu * s * (1.0 + pg * (1.0 - s)))
            c2_ref[at, :] = g * a
            return carry

        lax.fori_loop(0, pg_acc.shape[0] // chunk, one, 0)


def pre(first, wg, wu, wd):
    slots = first.shape[0]
    ff = wd.shape[1]
    per = 2
    weights = pl.BlockSpec((per * SLICE, ff), lambda q: (q, 0))
    whole = pl.BlockSpec((slots, ff), lambda q: (0, 0))
    return pl.pallas_call(
        functools.partial(pre_kernel, per=per),
        grid=(SLICES // per,),
        in_specs=[
            pl.BlockSpec((slots, per * GROUP), lambda q: (0, q)),
            pl.BlockSpec((slots, LANES), lambda q: (0, SLICES * GROUP // LANES)),
            weights,
            weights,
            weights,
        ],
        out_specs=[whole] * 5,
        out_shape=[
            jax.ShapeDtypeStruct((slots, ff), F32),
            jax.ShapeDtypeStruct((slots, ff), F32),
            jax.ShapeDtypeStruct((slots, ff), F32),
            jax.ShapeDtypeStruct((slots, ff), BF),
            jax.ShapeDtypeStruct((slots, ff), BF),
        ],
        scratch_shapes=[pltpu.VMEM((slots, ff), F32)] * 2,
        compiler_params=params(),
        name="pre",
    )(first, first, wg, wu, wd)


def hidden_kernel(dy_ref, wd_ref, u_ref, c1_ref, c2_ref, p_ref, h_ref, gate_ref, u_acc, gate_acc):
    step = pl.program_id(0)
    u_acc[...] = u_ref[...] + dot_nn(dy_ref[...], wd_ref[...])

    @pl.when(step == 0)
    def _():
        gate_acc[...] = jnp.zeros_like(gate_acc)

    chunk = 64

    def one(i, carry):
        at = pl.ds(pl.multiple_of(i * chunk, chunk), chunk)
        u = u_acc[at, :]
        h_ref[0, at, :] = (u * c1_ref[at, :]).astype(BF)
        h_ref[1, at, :] = (u * c2_ref[at, :]).astype(BF)
        both = u * p_ref[at, :].astype(F32)
        folded = both[:, :LANES]
        for k in range(1, both.shape[1] // LANES):
            folded += both[:, k * LANES : (k + 1) * LANES]
        gate_acc[at, :] += folded
        return carry

    lax.fori_loop(0, u_acc.shape[0] // chunk, one, 0)

    @pl.when(step == pl.num_programs(0) - 1)
    def _():
        total = jnp.sum(gate_acc[...], axis=1, keepdims=True)
        gate_ref[...] = jnp.broadcast_to(total, gate_ref.shape).astype(BF)


def hidden(second, wd_b, u_a, c1, c2, p):
    slots, ff = p.shape
    blk = 256
    col = pl.BlockSpec((slots, blk), lambda j: (0, j))
    depth = second.shape[1]
    return pl.pallas_call(
        hidden_kernel,
        grid=(ff // blk,),
        in_specs=[
            pl.BlockSpec((slots, depth), lambda j: (0, 0)),
            pl.BlockSpec((depth, blk), lambda j: (0, j)),
            col,
            col,
            col,
            col,
        ],
        out_specs=[pl.BlockSpec((2, slots, blk), lambda j: (0, 0, j)), pl.BlockSpec((slots, LANES), lambda j: (0, 0))],
        out_shape=[jax.ShapeDtypeStruct((2, slots, ff), BF), jax.ShapeDtypeStruct((slots, LANES), BF)],
        scratch_shapes=[pltpu.VMEM((slots, blk), F32), pltpu.VMEM((slots, LANES), F32)],
        compiler_params=params(),
        name="hidden",
    )(second, wd_b, u_a, c1, c2, p)


def input_kernel(h_ref, wg_ref, wu_ref, gate_ref, out_ref):
    out_ref[...] = (dot_nt(h_ref[0], wg_ref[...]) + dot_nt(h_ref[1], wu_ref[...])).astype(BF)

    @pl.when(pl.program_id(0) == pl.num_programs(0) - 1)
    def _():
        out_ref[:, out_ref.shape[1] - LANES :] = gate_ref[...]


def input_rows(h, wg, wu, gate):
    _, slots, ff = h.shape
    wide = wg.shape[0] + LANES
    blk = wide // 3
    weights = pl.BlockSpec((blk, ff), lambda j: (j, 0))
    return pl.pallas_call(
        input_kernel,
        grid=(3,),
        in_specs=[
            pl.BlockSpec((2, slots, ff), lambda j: (0, 0, 0)),
            weights,
            weights,
            pl.BlockSpec((slots, LANES), lambda j: (0, 0)),
        ],
        out_specs=pl.BlockSpec((slots, blk), lambda j: (0, j)),
        out_shape=jax.ShapeDtypeStruct((slots, wide), BF),
        compiler_params=params(),
        name="input_rows",
    )(h, wg, wu, gate)


def part_kernel(own_ids, mate_ids, ff_ids, own_ref, mate_ref, rhs_ref, rhs_mate_ref, out_ref, *, lo, hi):
    del own_ids, mate_ids, ff_ids
    out_ref[0] = (
        dot_tn(own_ref[:, lo:hi], rhs_ref[0]) + dot_tn(mate_ref[:, lo:hi], rhs_mate_ref[0])
    ).astype(BF)


def partials(own, mate, width, lo, hi, rhs, rhs_mate, own_ids, mate_ids, ff_ids):
    steps = own_ids.shape[0]
    slots = own.shape[0]
    ff = rhs.shape[2]
    rhs_spec = pl.BlockSpec((1, slots, ff), lambda i, own_ids, mate_ids, ff_ids: (ff_ids[i], 0, 0))
    return pl.pallas_call(
        functools.partial(part_kernel, lo=lo, hi=hi),
        grid_spec=pltpu.PrefetchScalarGridSpec(
            num_scalar_prefetch=3,
            grid=(steps,),
            in_specs=[
                pl.BlockSpec((slots, width), lambda i, own_ids, mate_ids, ff_ids: (0, own_ids[i])),
                pl.BlockSpec((slots, width), lambda i, own_ids, mate_ids, ff_ids: (0, mate_ids[i])),
                rhs_spec,
                rhs_spec,
            ],
            out_specs=pl.BlockSpec((1, hi - lo, ff), lambda i, own_ids, mate_ids, ff_ids: (i, 0, 0)),
        ),
        out_shape=jax.ShapeDtypeStruct((steps, hi - lo, ff), BF),
        compiler_params=params(),
        name="partials",
    )(own_ids, mate_ids, ff_ids, own, mate, rhs, rhs_mate)


def unpack_kernel(hot_ref, ids_ref, rows_ref, gates_ref, out_ref, gate_ref):
    out_ref[...] = dot_tn(hot_ref[...], rows_ref[...]).astype(BF)

    @pl.when(pl.program_id(0) == 0)
    def _():
        hot = hot_ref[...]
        expert = lax.broadcasted_iota(jnp.int32, hot.shape, 0) // CAP
        for k in range(2):
            chosen = jnp.where(expert == ids_ref[k : k + 1, :], hot.astype(F32), 0.0).astype(BF)
            gate_ref[k : k + 1, :] = dot_tn(gates_ref[...], chosen)[0:1, :].astype(BF)


def unpack(hot, ids, back, width):
    slots, tok_dev = hot.shape
    steps = 4
    whole = lambda shape: pl.BlockSpec(shape, lambda i: (0, 0))
    return pl.pallas_call(
        unpack_kernel,
        grid=(steps,),
        in_specs=[
            whole((slots, tok_dev)),
            whole((2, tok_dev)),
            pl.BlockSpec((slots, width // steps), lambda i: (0, i)),
            pl.BlockSpec((slots, LANES), lambda i: (0, width // LANES)),
        ],
        out_specs=[pl.BlockSpec((tok_dev, width // steps), lambda i: (0, i)), whole((2, tok_dev))],
        out_shape=[jax.ShapeDtypeStruct((tok_dev, width), BF), jax.ShapeDtypeStruct((2, tok_dev), BF)],
        compiler_params=params(),
        name="unpack",
    )(hot, ids, back, back)


UP = [(i, (i + 2) % 8) for i in range(8)]
DOWN = [(i, (i - 2) % 8) for i in range(8)]
SWAP = [(i, i ^ 1) for i in range(8)]


def ring(parts, perm):
    total = parts[0]
    for part in parts[1:]:
        arrived = lax.ppermute(total, "dp", perm)
        total = (arrived.astype(F32) + part.astype(F32)).astype(BF)
    return total


def body(tokens_in, out_grad, expert_ids, gate_probs, gate_up, down_proj):
    width = tokens_in.shape[1]
    owners = lax.axis_size("expert")
    ff = gate_up.shape[3]
    slots = owners * CAP
    me = lax.axis_index("dp")
    z, core = me // 2, me % 2

    ids = expert_ids.T
    first, second, hot = pack(ids, gate_probs.T, tokens_in, out_grad, slots)

    def exchange(rows):
        wide = rows.shape[1]
        got = lax.all_to_all(rows.reshape(owners, CAP, wide), "expert", split_axis=0, concat_axis=0, tiled=True)
        return got.reshape(slots, wide)

    first = exchange(first)
    second = exchange(second)

    wg = gate_up[:, 0, 0, :]
    wu = gate_up[:, 1, 0, :]
    wd = down_proj[:, 0, :]
    wd_b = wd.reshape(SLICES, SLICE, ff)[:, PART_A:].reshape(SLICES * PART_B, ff)

    order = ((z + jnp.array([3, 2, 1, 0])) % 4).astype(jnp.int32)
    all_z = jnp.arange(4, dtype=jnp.int32)
    theirs = 2 * all_z + (1 - core)
    none = jnp.zeros((4,), jnp.int32)

    mate_first = lax.ppermute(pick(first, theirs, GROUP), "dp", SWAP)
    u_a, c1, c2, p, gp = pre(first, wg, wu, wd)
    gp = gp[None]
    gp_mate = lax.ppermute(gp, "dp", SWAP)
    down_a = partials(first, mate_first, GROUP, SLICE, GROUP, gp, gp_mate, 2 * order + core, order, none)
    half = PART_A // 2
    grad_a = jnp.concatenate(
        [
            ring([down_a[j, :half] for j in (0, 1, 2, 3)], UP),
            ring([down_a[j, half:] for j in (2, 1, 0, 3)], DOWN),
        ],
        axis=0,
    )

    mate_second = lax.ppermute(pick(second, theirs, PART_B), "dp", SWAP)
    h, gate_rows = hidden(second, wd_b, u_a, c1, c2, p)
    h_mate = lax.ppermute(h, "dp", SWAP)
    down_b = partials(second, mate_second, PART_B, 0, PART_B, gp, gp_mate, 2 * order + core, order, none)

    pick_z = jnp.stack([order[0], order[2]])
    pick_f = jnp.array([0, 1], jnp.int32)
    both_1 = partials(first, mate_first, GROUP, 0, SLICE, h, h_mate, 2 * pick_z + core, pick_z, pick_f)
    back = exchange(input_rows(h, wg, wu, gate_rows))
    rest_z = jnp.stack([order[1], order[1], order[2], order[0], order[3], order[3]])
    rest_f = jnp.array([0, 1, 0, 1, 0, 1], jnp.int32)
    both_2 = partials(first, mate_first, GROUP, 0, SLICE, h, h_mate, 2 * rest_z + core, rest_z, rest_f)

    cut = SLICE // 2
    half = PART_B // 2
    ring_gate = [both_1[0], both_2[0], both_2[2], both_2[4]]
    ring_up = [both_1[1], both_2[1], both_2[3], both_2[5]]
    down_up = [down_b[j, :half] for j in (0, 1, 2, 3)]
    down_dn = [down_b[j, half:] for j in (2, 1, 0, 3)]
    gate_lo = ring([t[:cut] for t in ring_gate], UP)
    up_lo = ring([t[:cut] for t in ring_up], DOWN)
    gate_hi = ring([jnp.concatenate([t[cut:], d], axis=0) for t, d in zip(ring_gate, down_up)], UP)
    up_hi = ring([jnp.concatenate([t[cut:], d], axis=0) for t, d in zip(ring_up, down_dn)], DOWN)

    grad_gate = jnp.concatenate([gate_lo, gate_hi[:cut]], axis=0)
    grad_up = jnp.concatenate([up_lo, up_hi[:cut]], axis=0)
    gate_up_grad = jnp.stack([grad_gate, grad_up], axis=1)[:, :, None, :]
    down_grad = jnp.concatenate([grad_a, gate_hi[cut:], up_hi[cut:]], axis=0)[:, None, :]

    input_grad, gate_grad = unpack(hot, ids, back, width)
    return (input_grad, gate_grad.T, gate_up_grad, down_grad)


def solution(mesh):
    placed = (
        P(("dp", "expert"), None),
        P(("dp", "expert"), None),
        P(("dp", "expert"), None),
        P(("dp", "expert"), None),
        P(None, None, "expert", None),
        P(None, "expert", None),
    )
    return jax.shard_map(
        body,
        mesh=mesh,
        in_specs=placed,
        out_specs=(
            P(("dp", "expert"), None),
            P(("dp", "expert"), None),
            P("dp", None, "expert", None),
            P("dp", "expert", None),
        ),
        check_vma=False,
    )
```

time: 313 us -> 331 us (1.058)
  Pallas kernels: 0 us -> 74.4 us
  matrix products: 54.8 us -> 0 us
  local copies, waits for them, and re-layouts: 37.6 us -> 64.4 us
  waiting for transfers between devices: 156 us -> 130 us
  starting transfers between devices: 29.5 us -> 48.5 us
  between operations: 14.3 us -> 1.07 us
  other arithmetic: 19.7 us -> 11.5 us
    pallas_call x0 -> x11, Pallas kernels: none -> 74.4 us  [the longest x4 26.2 us: partials(): pl.pallas_call(functools.partial(part_kernel, lo=lo, hi=hi), grid_spec=pl...]
    all_to_all x5 -> x3, waiting for transfers between devices: 156 us -> 99.7 us  [exchange(): lax.all_to_all(rows.reshape(owners, CAP, wide), 'expert', split_axis=0, c...]
    dot_general x6 -> x0, matrix products: 54.8 us -> none  [the longest x1 12.6 us: body(): jnp.einsum('secgf,dgef->secd', rowwise_hidden_grads, gate_up, preferred_e...]
    ppermute x0 -> x22, waiting for transfers between devices: none -> 30.2 us  [the longest x18 30.2 us: ring(): arrived = lax.ppermute(total, 'dp', perm)]
    slice x3 -> x11, local copies, waits for them, and re-layouts: 1.59 us -> 30.7 us  [the longest x1 24.6 us: body(): wu = gate_up[:, 1, 0, :]]
    ppermute x0 -> x22, starting transfers between devices: none -> 28.5 us  [the longest x18 27.5 us: ring(): arrived = lax.ppermute(total, 'dp', perm)]
    gather x5 -> x0, local copies, waits for them, and re-layouts: 20.9 us -> none  [the longest x1 6.7 us: body(): slot_rows[slot_of].reshape(tok_dev, top_win, width).astype(jnp.float32)]
    squeeze x0 -> x3, local copies, waits for them, and re-layouts: none -> 16.1 us  [the longest x1 15.2 us: body(): wu = gate_up[:, 1, 0, :]]
  transfers between devices with their start and end apart: 6 -> 25, of which waited for: 4 -> 10; matrix products, arithmetic and copies ran while one was open for 20% -> 18% of each run, Pallas kernels for 0% -> 21%
where the time goes in v1:
time: 331 us; the launch traced here: 330 us
  waiting for transfers between devices  130 us (39%)
  Pallas kernels  74.4 us (22%)
  local copies, waits for them, and re-layouts  64.4 us (19%)
  starting transfers between devices  48.5 us (15%)
  other arithmetic  11.5 us (3%)
    all_to_all x3, waiting for transfers between devices, exchange(): lax.all_to_all(rows.reshape(owners, CAP, wide), 'expert', split_axis=0, c...  99.7 us
    ppermute x18, waiting for transfers between devices, ring(): arrived = lax.ppermute(total, 'dp', perm)  30.2 us
    ppermute x18, starting transfers between devices, ring(): arrived = lax.ppermute(total, 'dp', perm)  27.5 us
    pallas_call x4, Pallas kernels, partials(): pl.pallas_call(functools.partial(part_kernel, lo=lo, hi=hi), grid_spec=pl...  26.2 us
    slice x1, local copies, waits for them, and re-layouts, body(): wu = gate_up[:, 1, 0, :]  24.6 us
    all_to_all x3, starting transfers between devices, exchange(): lax.all_to_all(rows.reshape(owners, CAP, wide), 'expert', split_axis=0, c...  20 us
    pallas_call x1, Pallas kernels, pre(): pl.pallas_call(functools.partial(pre_kernel, per=per), grid=(SLICES // pe...  16.2 us
    squeeze x1, local copies, waits for them, and re-layouts, body(): wu = gate_up[:, 1, 0, :]  15.2 us
  transfers between devices with their start and end apart: 25, of which 10 were waited for; matrix products, arithmetic and copies ran while one was open for 18% of the time, Pallas kernels for 21%

profile of v1, /device:TPU:0, one launch (start us, length us, event | category | flops | bytes accessed | tf_op | source)
XLA Modules:
  0.0 329.8 jit_solution(6823008726259004405)
XLA Ops:
  0.6 1.2 copy-done.6
  1.9 1.2 copy-done.7
  4.4 5.1 %pack.1 = (bf16[512,7296]{1,0:T(8,128)(2,1)}, bf16[512,1024]{1,0:T(8,128)(2,1)}, bf16[512,128]{1,0:T(8,128)(2,1)S(1)}) custom-call(s32[2,128]{1,0:T(2,128)S(1)} %bitcast.133, bf16[2,128]{1,0:T(2,128)(2,1)S(1)} %bitcast.135, bf16[128,4096]{1,0:T(8,128)(2,1)S(1)} %copy-done.6, bf16[128,4096]{1,0:T(8,128)(2,1)S(1)} %copy-done.7), custom_call_target="tpu_custom_call" | custom-call | tf_op jit(solution)/shard_map/pack/pallas_call | solution.py:76
  9.5 7.1 %all-to-all-start.1 = ((bf16[16,32,7296]{2,1,0:T(8,128)(2,1)}), bf16[16,32,7296]{2,1,0:T(8,128)(2,1)}, u32[]{:S(2)}, u32[]{:S(2)}) async-start(bf16[16,32,7296]{2,1,0:T(8,128)(2,1)} %bitcast.138), calls=%async_computation.1 | async-start | bytes 14942208 | tf_op jit(solution)/shard_map/all_to_all | solution.py:355
  16.7 2.7 slice.250
  19.3 24.6 %fusion.13 = (bf16[4096,1,1,768]{3,1,2,0:T(2,128)(2,1)}, bf16[4096,1,1,768]{3,1,2,0:T(2,128)(2,1)}) fusion(bf16[4096,2,1,768]{3,1,2,0:T(2,128)(2,1)} %param.13), kind=kLoop, calls=%fused_computation.79 | loop fusion | bytes 25165824 | tf_op jit(solution)/shard_map/slice | solution.py:362
  43.9 83.6 %all-to-all-done.1 = bf16[16,32,7296]{2,1,0:T(8,128)(2,1)} async-done(((bf16[16,32,7296]{2,1,0:T(8,128)(2,1)}), bf16[16,32,7296]{2,1,0:T(8,128)(2,1)}, u32[]{:S(2)}, u32[]{:S(2)}) %all-to-all-start.1) | async-done | bytes 7471136 | tf_op jit(solution)/shard_map/all_to_all | solution.py:355
  127.5 5.4 %all-to-all-start = ((bf16[16,32,1024]{2,1,0:T(8,128)(2,1)}), bf16[16,32,1024]{2,1,0:T(8,128)(2,1)S(1)}, u32[]{:S(2)}, u32[]{:S(2)}) async-start(bf16[16,32,1024]{2,1,0:T(8,128)(2,1)} %bitcast.2), calls=%async_computation | async-start | bytes 2097152 | tf_op jit(solution)/shard_map/all_to_all | solution.py:355
  133.0 5.1 %pick.2 = bf16[512,3584]{1,0:T(8,128)(2,1)} custom-call(s32[4]{0:T(128)S(1)} %multiply_add_fusion.2.index_ref, bf16[512,7296]{1,0:T(8,128)(2,1)} %bitcast.7.rows_ref.gate_ref.src_ref.own_ref), custom_call_target="tpu_custom_call" | custom-call | tf_op jit(solution)/shard_map/pick/pallas_call | solution.py:102
  138.1 15.2 %copy_bitcast_fusion = (bf16[4096,768]{1,0:T(8,128)(2,1)}, bf16[4096,768]{1,0:T(8,128)(2,1)}) fusion(bf16[4096,1,1,768]{3,1,2,0:T(2,128)(2,1)} %get-tuple-element.36, bf16[4096,1,1,768]{3,1,2,0:T(2,128)(2,1)} %get-tuple-element.37), kind=kLoop, calls=%fused_computation | loop fusion | bytes 25165824 | tf_op jit(solution)/shard_map/squeeze | solution.py:362
  153.3 16.2 %pre.1 = (f32[512,768]{1,0:T(8,128)S(1)}, f32[512,768]{1,0:T(8,128)S(1)}, f32[512,768]{1,0:T(8,128)}, bf16[512,768]{1,0:T(8,128)(2,1)S(1)}, bf16[512,768]{1,0:T(8,128)(2,1)S(1)}) custom-call(bf16[512,7296]{1,0:T(8,128)(2,1)} %bitcast.7.rows_ref.gate_ref.src_ref.own_ref, bf16[512,7296]{1,0:T(8,128)(2,1)} %bitcast.7.rows_ref.gate_ref.src_ref.own_ref, ...), custom_call_target="tpu_custom_call" | custom-call | tf_op jit(solution)/shard_map/pre/pallas_call | solution.py:159
  169.5 1.1 copy-done.4
  170.7 1.2 copy-done.5
  172.7 1.4 copy-done.3
  174.1 1.1 copy-done.9
  175.3 4.3 %hidden.1 = (bf16[2,512,768]{2,1,0:T(8,128)(2,1)S(1)}, bf16[512,128]{1,0:T(8,128)(2,1)S(1)}) custom-call(bf16[512,1024]{1,0:T(8,128)(2,1)S(1)} %bitcast.126, bf16[1024,768]{1,0:T(8,128)(2,1)S(1)} %bitcast.129, f32[512,768]{1,0:T(8,128)} %copy-done.4, f32[512,768]{1,0:T(8,128)} %copy-done.5, f32[512,768]{1,0:T(8,128)} %get-tuple-element.21.c2_ref, ...), custom_call_target="tpu_custom_call" | custom-call | tf_op jit(solution)/shard_map/hidden/pallas_call | solution.py:218
  179.5 10.6 %input_rows.1 = bf16[512,4224]{1,0:T(8,128)(2,1)S(1)} custom-call(bf16[2,512,768]{2,1,0:T(8,128)(2,1)S(1)} %get-tuple-element.23.h_ref.rhs_ref, bf16[4096,768]{1,0:T(8,128)(2,1)} %get-tuple-element.75.wg_ref, bf16[4096,768]{1,0:T(8,128)(2,1)} %get-tuple-element.74.wu_ref, bf16[512,128]{1,0:T(8,128)(2,1)S(1)} %get-tuple-element.24.gate_ref), custom_call_target="tpu_custom_call" | custom-call | tf_op jit(solution)/shard_map/input_rows/pallas_call | solution.py:250
  190.1 2.1 copy-done
  192.2 7.4 %all-to-all-start.2 = ((bf16[16,32,4224]{2,1,0:T(8,128)(2,1)}), bf16[16,32,4224]{2,1,0:T(8,128)(2,1)}, u32[]{:S(2)}, u32[]{:S(2)}) async-start(bf16[16,32,4224]{2,1,0:T(8,128)(2,1)} %bitcast.125), calls=%async_computation.2 | async-start | bytes 8650752 | tf_op jit(solution)/shard_map/all_to_all | solution.py:355
  200.4 2.1 pick.3
  203.4 2.6 stack.16.mate_ids
  206.0 1.4 multiply_add_fusion.3
  207.4 4.1 %partials.6 = bf16[4,128,768]{2,1,0:T(8,128)(2,1)S(1)} custom-call(s32[4]{0:T(128)S(1)} %get-tuple-element.34.own_ids, s32[4]{0:T(128)S(1)} %get-tuple-element.35.mate_ids, s32[4]{0:T(128)S(1)} %broadcast.18.ff_ids, bf16[512,1024]{1,0:T(8,128)(2,1)S(1)} %bitcast.128, bf16[512,512]{1,0:T(8,128)(2,1)} %collective-permute-done.5.mate_ref, ...), custom_call_target="tpu_custom_call" | custom-call | tf_op jit(solution)/shard_map/partials/pallas_call | solution.py:278
  212.4 4.4 %partials.4 = bf16[2,512,768]{2,1,0:T(8,128)(2,1)S(1)} custom-call(s32[2]{0:T(128)S(1)} %get-tuple-element.32.own_ids, s32[2]{0:T(128)S(1)} %get-tuple-element.33.mate_ids, s32[2]{0:T(128)S(1)} %call_exported.0.ff_ids, bf16[512,7296]{1,0:T(8,128)(2,1)} %bitcast.7.rows_ref.gate_ref.src_ref.own_ref, bf16[512,3584]{1,0:T(8,128)(2,1)} %collective-permute-done.mate_ref, ...), custom_call_target="tpu_custom_call" | custom-call | tf_op jit(solution)/shard_map/partials/pallas_call | solution.py:278
  218.5 3.9 %collective-permute-start.13 = (bf16[320,768]{1,0:T(8,128)(2,1)}, bf16[320,768]{1,0:T(8,128)(2,1)}, u32[]{:S(2)}, u32[]{:S(2)}) collective-permute-start(bf16[320,768]{1,0:T(8,128)(2,1)} %pad_maximum_fusion.1), channel_id=1, source_target_pairs={{0,96},{16,112},{32,0},{48,16},{64,32},{80,48},{96,64},{112,80},{1... | collective-permute-start | bytes 1474568 | tf_op jit(solution)/shard_map/ppermute | solution.py:337
  222.4 3.2 collective-permute-start.10
  225.6 6.4 %partials.7 = bf16[4,384,768]{2,1,0:T(8,128)(2,1)S(1)} custom-call(s32[4]{0:T(128)S(1)} %get-tuple-element.34.own_ids, s32[4]{0:T(128)S(1)} %get-tuple-element.35.mate_ids, s32[4]{0:T(128)S(1)} %broadcast.18.ff_ids, bf16[512,7296]{1,0:T(8,128)(2,1)} %bitcast.7.rows_ref.gate_ref.src_ref.own_ref, bf16[512,3584]{1,0:T(8,128)(2,1)} %collective-permute-done.mate_ref, ...), custom_call_target="tpu_custom_call" | custom-call | tf_op jit(solution)/shard_map/partials/pallas_call | solution.py:278
  232.2 3.2 collective-permute-start.19
  235.4 11.3 %partials.5 = bf16[6,512,768]{2,1,0:T(8,128)(2,1)} custom-call(s32[6]{0:T(128)S(1)} %multiply_add_fusion.1.own_ids, s32[6]{0:T(128)S(1)} %stack.16.mate_ids, s32[6]{0:T(128)S(1)} %copy-done.13, bf16[512,7296]{1,0:T(8,128)(2,1)} %bitcast.7.rows_ref.gate_ref.src_ref.own_ref, bf16[512,3584]{1,0:T(8,128)(2,1)} %collective-permute-done.mate_ref, ...), custom_call_target="tpu_custom_call" | custom-call | tf_op jit(solution)/shard_map/partials/pallas_call | solution.py:278
  246.7 1.7 slice_bitcast_fusion.8
  249.8 16.1 %all-to-all-done.2 = bf16[16,32,4224]{2,1,0:T(8,128)(2,1)} async-done(((bf16[16,32,4224]{2,1,0:T(8,128)(2,1)}), bf16[16,32,4224]{2,1,0:T(8,128)(2,1)}, u32[]{:S(2)}, u32[]{:S(2)}) %all-to-all-start.2) | async-done | bytes 4325408 | tf_op jit(solution)/shard_map/all_to_all | solution.py:355
  266.0 4.9 %unpack.1 = (bf16[128,4096]{1,0:T(8,128)(2,1)}, bf16[2,128]{1,0:T(2,128)(2,1)}) custom-call(bf16[512,128]{1,0:T(8,128)(2,1)S(1)} %get-tuple-element.16.hot_ref, s32[2,128]{1,0:T(2,128)S(1)} %bitcast.134, bf16[512,4224]{1,0:T(8,128)(2,1)} %bitcast.12.rows_ref.gates_ref, bf16[512,4224]{1,0:T(8,128)(2,1)} %bitcast.12.rows_ref.gates_ref), custom_call_target="tpu_custom_call" | custom-call | tf_op jit(solution)/shard_map/unpack/pallas_call | solution.py:313
  270.9 3.9 %collective-permute-start.20 = (bf16[192,768]{1,0:T(8,128)(2,1)S(1)}, bf16[192,768]{1,0:T(8,128)(2,1)S(1)}, u32[]{:S(2)}, u32[]{:S(2)}) collective-permute-start(bf16[192,768]{1,0:T(8,128)(2,1)S(1)} %copy-done.21), channel_id=1, source_target_pairs={{0,96},{16,112},{32,0},{48,16},{64,32},{80,48},{96,64},{112,80},{1... | collective-permute-start | bytes 884744 | tf_op jit(solution)/shard_map/ppermute | solution.py:337
  274.9 1.5 fusion.5
  276.5 3.2 collective-permute-start.11
  279.7 1.1 add_convert_fusion.2
  281.0 1.4 collective-permute-done.20
  284.2 3.1 collective-permute-start.21
  287.4 2.3 collective-permute-done.3
  290.8 1.3 fusion.4
  292.6 3.5 %collective-permute-done.18 = bf16[192,768]{1,0:T(8,128)(2,1)S(1)} collective-permute-done((bf16[192,768]{1,0:T(8,128)(2,1)S(1)}, bf16[192,768]{1,0:T(8,128)(2,1)S(1)}, u32[]{:S(2)}, u32[]{:S(2)}) %collective-permute-start.18) | collective-permute-done | bytes 294944 | tf_op jit(solution)/shard_map/ppermute | solution.py:337
  297.2 10.5 %collective-permute-done.21 = bf16[192,768]{1,0:T(8,128)(2,1)S(1)} collective-permute-done((bf16[192,768]{1,0:T(8,128)(2,1)S(1)}, bf16[192,768]{1,0:T(8,128)(2,1)S(1)}, u32[]{:S(2)}, u32[]{:S(2)}) %collective-permute-start.21) | collective-permute-done | bytes 294944 | tf_op jit(solution)/shard_map/ppermute | solution.py:337
  307.9 4.0 %collective-permute-start.15 = (bf16[320,768]{1,0:T(8,128)(2,1)S(1)}, bf16[320,768]{1,0:T(8,128)(2,1)S(1)}, u32[]{:S(2)}, u32[]{:S(2)}) collective-permute-start(bf16[320,768]{1,0:T(8,128)(2,1)S(1)} %add_convert_fusion.1), channel_id=1, source_target_pairs={{0,96},{16,112},{32,0},{48,16},{64,32},{80,48},{96,64},{112,80},{1... | collective-permute-start | bytes 1474568 | tf_op jit(solution)/shard_map/ppermute | solution.py:337
  312.1 1.5 collective-permute-done.4
  313.7 2.4 collective-permute-done.12
  316.0 1.3 fusion.3
  317.3 7.6 %collective-permute-done.15 = bf16[320,768]{1,0:T(8,128)(2,1)S(1)} collective-permute-done((bf16[320,768]{1,0:T(8,128)(2,1)S(1)}, bf16[320,768]{1,0:T(8,128)(2,1)S(1)}, u32[]{:S(2)}, u32[]{:S(2)}) %collective-permute-start.15) | collective-permute-done | bytes 491552 | tf_op jit(solution)/shard_map/ppermute | solution.py:337
  326.1 2.8 copy.15
  (99 shorter events, 15.2 us)
Async XLA Ops:
  0.6 1.2 copy-start.6
  1.9 1.2 copy-start.7
  3.1 0.7 copy-start.10
  9.5 118.0 %all-to-all-start.1 = ((bf16[16,32,7296]{2,1,0:T(8,128)(2,1)}), bf16[16,32,7296]{2,1,0:T(8,128)(2,1)}, u32[]{:S(2)}, u32[]{:S(2)}) async-start(bf16[16,32,7296]{2,1,0:T(8,128)(2,1)} %bitcast.138), calls=%async_computation.1 | async-start | bytes 14942208 | tf_op jit(solution)/shard_map/all_to_all | solution.py:355
  127.5 45.2 %all-to-all-start = ((bf16[16,32,1024]{2,1,0:T(8,128)(2,1)}), bf16[16,32,1024]{2,1,0:T(8,128)(2,1)S(1)}, u32[]{:S(2)}, u32[]{:S(2)}) async-start(bf16[16,32,1024]{2,1,0:T(8,128)(2,1)} %bitcast.2), calls=%async_computation | async-start | bytes 2097152 | tf_op jit(solution)/shard_map/all_to_all | solution.py:355
  138.1 74.3 %collective-permute-start = (bf16[512,3584]{1,0:T(8,128)(2,1)}, bf16[512,3584]{1,0:T(8,128)(2,1)}, u32[]{:S(2)}, u32[]{:S(2)}) collective-permute-start(bf16[512,3584]{1,0:T(8,128)(2,1)} %pick.2), channel_id=1, source_target_pairs={{0,16},{16,0},{32,48},{48,32},{64,80},{80,64},{96,112},{112,96},{1... | collective-permute-start | bytes 11010056 | tf_op jit(solution)/shard_map/ppermute | solution.py:371
  169.5 1.1 copy-start.4
  170.7 1.2 copy-start.5
  171.8 0.9 copy-start.8
  172.7 1.4 copy-start.3
  174.1 1.1 copy-start.9
  190.1 2.1 copy-start
  192.2 10.5 %copy-start.22 = (s32[4]{0:T(128)S(1)}, s32[4]{0:T(128)}, u32[]{:S(2)}) copy-start(s32[4]{0:T(128)} %constant.55.clone) | copy-start | bytes 52
  192.2 73.7 %all-to-all-start.2 = ((bf16[16,32,4224]{2,1,0:T(8,128)(2,1)}), bf16[16,32,4224]{2,1,0:T(8,128)(2,1)}, u32[]{:S(2)}, u32[]{:S(2)}) async-start(bf16[16,32,4224]{2,1,0:T(8,128)(2,1)} %bitcast.125), calls=%async_computation.2 | async-start | bytes 8650752 | tf_op jit(solution)/shard_map/all_to_all | solution.py:355
  199.6 12.7 %collective-permute-start.1 = (bf16[2,512,768]{2,1,0:T(8,128)(2,1)S(1)}, bf16[2,512,768]{2,1,0:T(8,128)(2,1)}, u32[]{:S(2)}, u32[]{:S(2)}) collective-permute-start(bf16[2,512,768]{2,1,0:T(8,128)(2,1)S(1)} %get-tuple-element.23.h_ref.rhs_ref), channel_id=1, source_target_pairs={{0,16},{16,0},{32,48},{48,32},{64,80},{80,64},{96,112},{112,96},{1... | collective-permute-start | bytes 4718600 | tf_op jit(solution)/shard_map/ppermute | solution.py:387
  200.1 7.3 %collective-permute-start.6 = (bf16[1,512,768]{2,1,0:T(8,128)(2,1)S(1)}, bf16[1,512,768]{2,1,0:T(8,128)(2,1)}, u32[]{:S(2)}, u32[]{:S(2)}) collective-permute-start(bf16[1,512,768]{2,1,0:T(8,128)(2,1)S(1)} %bitcast.130), channel_id=1, source_target_pairs={{0,16},{16,0},{32,48},{48,32},{64,80},{80,64},{96,112},{112,96},{1... | collective-permute-start | bytes 2359304 | tf_op jit(solution)/shard_map/ppermute | solution.py:374
  202.4 4.9 %collective-permute-start.5 = (bf16[512,512]{1,0:T(8,128)(2,1)}, bf16[512,512]{1,0:T(8,128)(2,1)}, u32[]{:S(2)}, u32[]{:S(2)}) collective-permute-start(bf16[512,512]{1,0:T(8,128)(2,1)} %pick.3), channel_id=1, source_target_pairs={{0,16},{16,0},{32,48},{48,32},{64,80},{80,64},{96,112},{112,96},{1... | collective-permute-start | bytes 1572872 | tf_op jit(solution)/shard_map/ppermute | solution.py:385
  218.5 58.0 %collective-permute-start.13 = (bf16[320,768]{1,0:T(8,128)(2,1)}, bf16[320,768]{1,0:T(8,128)(2,1)}, u32[]{:S(2)}, u32[]{:S(2)}) collective-permute-start(bf16[320,768]{1,0:T(8,128)(2,1)} %pad_maximum_fusion.1), channel_id=1, source_target_pairs={{0,96},{16,112},{32,0},{48,16},{64,32},{80,48},{96,64},{112,80},{1... | collective-permute-start | bytes 1474568 | tf_op jit(solution)/shard_map/ppermute | solution.py:337
  222.4 48.5 %collective-permute-start.2 = (bf16[256,768]{1,0:T(8,128)(2,1)}, bf16[256,768]{1,0:T(8,128)(2,1)}, u32[]{:S(2)}, u32[]{:S(2)}) collective-permute-start(bf16[256,768]{1,0:T(8,128)(2,1)} %get-tuple-element.58), channel_id=1, source_target_pairs={{0,32},{16,48},{32,64},{48,80},{64,96},{80,112},{96,0},{112,16},{1... | collective-permute-start | bytes 1179656 | tf_op jit(solution)/shard_map/ppermute | solution.py:337
  222.4 13.0 %copy-start.13 = (s32[6]{0:T(128)S(1)}, s32[6]{0:T(128)}, u32[]{:S(2)}) copy-start(s32[6]{0:T(128)} %constant.56.clone.ff_ids) | copy-start | bytes 76
  222.4 52.5 %collective-permute-start.10 = (bf16[256,768]{1,0:T(8,128)(2,1)}, bf16[256,768]{1,0:T(8,128)(2,1)}, u32[]{:S(2)}, u32[]{:S(2)}) collective-permute-start(bf16[256,768]{1,0:T(8,128)(2,1)} %get-tuple-element.60), channel_id=1, source_target_pairs={{0,96},{16,112},{32,0},{48,16},{64,32},{80,48},{96,64},{112,80},{1... | collective-permute-start | bytes 1179656 | tf_op jit(solution)/shard_map/ppermute | solution.py:337
  232.0 16.6 %copy-start.1 = (bf16[4,384,768]{2,1,0:T(8,128)(2,1)}, bf16[4,384,768]{2,1,0:T(8,128)(2,1)S(1)}, u32[]{:S(2)}) copy-start(bf16[4,384,768]{2,1,0:T(8,128)(2,1)S(1)} %partials.7) | copy-start | bytes 7077892
  232.1 16.4 %collective-permute-start.16 = (bf16[192,768]{1,0:T(8,128)(2,1)S(1)}, bf16[192,768]{1,0:T(8,128)(2,1)S(1)}, u32[]{:S(2)}, u32[]{:S(2)}) collective-permute-start(bf16[192,768]{1,0:T(8,128)(2,1)S(1)} %get-tuple-element.56), channel_id=1, source_target_pairs={{0,32},{16,48},{32,64},{48,80},{64,96},{80,112},{96,0},{112,16},{1... | collective-permute-start | bytes 884744 | tf_op jit(solution)/shard_map/ppermute | solution.py:337
  232.2 16.4 %collective-permute-start.19 = (bf16[192,768]{1,0:T(8,128)(2,1)S(1)}, bf16[192,768]{1,0:T(8,128)(2,1)S(1)}, u32[]{:S(2)}, u32[]{:S(2)}) collective-permute-start(bf16[192,768]{1,0:T(8,128)(2,1)S(1)} %get-tuple-element.57), channel_id=1, source_target_pairs={{0,96},{16,112},{32,0},{48,16},{64,32},{80,48},{96,64},{112,80},{1... | collective-permute-start | bytes 884744 | tf_op jit(solution)/shard_map/ppermute | solution.py:337
  248.5 17.5 %copy-start.11 = (s32[128,2]{0,1:T(2,128)S(1)}, s32[128,2]{0,1:T(2,128)}, u32[]{:S(2)}) copy-start(s32[128,2]{0,1:T(2,128)} %param.11) | copy-start | bytes 3076
  248.5 35.6 %collective-permute-start.7 = (bf16[320,768]{1,0:T(8,128)(2,1)S(1)}, bf16[320,768]{1,0:T(8,128)(2,1)S(1)}, u32[]{:S(2)}, u32[]{:S(2)}) collective-permute-start(bf16[320,768]{1,0:T(8,128)(2,1)S(1)} %pad_maximum_fusion), channel_id=1, source_target_pairs={{0,32},{16,48},{32,64},{48,80},{64,96},{80,112},{96,0},{112,16},{1... | collective-permute-start | bytes 1474568 | tf_op jit(solution)/shard_map/ppermute | solution.py:337
  249.6 31.3 %collective-permute-start.17 = (bf16[192,768]{1,0:T(8,128)(2,1)}, bf16[192,768]{1,0:T(8,128)(2,1)}, u32[]{:S(2)}, u32[]{:S(2)}) collective-permute-start(bf16[192,768]{1,0:T(8,128)(2,1)} %get-tuple-element.54), channel_id=1, source_target_pairs={{0,32},{16,48},{32,64},{48,80},{64,96},{80,112},{96,0},{112,16},{1... | collective-permute-start | bytes 884744 | tf_op jit(solution)/shard_map/ppermute | solution.py:337
  266.0 5.0 %copy-start.21 = (bf16[192,768]{1,0:T(8,128)(2,1)S(1)}, bf16[192,768]{1,0:T(8,128)(2,1)}, u32[]{:S(2)}) copy-start(bf16[192,768]{1,0:T(8,128)(2,1)} %get-tuple-element.55) | copy-start | bytes 884740
  266.0 13.8 %copy-start.20 = (bf16[64,768]{1,0:T(8,128)(2,1)S(1)}, bf16[64,768]{1,0:T(8,128)(2,1)}, u32[]{:S(2)}) copy-start(bf16[64,768]{1,0:T(8,128)(2,1)} %get-tuple-element.65) | copy-start | bytes 294916
  270.9 11.4 %copy-start.2 = (bf16[4,384,768]{2,1,0:T(8,128)(2,1)S(1)}, bf16[4,384,768]{2,1,0:T(8,128)(2,1)}, u32[]{:S(2)}) copy-start(bf16[4,384,768]{2,1,0:T(8,128)(2,1)} %copy-done.1) | copy-start | bytes 7077892
  270.9 16.4 %copy-start.19 = (bf16[64,768]{1,0:T(8,128)(2,1)S(1)}, bf16[64,768]{1,0:T(8,128)(2,1)}, u32[]{:S(2)}) copy-start(bf16[64,768]{1,0:T(8,128)(2,1)} %get-tuple-element.68) | copy-start | bytes 294916
  270.9 11.4 %collective-permute-start.20 = (bf16[192,768]{1,0:T(8,128)(2,1)S(1)}, bf16[192,768]{1,0:T(8,128)(2,1)S(1)}, u32[]{:S(2)}, u32[]{:S(2)}) collective-permute-start(bf16[192,768]{1,0:T(8,128)(2,1)S(1)} %copy-done.21), channel_id=1, source_target_pairs={{0,96},{16,112},{32,0},{48,16},{64,32},{80,48},{96,64},{112,80},{1... | collective-permute-start | bytes 884744 | tf_op jit(solution)/shard_map/ppermute | solution.py:337
  276.4 13.3 %collective-permute-start.3 = (bf16[256,768]{1,0:T(8,128)(2,1)S(1)}, bf16[256,768]{1,0:T(8,128)(2,1)S(1)}, u32[]{:S(2)}, u32[]{:S(2)}) collective-permute-start(bf16[256,768]{1,0:T(8,128)(2,1)S(1)} %get-tuple-element.42), channel_id=1, source_target_pairs={{0,32},{16,48},{32,64},{48,80},{64,96},{80,112},{96,0},{112,16},{1... | collective-permute-start | bytes 1179656 | tf_op jit(solution)/shard_map/ppermute | solution.py:337
  276.5 14.3 %collective-permute-start.11 = (bf16[256,768]{1,0:T(8,128)(2,1)S(1)}, bf16[256,768]{1,0:T(8,128)(2,1)S(1)}, u32[]{:S(2)}, u32[]{:S(2)}) collective-permute-start(bf16[256,768]{1,0:T(8,128)(2,1)S(1)} %get-tuple-element.43), channel_id=1, source_target_pairs={{0,96},{16,112},{32,0},{48,16},{64,32},{80,48},{96,64},{112,80},{1... | collective-permute-start | bytes 1179656 | tf_op jit(solution)/shard_map/ppermute | solution.py:337
  280.9 26.9 %collective-permute-start.14 = (bf16[320,768]{1,0:T(8,128)(2,1)S(1)}, bf16[320,768]{1,0:T(8,128)(2,1)S(1)}, u32[]{:S(2)}, u32[]{:S(2)}) collective-permute-start(bf16[320,768]{1,0:T(8,128)(2,1)S(1)} %add_convert_fusion.2), channel_id=1, source_target_pairs={{0,96},{16,112},{32,0},{48,16},{64,32},{80,48},{96,64},{112,80},{1... | collective-permute-start | bytes 1474568 | tf_op jit(solution)/shard_map/ppermute | solution.py:337
  283.4 12.6 %collective-permute-start.18 = (bf16[192,768]{1,0:T(8,128)(2,1)S(1)}, bf16[192,768]{1,0:T(8,128)(2,1)S(1)}, u32[]{:S(2)}, u32[]{:S(2)}) collective-permute-start(bf16[192,768]{1,0:T(8,128)(2,1)S(1)} %get-tuple-element.52), channel_id=1, source_target_pairs={{0,32},{16,48},{32,64},{48,80},{64,96},{80,112},{96,0},{112,16},{1... | collective-permute-start | bytes 884744 | tf_op jit(solution)/shard_map/ppermute | solution.py:337
  284.2 23.5 %collective-permute-start.21 = (bf16[192,768]{1,0:T(8,128)(2,1)S(1)}, bf16[192,768]{1,0:T(8,128)(2,1)S(1)}, u32[]{:S(2)}, u32[]{:S(2)}) collective-permute-start(bf16[192,768]{1,0:T(8,128)(2,1)S(1)} %get-tuple-element.53), channel_id=1, source_target_pairs={{0,96},{16,112},{32,0},{48,16},{64,32},{80,48},{96,64},{112,80},{1... | collective-permute-start | bytes 884744 | tf_op jit(solution)/shard_map/ppermute | solution.py:337
  287.4 20.4 %copy-start.18 = (bf16[64,768]{1,0:T(8,128)(2,1)S(1)}, bf16[64,768]{1,0:T(8,128)(2,1)}, u32[]{:S(2)}) copy-start(bf16[64,768]{1,0:T(8,128)(2,1)} %get-tuple-element.64) | copy-start | bytes 294916
  287.4 24.5 %copy-start.17 = (bf16[64,768]{1,0:T(8,128)(2,1)S(1)}, bf16[64,768]{1,0:T(8,128)(2,1)}, u32[]{:S(2)}) copy-start(bf16[64,768]{1,0:T(8,128)(2,1)} %get-tuple-element.67) | copy-start | bytes 294916
  289.8 22.2 %collective-permute-start.8 = (bf16[320,768]{1,0:T(8,128)(2,1)S(1)}, bf16[320,768]{1,0:T(8,128)(2,1)S(1)}, u32[]{:S(2)}, u32[]{:S(2)}) collective-permute-start(bf16[320,768]{1,0:T(8,128)(2,1)S(1)} %add_convert_fusion.5), channel_id=1, source_target_pairs={{0,32},{16,48},{32,64},{48,80},{64,96},{80,112},{96,0},{112,16},{1... | collective-permute-start | bytes 1474568 | tf_op jit(solution)/shard_map/ppermute | solution.py:337
  292.1 21.6 %collective-permute-start.4 = (bf16[256,768]{1,0:T(8,128)(2,1)S(1)}, bf16[256,768]{1,0:T(8,128)(2,1)S(1)}, u32[]{:S(2)}, u32[]{:S(2)}) collective-permute-start(bf16[256,768]{1,0:T(8,128)(2,1)S(1)} %get-tuple-element.40), channel_id=1, source_target_pairs={{0,32},{16,48},{32,64},{48,80},{64,96},{80,112},{96,0},{112,16},{1... | collective-permute-start | bytes 1179656 | tf_op jit(solution)/shard_map/ppermute | solution.py:337
  296.1 20.0 %collective-permute-start.12 = (bf16[256,768]{1,0:T(8,128)(2,1)S(1)}, bf16[256,768]{1,0:T(8,128)(2,1)S(1)}, u32[]{:S(2)}, u32[]{:S(2)}) collective-permute-start(bf16[256,768]{1,0:T(8,128)(2,1)S(1)} %get-tuple-element.41), channel_id=1, source_target_pairs={{0,96},{16,112},{32,0},{48,16},{64,32},{80,48},{96,64},{112,80},{1... | collective-permute-start | bytes 1179656 | tf_op jit(solution)/shard_map/ppermute | solution.py:337
  307.8 17.2 %copy-start.16 = (bf16[64,768]{1,0:T(8,128)(2,1)S(1)}, bf16[64,768]{1,0:T(8,128)(2,1)}, u32[]{:S(2)}) copy-start(bf16[64,768]{1,0:T(8,128)(2,1)} %get-tuple-element.63) | copy-start | bytes 294916
  307.9 17.0 %collective-permute-start.15 = (bf16[320,768]{1,0:T(8,128)(2,1)S(1)}, bf16[320,768]{1,0:T(8,128)(2,1)S(1)}, u32[]{:S(2)}, u32[]{:S(2)}) collective-permute-start(bf16[320,768]{1,0:T(8,128)(2,1)S(1)} %add_convert_fusion.1), channel_id=1, source_target_pairs={{0,96},{16,112},{32,0},{48,16},{64,32},{80,48},{96,64},{112,80},{1... | collective-permute-start | bytes 1474568 | tf_op jit(solution)/shard_map/ppermute | solution.py:337
  312.0 13.1 %copy-start.15 = (bf16[64,768]{1,0:T(8,128)(2,1)S(1)}, bf16[64,768]{1,0:T(8,128)(2,1)}, u32[]{:S(2)}) copy-start(bf16[64,768]{1,0:T(8,128)(2,1)} %get-tuple-element.62) | copy-start | bytes 294916
  312.1 13.1 %collective-permute-start.9 = (bf16[320,768]{1,0:T(8,128)(2,1)S(1)}, bf16[320,768]{1,0:T(8,128)(2,1)S(1)}, u32[]{:S(2)}, u32[]{:S(2)}) collective-permute-start(bf16[320,768]{1,0:T(8,128)(2,1)S(1)} %add_convert_fusion.4), channel_id=1, source_target_pairs={{0,32},{16,48},{32,64},{48,80},{64,96},{80,112},{96,0},{112,16},{1... | collective-permute-start | bytes 1474568 | tf_op jit(solution)/shard_map/ppermute | solution.py:337
  325.1 0.8 copy-start.14
  326.1 2.8 slice-start
  (1 other events, 0.7 us)

commit v2 on v1

v2 whole, which is shorter than its diff:
```python
import functools

import jax
import jax.numpy as jnp
from jax import lax
from jax.experimental import pallas as pl
from jax.experimental.pallas import tpu as pltpu
from jax.sharding import PartitionSpec as P

BF = jnp.bfloat16
F32 = jnp.float32
SLICE = 512
PART_A = 256
PART_B = SLICE - PART_A
GROUP = SLICE + PART_A
SLICES = 8
CAP = 32
LANES = 128


def params(mib):
    return pltpu.CompilerParams(vmem_limit_bytes=mib * 1024 * 1024)


def in_hbm(x):
    return pltpu.with_memory_space_constraint(x, pltpu.HBM)


def dot_nn(a, b):
    return lax.dot_general(a, b, (((1,), (0,)), ((), ())), preferred_element_type=F32)


def dot_nt(a, b):
    return lax.dot_general(a, b, (((1,), (1,)), ((), ())), preferred_element_type=F32)


def dot_tn(a, b):
    return lax.dot_general(a, b, (((0,), (0,)), ((), ())), preferred_element_type=F32)


def pack_kernel(ids_ref, gates_ref, tok_ref, dy_ref, first_ref, second_ref, hot_ref, *, step_experts):
    tokens = ids_ref.shape[1]
    base = pl.program_id(0) * step_experts
    expert = lax.broadcasted_iota(jnp.int32, (8, tokens), 0) + base
    zero = jnp.zeros((8, tokens), F32)
    is_0 = ids_ref[0:1, :] == expert
    is_1 = ids_ref[1:2, :] == expert
    named = is_0 | is_1
    member = jnp.where(named, 1.0, 0.0).astype(BF)
    row = lax.broadcasted_iota(jnp.int32, (tokens, tokens), 0)
    col = lax.broadcasted_iota(jnp.int32, (tokens, tokens), 1)
    earlier = jnp.where(row < col, 1.0, 0.0).astype(BF)
    place = jnp.where(named, dot_nn(member, earlier), -1.0)
    gates = gates_ref[...].astype(F32)
    weight = jnp.where(is_0, gates[0:1, :], zero) + jnp.where(is_1, gates[1:2, :], zero)
    rows = step_experts * CAP
    place_all = jnp.broadcast_to(place[:step_experts, None, :], (step_experts, CAP, tokens)).reshape(rows, tokens)
    weight_all = jnp.broadcast_to(weight[:step_experts, None, :], (step_experts, CAP, tokens)).reshape(rows, tokens)
    slot = (lax.broadcasted_iota(jnp.int32, (rows, tokens), 0) % CAP).astype(F32)
    hot = jnp.where(place_all == slot, 1.0, 0.0)
    slot_gate = jnp.sum(hot * weight_all, axis=1, keepdims=True)
    first_ref[:, SLICES * GROUP :] = jnp.broadcast_to(slot_gate, (rows, LANES)).astype(BF)
    hot = hot.astype(BF)
    hot_ref[...] = hot
    for q in range(SLICES):
        cols = slice(q * SLICE, (q + 1) * SLICE)
        first_ref[:, q * GROUP : q * GROUP + SLICE] = dot_nn(hot, tok_ref[:, cols]).astype(BF)
        grads = dot_nn(hot, dy_ref[:, cols]).astype(BF)
        first_ref[:, q * GROUP + SLICE : (q + 1) * GROUP] = grads[:, :PART_A]
        second_ref[:, q * PART_B : (q + 1) * PART_B] = grads[:, PART_A:]


def pack(ids, gates, tokens_in, out_grad, slots):
    steps = 4
    tok_dev, width = tokens_in.shape
    rows = slots // steps
    wide = SLICES * GROUP + LANES
    whole = lambda shape: pl.BlockSpec(shape, lambda i: (0, 0))
    return pl.pallas_call(
        functools.partial(pack_kernel, step_experts=rows // CAP),
        grid=(steps,),
        in_specs=[whole((2, tok_dev)), whole((2, tok_dev)), whole((tok_dev, width)), whole((tok_dev, width))],
        out_specs=[
            pl.BlockSpec((rows, wide), lambda i: (i, 0)),
            pl.BlockSpec((rows, SLICES * PART_B), lambda i: (i, 0)),
            pl.BlockSpec((rows, tok_dev), lambda i: (i, 0)),
        ],
        out_shape=[
            pltpu.HBM((slots, wide), BF),
            pltpu.HBM((slots, SLICES * PART_B), BF),
            pltpu.HBM((slots, tok_dev), BF),
        ],
        compiler_params=params(24),
        name="pack",
    )(in_hbm(ids), in_hbm(gates), in_hbm(tokens_in), in_hbm(out_grad))


def pre_kernel(rows_ref, gate_ref, w_ref, wd_ref, u_ref, c1_ref, c2_ref, p_ref, gp_ref, pg_acc, pu_acc, *, per):
    step = pl.program_id(0)

    @pl.when(step == 0)
    def _():
        pg_acc[...] = jnp.zeros_like(pg_acc)
        pu_acc[...] = jnp.zeros_like(pu_acc)
        u_ref[...] = jnp.zeros_like(u_ref)

    x = jnp.concatenate([rows_ref[:, k * GROUP : k * GROUP + SLICE] for k in range(per)], axis=1)
    pg_acc[...] += dot_nn(x, w_ref[0])
    pu_acc[...] += dot_nn(x, w_ref[1])
    dy = jnp.concatenate([rows_ref[:, k * GROUP + SLICE : (k + 1) * GROUP] for k in range(per)], axis=1)
    u_ref[...] += dot_nn(dy, wd_ref[...].reshape(per * PART_A, wd_ref.shape[3]))

    @pl.when(step == pl.num_programs(0) - 1)
    def _():
        chunk = 32

        def one(i, carry):
            at = pl.ds(pl.multiple_of(i * chunk, chunk), chunk)
            pg = pg_acc[at, :]
            pu = pu_acc[at, :]
            g = gate_ref[at, :].astype(F32)[:, :1]
            s = jax.nn.sigmoid(pg)
            a = pg * s
            product = a * pu
            p_ref[at, :] = product.astype(BF)
            gp_ref[at, :] = (g * product).astype(BF)
            c1_ref[at, :] = g * (pu * s * (1.0 + pg * (1.0 - s)))
            c2_ref[at, :] = g * a
            return carry

        lax.fori_loop(0, pg_acc.shape[0] // chunk, one, 0)


def pre(first, w, wd):
    slots = first.shape[0]
    ff = wd.shape[3]
    per = 2
    whole = pl.BlockSpec((slots, ff), lambda q: (0, 0))
    return pl.pallas_call(
        functools.partial(pre_kernel, per=per),
        grid=(SLICES // per,),
        in_specs=[
            pl.BlockSpec((slots, per * GROUP), lambda q: (0, q)),
            pl.BlockSpec((slots, LANES), lambda q: (0, SLICES * GROUP // LANES)),
            pl.BlockSpec((2, per * SLICE, ff), lambda q: (0, q, 0)),
            pl.BlockSpec((per, 1, PART_A, ff), lambda q: (q, 0, 0, 0)),
        ],
        out_specs=[whole] * 5,
        out_shape=[
            jax.ShapeDtypeStruct((slots, ff), F32),
            jax.ShapeDtypeStruct((slots, ff), F32),
            jax.ShapeDtypeStruct((slots, ff), F32),
            jax.ShapeDtypeStruct((slots, ff), BF),
            jax.ShapeDtypeStruct((slots, ff), BF),
        ],
        scratch_shapes=[pltpu.VMEM((slots, ff), F32)] * 2,
        compiler_params=params(36),
        name="pre",
    )(first, first, w, wd)


def hidden_kernel(dy_ref, wd_ref, u_ref, c1_ref, c2_ref, p_ref, h_ref, gate_ref, u_acc, gate_acc):
    step = pl.program_id(0)
    u_acc[...] = u_ref[...] + dot_nn(dy_ref[...], wd_ref[...].reshape(dy_ref.shape[1], wd_ref.shape[3]))

    @pl.when(step == 0)
    def _():
        gate_acc[...] = jnp.zeros_like(gate_acc)

    chunk = 64

    def one(i, carry):
        at = pl.ds(pl.multiple_of(i * chunk, chunk), chunk)
        u = u_acc[at, :]
        h_ref[0, at, :] = (u * c1_ref[at, :]).astype(BF)
        h_ref[1, at, :] = (u * c2_ref[at, :]).astype(BF)
        both = u * p_ref[at, :].astype(F32)
        folded = both[:, :LANES]
        for k in range(1, both.shape[1] // LANES):
            folded += both[:, k * LANES : (k + 1) * LANES]
        gate_acc[at, :] += folded
        return carry

    lax.fori_loop(0, u_acc.shape[0] // chunk, one, 0)

    @pl.when(step == pl.num_programs(0) - 1)
    def _():
        total = jnp.sum(gate_acc[...], axis=1, keepdims=True)
        gate_ref[...] = jnp.broadcast_to(total, gate_ref.shape).astype(BF)


def hidden(second, wd, u_a, c1, c2, p):
    slots, ff = p.shape
    blk = 256
    col = pl.BlockSpec((slots, blk), lambda j: (0, j))
    depth = second.shape[1]
    return pl.pallas_call(
        hidden_kernel,
        grid=(ff // blk,),
        in_specs=[
            pl.BlockSpec((slots, depth), lambda j: (0, 0)),
            pl.BlockSpec((SLICES, 1, PART_B, blk), lambda j: (0, 1, 0, j)),
            col,
            col,
            col,
            col,
        ],
        out_specs=[pl.BlockSpec((2, slots, blk), lambda j: (0, 0, j)), pl.BlockSpec((slots, LANES), lambda j: (0, 0))],
        out_shape=[jax.ShapeDtypeStruct((2, slots, ff), BF), jax.ShapeDtypeStruct((slots, LANES), BF)],
        scratch_shapes=[pltpu.VMEM((slots, blk), F32), pltpu.VMEM((slots, LANES), F32)],
        compiler_params=params(24),
        name="hidden",
    )(second, wd, u_a, c1, c2, p)


def input_kernel(h_ref, w_ref, gate_ref, out_ref):
    out_ref[...] = (dot_nt(h_ref[0], w_ref[0]) + dot_nt(h_ref[1], w_ref[1])).astype(BF)

    @pl.when(pl.program_id(0) == pl.num_programs(0) - 1)
    def _():
        out_ref[:, out_ref.shape[1] - LANES :] = gate_ref[...]


def input_rows(h, w, gate):
    _, slots, ff = h.shape
    wide = w.shape[1] + LANES
    steps = 11
    blk = wide // steps
    return pl.pallas_call(
        input_kernel,
        grid=(steps,),
        in_specs=[
            pl.BlockSpec((2, slots, ff), lambda j: (0, 0, 0)),
            pl.BlockSpec((2, blk, ff), lambda j: (0, j, 0)),
            pl.BlockSpec((slots, LANES), lambda j: (0, 0)),
        ],
        out_specs=pl.BlockSpec((slots, blk), lambda j: (0, j)),
        out_shape=pltpu.HBM((slots, wide), BF),
        compiler_params=params(24),
        name="input_rows",
    )(h, w, gate)


def down_kernel(me_ref, own_ref, mate_ref, gp_ref, gp_mate_ref, up_ref, dn_ref):
    del me_ref
    part = (dot_tn(own_ref[...], gp_ref[...]) + dot_tn(mate_ref[...], gp_mate_ref[...])).astype(BF)
    up_ref[0] = part[: PART_A // 2]
    dn_ref[0] = part[PART_A // 2 :]


def down_slice(me_ref, step):
    me = me_ref[0]
    return 2 * ((me // 2 + 3 - step) % 4) + me % 2


def down_parts(me, own, mate, gp, gp_mate):
    slots, ff = gp.shape
    rows = pl.BlockSpec((slots, PART_A), lambda i, me: (0, 3 * down_slice(me, i) + 2))
    whole = pl.BlockSpec((slots, ff), lambda i, me: (0, 0))
    out = pl.BlockSpec((1, PART_A // 2, ff), lambda i, me: (i, 0, 0))
    return pl.pallas_call(
        down_kernel,
        grid_spec=pltpu.PrefetchScalarGridSpec(
            num_scalar_prefetch=1, grid=(4,), in_specs=[rows, rows, whole, whole], out_specs=[out, out]
        ),
        out_shape=[jax.ShapeDtypeStruct((4, PART_A // 2, ff), BF)] * 2,
        compiler_params=params(16),
        name="down_parts",
    )(me, own, mate, gp, gp_mate)


UNIT = SLICE // 2
EXTRA = PART_B // 4


def unit_part(own_ref, mate_ref, dy_ref, dy_mate_ref, h_ref, h_mate_ref, gp_ref, gp_mate_ref, out_ref):
    ff = gp_ref.shape[1]
    for k in range(2):
        part = dot_tn(own_ref[...], h_ref[k]) + dot_tn(mate_ref[...], h_mate_ref[k])
        out_ref[:UNIT, k * ff : (k + 1) * ff] = part.astype(BF)
    down = (dot_tn(dy_ref[...], gp_ref[...]) + dot_tn(dy_mate_ref[...], gp_mate_ref[...])).astype(BF)
    out_ref[UNIT:, :ff] = down[:EXTRA]
    out_ref[UNIT:, ff:] = down[EXTRA:]


def head_kernel(me_ref, *refs):
    del me_ref
    ins, (up_ref, dn_ref) = refs[:8], refs[8:]

    @pl.when(pl.program_id(0) == 0)
    def _():
        unit_part(*ins, up_ref)

    @pl.when(pl.program_id(0) == 1)
    def _():
        unit_part(*ins, dn_ref)


def rest_kernel(me_ref, *refs):
    del me_ref
    unit_part(*refs[:8], refs[8].at[0])


def units(me, first, mate_first, second, mate_second, h, h_mate, gp, gp_mate, head):
    _, slots, ff = h.shape

    def at(i, me_ref):
        me = me_ref[0]
        hop = (0 if head else 1) + i // 2
        z = me // 2
        turn = jnp.where(i % 2 == 0, z + 3 - hop, z + 1 + hop) % 4
        return 2 * turn + me % 2

    rows = pl.BlockSpec((slots, UNIT), lambda i, me: (0, 3 * at(i, me) + i % 2))
    grads = pl.BlockSpec((slots, PART_B // 2), lambda i, me: (0, 2 * at(i, me) + i % 2))
    hid = pl.BlockSpec((2, slots, ff), lambda i, me: (0, 0, 0))
    whole = pl.BlockSpec((slots, ff), lambda i, me: (0, 0))
    shape = (UNIT + EXTRA, 2 * ff)
    if head:
        steps = 2
        out_specs = [pl.BlockSpec(shape, lambda i, me: (0, 0))] * 2
        out_shape = [jax.ShapeDtypeStruct(shape, BF)] * 2
    else:
        steps = 6
        out_specs = pl.BlockSpec((1,) + shape, lambda i, me: (i, 0, 0))
        out_shape = jax.ShapeDtypeStruct((6,) + shape, BF)
    return pl.pallas_call(
        head_kernel if head else rest_kernel,
        grid_spec=pltpu.PrefetchScalarGridSpec(
            num_scalar_prefetch=1,
            grid=(steps,),
            in_specs=[rows, rows, grads, grads, hid, hid, whole, whole],
            out_specs=out_specs,
        ),
        out_shape=out_shape,
        compiler_params=params(24),
        name="units_head" if head else "units_rest",
    )(me, first, mate_first, second, mate_second, h, h_mate, gp, gp_mate)


def unpack_kernel(hot_ref, ids_ref, rows_ref, gates_ref, out_ref, gate_ref):
    out_ref[...] = dot_tn(hot_ref[...], rows_ref[...]).astype(BF)

    @pl.when(pl.program_id(0) == 0)
    def _():
        hot = hot_ref[...]
        expert = lax.broadcasted_iota(jnp.int32, hot.shape, 0) // CAP
        for k in range(2):
            chosen = jnp.where(expert == ids_ref[k : k + 1, :], hot.astype(F32), 0.0).astype(BF)
            gate_ref[k : k + 1, :] = dot_tn(gates_ref[...], chosen)[0:1, :].astype(BF)


def unpack(hot, ids, back, width):
    slots, tok_dev = hot.shape
    steps = 4
    whole = lambda shape: pl.BlockSpec(shape, lambda i: (0, 0))
    return pl.pallas_call(
        unpack_kernel,
        grid=(steps,),
        in_specs=[
            whole((slots, tok_dev)),
            whole((2, tok_dev)),
            pl.BlockSpec((slots, width // steps), lambda i: (0, i)),
            pl.BlockSpec((slots, LANES), lambda i: (0, width // LANES)),
        ],
        out_specs=[pl.BlockSpec((tok_dev, width // steps), lambda i: (0, i)), whole((2, tok_dev))],
        out_shape=[jax.ShapeDtypeStruct((tok_dev, width), BF), jax.ShapeDtypeStruct((2, tok_dev), BF)],
        compiler_params=params(16),
        name="unpack",
    )(hot, ids, in_hbm(back), in_hbm(back))


UP = [(i, (i + 2) % 8) for i in range(8)]
DOWN = [(i, (i - 2) % 8) for i in range(8)]
SWAP = [(i, i ^ 1) for i in range(8)]


def ring(parts, perm):
    total = parts[0]
    for part in parts[1:]:
        arrived = lax.ppermute(total, "dp", perm)
        total = (arrived.astype(F32) + part.astype(F32)).astype(BF)
    return total


def body(tokens_in, out_grad, expert_ids, gate_probs, gate_up, down_proj):
    width = tokens_in.shape[1]
    owners = lax.axis_size("expert")
    ff = gate_up.shape[3]
    slots = owners * CAP
    me = lax.axis_index("dp")

    ids = expert_ids.T
    first, second, hot = pack(ids, gate_probs.T, tokens_in, out_grad, slots)

    def exchange(rows):
        wide = rows.shape[1]
        got = lax.all_to_all(rows.reshape(owners, CAP, wide), "expert", split_axis=0, concat_axis=0, tiled=True)
        return got.reshape(slots, wide)

    def swap(x):
        return lax.ppermute(x, "dp", SWAP)

    first, gate_up, down_proj, me = lax.optimization_barrier((exchange(first), gate_up, down_proj, me))
    second = exchange(second)
    me = me.reshape(1).astype(jnp.int32)
    mate_first = swap(first)
    w = jnp.transpose(gate_up[:, :, 0], (1, 0, 2))
    wd = down_proj.reshape(SLICES, 2, PART_A, ff)
    u_a, c1, c2, p, gp = pre(first, w, wd)
    gp_mate = swap(gp)
    down_up, down_dn = down_parts(me, first, mate_first, gp, gp_mate)
    second, down_up, down_dn = lax.optimization_barrier((second, down_up, down_dn))
    grad_a = jnp.concatenate(
        [ring([down_up[j] for j in (0, 1, 2, 3)], UP), ring([down_dn[j] for j in (2, 1, 0, 3)], DOWN)], axis=0
    )

    mate_second = swap(second)
    h, gate_rows = hidden(second, wd, u_a, c1, c2, p)
    h_mate = swap(h)
    head_up, head_dn = units(me, first, mate_first, second, mate_second, h, h_mate, gp, gp_mate, True)
    h, head_up, head_dn = lax.optimization_barrier((h, head_up, head_dn))
    back = exchange(input_rows(h, w, gate_rows))
    rest = units(me, first, mate_first, second, mate_second, h, h_mate, gp, gp_mate, False)
    sum_up = ring([head_up, rest[0], rest[2], rest[4]], UP)
    sum_dn = ring([head_dn, rest[1], rest[3], rest[5]], DOWN)

    sums = jnp.concatenate([sum_up[:UNIT], sum_dn[:UNIT]], axis=0)
    gate_up_grad = sums.reshape(SLICE, 2, 1, ff)
    down_b = [t[UNIT:, k * ff : (k + 1) * ff] for t in (sum_up, sum_dn) for k in range(2)]
    down_grad = jnp.concatenate([grad_a] + down_b, axis=0)[:, None, :]

    input_grad, gate_grad = unpack(hot, ids, back, width)
    return (input_grad, gate_grad.T, gate_up_grad, down_grad)


def solution(mesh):
    placed = (
        P(("dp", "expert"), None),
        P(("dp", "expert"), None),
        P(("dp", "expert"), None),
        P(("dp", "expert"), None),
        P(None, None, "expert", None),
        P(None, "expert", None),
    )
    return jax.shard_map(
        body,
        mesh=mesh,
        in_specs=placed,
        out_specs=(
            P(("dp", "expert"), None),
            P(("dp", "expert"), None),
            P("dp", None, "expert", None),
            P("dp", "expert", None),
        ),
        check_vma=False,
    )
```

time: 331 us -> 302 us (0.912)
  local copies, waits for them, and re-layouts: 64.4 us -> 43.3 us
  waiting for transfers between devices: 130 us -> 146 us
  Pallas kernels: 74.4 us -> 60.5 us
  starting transfers between devices: 48.5 us -> 41 us
    slice x11 -> x2, local copies, waits for them, and re-layouts: 30.7 us -> 0.11 us  [body(): sums = jnp.concatenate([sum_up[:UNIT], sum_dn[:UNIT]], axis=0)]
    squeeze x3 -> x2, local copies, waits for them, and re-layouts: 16.1 us -> 0.7 us  [the longest x1 0.69 us: body(): down_up[j]]
    unnamed x47 -> x71, local copies, waits for them, and re-layouts: 14.9 us -> 29.3 us
    pallas_call x7 -> x4, Pallas kernels: 43.9 us -> 31.9 us  [the longest x2 14.7 us: units(): pl.pallas_call(head_kernel if head else rest_kernel, grid_spec=pltpu.Pref...]
    optimization_barrier x0 -> x1, local copies, waits for them, and re-layouts: none -> 11.9 us  [body(): lax.optimization_barrier((exchange(first), gate_up, down_proj, me))]
    all_to_all x3, waiting for transfers between devices: 99.7 us -> 109 us  [exchange(): lax.all_to_all(rows.reshape(owners, CAP, wide), 'expert', split_axis=0, c...]
    ppermute x18 -> x12, starting transfers between devices: 27.5 us -> 20.1 us  [ring(): arrived = lax.ppermute(total, 'dp', perm)]
    ppermute x4, waiting for transfers between devices: 0.01 us -> 5.24 us  [swap(): return lax.ppermute(x, 'dp', SWAP)]
  transfers between devices with their start and end apart: 25 -> 19, of which waited for: 10 -> 9; matrix products, arithmetic and copies ran while one was open for 18% -> 7% of each run, Pallas kernels for 21% -> 14%
where the time goes in v2:
time: 302 us; the launch traced here: 301 us
  waiting for transfers between devices  146 us (48%)
  Pallas kernels  60.5 us (20%)
  local copies, waits for them, and re-layouts  43.3 us (14%)
  starting transfers between devices  41 us (14%)
  other arithmetic  8.61 us (3%)
    all_to_all x3, waiting for transfers between devices, exchange(): lax.all_to_all(rows.reshape(owners, CAP, wide), 'expert', split_axis=0, c...  109 us
    ppermute x12, waiting for transfers between devices, ring(): arrived = lax.ppermute(total, 'dp', perm)  31.8 us
    unnamed x71, local copies, waits for them, and re-layouts  29.3 us
    ppermute x12, starting transfers between devices, ring(): arrived = lax.ppermute(total, 'dp', perm)  20.1 us
    all_to_all x3, starting transfers between devices, exchange(): lax.all_to_all(rows.reshape(owners, CAP, wide), 'expert', split_axis=0, c...  20.1 us
    pallas_call x2, Pallas kernels, units(): pl.pallas_call(head_kernel if head else rest_kernel, grid_spec=pltpu.Pref...  14.7 us
    pallas_call x1, Pallas kernels, pre(): pl.pallas_call(functools.partial(pre_kernel, per=per), grid=(SLICES // pe...  13.3 us
    pallas_call x1, Pallas kernels, input_rows(): pl.pallas_call(input_kernel, grid=(steps,), in_specs=[pl.BlockSpec((2, sl...  13.1 us
  transfers between devices with their start and end apart: 19, of which 9 were waited for; matrix products, arithmetic and copies ran while one was open for 7% of the time, Pallas kernels for 14%

profile of v2, /device:TPU:0, one launch (start us, length us, event | category | flops | bytes accessed | tf_op | source)
XLA Modules:
  0.0 300.8 jit_solution(16084042720650266961)
XLA Ops:
  0.6 6.8 %pack.1 = (bf16[512,6272]{1,0:T(8,128)(2,1)}, bf16[512,2048]{1,0:T(8,128)(2,1)}, bf16[512,128]{1,0:T(8,128)(2,1)}) custom-call(s32[2,128]{1,0:T(2,128)} %bitcast.80, bf16[2,128]{1,0:T(2,128)(2,1)} %bitcast.87, bf16[128,4096]{1,0:T(8,128)(2,1)} %tok_ref.1, bf16[128,4096]{1,0:T(8,128)(2,1)} %dy_ref.1), custom_call_target="tpu_custom_call" | custom-call | tf_op jit(solution)/shard_map/pack/pallas_call | solution.py:79
  7.4 7.2 %all-to-all-start.1 = ((bf16[16,32,6272]{2,1,0:T(8,128)(2,1)}), bf16[16,32,6272]{2,1,0:T(8,128)(2,1)}, u32[]{:S(2)}, u32[]{:S(2)}) async-start(bf16[16,32,6272]{2,1,0:T(8,128)(2,1)} %bitcast.83), calls=%async_computation.1 | async-start | bytes 12845056 | tf_op jit(solution)/shard_map/all_to_all | solution.py:398
  14.6 95.2 %all-to-all-done.1 = bf16[16,32,6272]{2,1,0:T(8,128)(2,1)} async-done(((bf16[16,32,6272]{2,1,0:T(8,128)(2,1)}), bf16[16,32,6272]{2,1,0:T(8,128)(2,1)}, u32[]{:S(2)}, u32[]{:S(2)}) %all-to-all-start.1) | async-done | bytes 6422560 | tf_op jit(solution)/shard_map/all_to_all | solution.py:398
  109.8 5.6 %all-to-all-start = ((bf16[16,32,2048]{2,1,0:T(8,128)(2,1)}), bf16[16,32,2048]{2,1,0:T(8,128)(2,1)S(1)}, u32[]{:S(2)}, u32[]{:S(2)}) async-start(bf16[16,32,2048]{2,1,0:T(8,128)(2,1)} %bitcast.84), calls=%async_computation | async-start | bytes 4194304 | tf_op jit(solution)/shard_map/all_to_all | solution.py:398
  115.4 11.9 %copy.13 = bf16[4096,2,1,768]{3,0,1,2:T(8,128)(2,1)} copy(bf16[4096,2,1,768]{3,1,2,0:T(2,128)(2,1)} %param.10) | data formatting | bytes 25165824 | tf_op jit(solution)/shard_map/optimization_barrier | solution.py:404
  127.3 2.8 copy-done.2
  130.1 13.3 %pre.1 = (f32[512,768]{1,0:T(8,128)S(1)}, f32[512,768]{1,0:T(8,128)S(1)}, f32[512,768]{1,0:T(8,128)S(1)}, bf16[512,768]{1,0:T(8,128)(2,1)S(1)}, bf16[512,768]{1,0:T(8,128)(2,1)S(1)}) custom-call(bf16[512,6272]{1,0:T(8,128)(2,1)} %bitcast.5.rows_ref.gate_ref.own_ref.refs_0_, bf16[512,6272]{1,0:T(8,128)(2,1)} %bitcast.5.rows_ref.gate_ref.own_ref.refs_0_, ...), custom_call_target="tpu_custom_call" | custom-call | tf_op jit(solution)/shard_map/pre/pallas_call | solution.py:139
  143.4 1.1 copy-done.14
  144.6 1.2 copy-done.16
  145.8 1.1 copy-done.18
  148.1 2.1 collective-permute-done.1.gp_mate_ref.refs_7_
  150.1 4.1 %down_parts.1 = (bf16[4,128,768]{2,1,0:T(8,128)(2,1)S(1)}, bf16[4,128,768]{2,1,0:T(8,128)(2,1)S(1)}) custom-call(s32[1]{0:T(128)} %bitcast.6.me_ref, bf16[512,6272]{1,0:T(8,128)(2,1)} %bitcast.5.rows_ref.gate_ref.own_ref.refs_0_, bf16[512,6272]{1,0:T(8,128)(2,1)} %collective-permute-done.mate_ref.refs_1_, ...), custom_call_target="tpu_custom_call" | custom-call | tf_op jit(solution)/shard_map/down_parts/pallas_call | solution.py:261
  157.2 3.3 %copy-done.3 = bf16[4096,1,768]{2,0,1:T(8,128)(2,1)S(1)} copy-done((bf16[4096,1,768]{2,0,1:T(8,128)(2,1)S(1)}, bf16[4096,1,768]{2,0,1:T(8,128)(2,1)}, u32[]{:S(2)}) %copy-start.3) | copy-done | bytes 6291480
  160.5 1.4 copy-done.15
  161.9 1.4 copy-done.17
  163.3 1.4 copy-done.19
  164.7 1.1 copy-done.25
  165.8 3.5 %hidden.1 = (bf16[2,512,768]{2,1,0:T(8,128)(2,1)S(1)}, bf16[512,128]{1,0:T(8,128)(2,1)S(1)}) custom-call(bf16[512,2048]{1,0:T(8,128)(2,1)S(1)} %bitcast.75, bf16[8,2,256,768]{3,2,1,0:T(8,128)(2,1)S(1)} %bitcast.79, f32[512,768]{1,0:T(8,128)S(1)} %copy-done.15, f32[512,768]{1,0:T(8,128)S(1)} %copy-done.17, f32[512,768]{1,0:T(8,128)S(1)} %copy-done.19, ...), custom_call_target="tpu_custom_call" | custom-call | tf_op jit(solution)/shard_map/hidden/pallas_call | solution.py:197
  169.7 3.2 %collective-permute-done.3.refs_5_ = bf16[2,512,768]{2,1,0:T(8,128)(2,1)S(1)} collective-permute-done((bf16[2,512,768]{2,1,0:T(8,128)(2,1)S(1)}, bf16[2,512,768]{2,1,0:T(8,128)(2,1)S(1)}, u32[]{:S(2)}, u32[]{:S(2)}) %collective-permute-start.3) | collective-permute-done | bytes 1572896 | tf_op jit(solution)/shard_map/ppermute | solution.py:402
  172.9 5.3 %units_head.1 = (bf16[320,1536]{1,0:T(8,128)(2,1)}, bf16[320,1536]{1,0:T(8,128)(2,1)}) custom-call(s32[1]{0:T(128)} %bitcast.6.me_ref, bf16[512,6272]{1,0:T(8,128)(2,1)} %bitcast.5.rows_ref.gate_ref.own_ref.refs_0_, bf16[512,6272]{1,0:T(8,128)(2,1)} %collective-permute-done.mate_ref.refs_1_, bf16[512,2048]{1,0:T(8,128)(2,1)S(1)} %bitcast.76, ...), custom_call_target="tpu_custom_call" | custom-call | tf_op jit(solution)/shard_map/units_head/pallas_call | solution.py:327
  178.3 1.9 collective-permute-start.4
  180.2 2.4 collective-permute-start.7
  182.6 1.6 copy-done.1
  184.2 1.4 copy-done.6
  185.6 1.6 copy-done.8
  187.2 1.1 copy-done.11
  188.4 1.4 copy-done.13
  189.8 9.3 %units_rest.1 = bf16[6,320,1536]{2,1,0:T(8,128)(2,1)S(1)} custom-call(s32[1]{0:T(128)} %bitcast.6.me_ref, bf16[512,6272]{1,0:T(8,128)(2,1)} %bitcast.5.rows_ref.gate_ref.own_ref.refs_0_, bf16[512,6272]{1,0:T(8,128)(2,1)} %collective-permute-done.mate_ref.refs_1_, bf16[512,2048]{1,0:T(8,128)(2,1)S(1)} %bitcast.77, bf16[512,2048]{1,0:T(8,128)(2,1)S(1)} %copy-done.8, ...), custom_call_target="tpu_custom_call" | custom-call | tf_op jit(solution)/shard_map/units_rest/pallas_call | solution.py:327
  199.1 5.6 %collective-permute-done.4 = bf16[320,1536]{1,0:T(8,128)(2,1)S(1)} collective-permute-done((bf16[320,1536]{1,0:T(8,128)(2,1)}, bf16[320,1536]{1,0:T(8,128)(2,1)S(1)}, u32[]{:S(2)}, u32[]{:S(2)}) %collective-permute-start.4) | collective-permute-done | bytes 983072 | tf_op jit(solution)/shard_map/ppermute | solution.py:381
  204.7 0.9 copy-done.29
  205.7 2.9 fusion.5
  209.0 2.8 collective-permute-start.8
  212.6 13.1 %input_rows.1 = bf16[512,4224]{1,0:T(8,128)(2,1)} custom-call(bf16[2,512,768]{2,1,0:T(8,128)(2,1)S(1)} %copy-done.6, bf16[2,4096,768]{2,1,0:T(8,128)(2,1)S(1)} %bitcast.73, bf16[512,128]{1,0:T(8,128)(2,1)S(1)} %get-tuple-element.49.gate_ref), custom_call_target="tpu_custom_call" | custom-call | tf_op jit(solution)/shard_map/input_rows/pallas_call | solution.py:229
  225.7 7.3 %all-to-all-start.2 = ((bf16[16,32,4224]{2,1,0:T(8,128)(2,1)}), bf16[16,32,4224]{2,1,0:T(8,128)(2,1)}, u32[]{:S(2)}, u32[]{:S(2)}) async-start(bf16[16,32,4224]{2,1,0:T(8,128)(2,1)} %bitcast.82), calls=%async_computation.2 | async-start | bytes 8650752 | tf_op jit(solution)/shard_map/all_to_all | solution.py:398
  233.1 3.3 %collective-permute-start.13 = (bf16[128,768]{1,0:T(8,128)(2,1)S(1)}, bf16[128,768]{1,0:T(8,128)(2,1)S(1)}, u32[]{:S(2)}, u32[]{:S(2)}) collective-permute-start(bf16[128,768]{1,0:T(8,128)(2,1)S(1)} %slice_bitcast_fusion.6), channel_id=1, source_target_pairs={{0,96},{16,112},{32,0},{48,16},{64,32},{80,48},{96,64},{112,80},{1... | collective-permute-start | bytes 589832 | tf_op jit(solution)/shard_map/ppermute | solution.py:381
  236.4 1.4 collective-permute-done.10
  237.7 1.0 fusion.11
  238.8 2.3 fusion.4
  241.3 3.1 %collective-permute-start.9 = (bf16[320,1536]{1,0:T(8,128)(2,1)S(1)}, bf16[320,1536]{1,0:T(8,128)(2,1)S(1)}, u32[]{:S(2)}, u32[]{:S(2)}) collective-permute-start(bf16[320,1536]{1,0:T(8,128)(2,1)S(1)} %get-tuple-element.63), channel_id=1, source_target_pairs={{0,96},{16,112},{32,0},{48,16},{64,32},{80,48},{96,64},{112,80},{1... | collective-permute-start | bytes 2949128 | tf_op jit(solution)/shard_map/ppermute | solution.py:381
  244.5 2.0 collective-permute-start.14
  246.5 1.0 collective-permute-done.11
  247.6 20.8 %collective-permute-done.14 = bf16[128,768]{1,0:T(8,128)(2,1)S(1)} collective-permute-done((bf16[128,768]{1,0:T(8,128)(2,1)S(1)}, bf16[128,768]{1,0:T(8,128)(2,1)S(1)}, u32[]{:S(2)}, u32[]{:S(2)}) %collective-permute-start.14) | collective-permute-done | bytes 196640 | tf_op jit(solution)/shard_map/ppermute | solution.py:381
  268.5 3.8 %collective-permute-start.15 = (bf16[128,768]{1,0:T(8,128)(2,1)S(1)}, bf16[128,768]{1,0:T(8,128)(2,1)S(1)}, u32[]{:S(2)}, u32[]{:S(2)}) collective-permute-start(bf16[128,768]{1,0:T(8,128)(2,1)S(1)} %fusion.7), channel_id=1, source_target_pairs={{0,96},{16,112},{32,0},{48,16},{64,32},{80,48},{96,64},{112,80},{1... | collective-permute-start | bytes 589832 | tf_op jit(solution)/shard_map/ppermute | solution.py:381
  272.3 3.1 %collective-permute-done.15 = bf16[128,768]{1,0:T(8,128)(2,1)S(1)} collective-permute-done((bf16[128,768]{1,0:T(8,128)(2,1)S(1)}, bf16[128,768]{1,0:T(8,128)(2,1)S(1)}, u32[]{:S(2)}, u32[]{:S(2)}) %collective-permute-start.15) | collective-permute-done | bytes 196640 | tf_op jit(solution)/shard_map/ppermute | solution.py:381
  275.5 2.0 fusion.3
  278.6 1.3 reshape.67
  281.8 14.2 %all-to-all-done.2 = bf16[16,32,4224]{2,1,0:T(8,128)(2,1)} async-done(((bf16[16,32,4224]{2,1,0:T(8,128)(2,1)}), bf16[16,32,4224]{2,1,0:T(8,128)(2,1)}, u32[]{:S(2)}, u32[]{:S(2)}) %all-to-all-start.2) | async-done | bytes 4325408 | tf_op jit(solution)/shard_map/all_to_all | solution.py:398
  295.9 4.9 %unpack.1 = (bf16[128,4096]{1,0:T(8,128)(2,1)}, bf16[2,128]{1,0:T(2,128)(2,1)}) custom-call(bf16[512,128]{1,0:T(8,128)(2,1)S(1)} %copy-done.26, s32[2,128]{1,0:T(2,128)S(1)} %bitcast.81, bf16[512,4224]{1,0:T(8,128)(2,1)} %bitcast.11.rows_ref.gates_ref, bf16[512,4224]{1,0:T(8,128)(2,1)} %bitcast.11.rows_ref.gates_ref), custom_call_target="tpu_custom_call" | custom-call | tf_op jit(solution)/shard_map/unpack/pallas_call | solution.py:357
  (87 shorter events, 9.1 us)
Async XLA Ops:
  7.4 102.4 %all-to-all-start.1 = ((bf16[16,32,6272]{2,1,0:T(8,128)(2,1)}), bf16[16,32,6272]{2,1,0:T(8,128)(2,1)}, u32[]{:S(2)}, u32[]{:S(2)}) async-start(bf16[16,32,6272]{2,1,0:T(8,128)(2,1)} %bitcast.83), calls=%async_computation.1 | async-start | bytes 12845056 | tf_op jit(solution)/shard_map/all_to_all | solution.py:398
  109.8 40.3 %collective-permute-start = (bf16[512,6272]{1,0:T(8,128)(2,1)}, bf16[512,6272]{1,0:T(8,128)(2,1)}, u32[]{:S(2)}, u32[]{:S(2)}) collective-permute-start(bf16[512,6272]{1,0:T(8,128)(2,1)} %bitcast.5.rows_ref.gate_ref.own_ref.refs_0_), channel_id=1, source_target_pairs={{0,16},{16,0},{32,48},{48,32},{64,80},{80,64},{96,112},{112,96},{1... | collective-permute-start | bytes 19267592 | tf_op jit(solution)/shard_map/ppermute | solution.py:402
  109.8 47.1 %all-to-all-start = ((bf16[16,32,2048]{2,1,0:T(8,128)(2,1)}), bf16[16,32,2048]{2,1,0:T(8,128)(2,1)S(1)}, u32[]{:S(2)}, u32[]{:S(2)}) async-start(bf16[16,32,2048]{2,1,0:T(8,128)(2,1)} %bitcast.84), calls=%async_computation | async-start | bytes 4194304 | tf_op jit(solution)/shard_map/all_to_all | solution.py:398
  127.3 2.8 copy-start.2
  143.4 1.1 copy-start.14
  144.6 1.2 copy-start.16
  145.8 1.1 copy-start.18
  147.8 2.3 collective-permute-start.1
  156.9 16.0 %copy-start = (bf16[16,32,2048]{2,1,0:T(8,128)(2,1)}, bf16[16,32,2048]{2,1,0:T(8,128)(2,1)S(1)}, u32[]{:S(2)}) copy-start(bf16[16,32,2048]{2,1,0:T(8,128)(2,1)S(1)} %all-to-all-done) | copy-start | bytes 6291460
  156.9 16.0 %collective-permute-start.2 = (bf16[512,2048]{1,0:T(8,128)(2,1)S(1)}, bf16[512,2048]{1,0:T(8,128)(2,1)S(1)}, u32[]{:S(2)}, u32[]{:S(2)}) collective-permute-start(bf16[512,2048]{1,0:T(8,128)(2,1)S(1)} %bitcast.74), channel_id=1, source_target_pairs={{0,16},{16,0},{32,48},{48,32},{64,80},{80,64},{96,112},{112,96},{1... | collective-permute-start | bytes 6291464 | tf_op jit(solution)/shard_map/ppermute | solution.py:402
  157.2 3.3 %copy-start.3 = (bf16[4096,1,768]{2,0,1:T(8,128)(2,1)S(1)}, bf16[4096,1,768]{2,0,1:T(8,128)(2,1)}, u32[]{:S(2)}) copy-start(bf16[4096,1,768]{2,0,1:T(8,128)(2,1)} %param.11) | copy-start | bytes 18874372
  160.5 1.4 copy-start.15
  161.9 1.4 copy-start.17
  163.3 1.4 copy-start.19
  164.7 1.1 copy-start.25
  165.8 7.1 %copy-start.10 = (bf16[512,768]{1,0:T(8,128)(2,1)S(1)}, bf16[512,768]{1,0:T(8,128)(2,1)}, u32[]{:S(2)}) copy-start(bf16[512,768]{1,0:T(8,128)(2,1)} %copy-done.9) | copy-start | bytes 2359300
  169.4 8.9 %copy-start.5 = (bf16[2,512,768]{2,1,0:T(8,128)(2,1)}, bf16[2,512,768]{2,1,0:T(8,128)(2,1)S(1)}, u32[]{:S(2)}) copy-start(bf16[2,512,768]{2,1,0:T(8,128)(2,1)S(1)} %get-tuple-element.48.refs_4_.h_ref) | copy-start | bytes 4718596
  169.4 3.5 %collective-permute-start.3 = (bf16[2,512,768]{2,1,0:T(8,128)(2,1)S(1)}, bf16[2,512,768]{2,1,0:T(8,128)(2,1)S(1)}, u32[]{:S(2)}, u32[]{:S(2)}) collective-permute-start(bf16[2,512,768]{2,1,0:T(8,128)(2,1)S(1)} %get-tuple-element.48.refs_4_.h_ref), channel_id=1, source_target_pairs={{0,16},{16,0},{32,48},{48,32},{64,80},{80,64},{96,112},{112,96},{1... | collective-permute-start | bytes 4718600 | tf_op jit(solution)/shard_map/ppermute | solution.py:402
  172.9 5.4 %copy-start.12 = (bf16[2,512,768]{2,1,0:T(8,128)(2,1)}, bf16[2,512,768]{2,1,0:T(8,128)(2,1)S(1)}, u32[]{:S(2)}) copy-start(bf16[2,512,768]{2,1,0:T(8,128)(2,1)S(1)} %collective-permute-done.3.refs_5_) | copy-start | bytes 4718596
  172.9 5.4 %copy-start.7 = (bf16[512,2048]{1,0:T(8,128)(2,1)}, bf16[512,2048]{1,0:T(8,128)(2,1)S(1)}, u32[]{:S(2)}) copy-start(bf16[512,2048]{1,0:T(8,128)(2,1)S(1)} %collective-permute-done.2.refs_3_) | copy-start | bytes 6291460
  178.3 34.3 %slice-start = ((s8[12582912]{0:T(1024)(128)(4,1)}), s8[4194304]{0:T(1024)(128)(4,1)S(1)}, s32[]{:S(2)}) async-start(s8[12582912]{0:T(1024)(128)(4,1)} %bitcast.71), calls=%async_computation.3 | async-start | bytes 8388608
  178.3 34.3 %slice-start.1 = ((s8[12582912]{0:T(1024)(128)(4,1)}), s8[4194304]{0:T(1024)(128)(4,1)S(1)}, s32[]{:S(2)}) async-start(s8[12582912]{0:T(1024)(128)(4,1)} %bitcast.71), calls=%async_computation.4 | async-start | bytes 8388608
  178.3 34.3 %slice-start.2 = ((s8[12582912]{0:T(1024)(128)(4,1)}), s8[4194304]{0:T(1024)(128)(4,1)S(1)}, s32[]{:S(2)}) async-start(s8[12582912]{0:T(1024)(128)(4,1)} %bitcast.71), calls=%async_computation.5 | async-start | bytes 8388608
  178.3 26.4 %collective-permute-start.4 = (bf16[320,1536]{1,0:T(8,128)(2,1)}, bf16[320,1536]{1,0:T(8,128)(2,1)S(1)}, u32[]{:S(2)}, u32[]{:S(2)}) collective-permute-start(bf16[320,1536]{1,0:T(8,128)(2,1)} %get-tuple-element.52), channel_id=1, source_target_pairs={{0,32},{16,48},{32,64},{48,80},{64,96},{80,112},{96,0},{112,16},{1... | collective-permute-start | bytes 2949128 | tf_op jit(solution)/shard_map/ppermute | solution.py:381
  180.2 25.4 %collective-permute-start.7 = (bf16[320,1536]{1,0:T(8,128)(2,1)}, bf16[320,1536]{1,0:T(8,128)(2,1)}, u32[]{:S(2)}, u32[]{:S(2)}) collective-permute-start(bf16[320,1536]{1,0:T(8,128)(2,1)} %get-tuple-element.53), channel_id=1, source_target_pairs={{0,96},{16,112},{32,0},{48,16},{64,32},{80,48},{96,64},{112,80},{1... | collective-permute-start | bytes 2949128 | tf_op jit(solution)/shard_map/ppermute | solution.py:381
  182.6 1.6 copy-start.1
  184.2 1.4 copy-start.6
  185.6 1.6 copy-start.8
  187.2 1.1 copy-start.11
  188.4 1.4 copy-start.13
  199.1 9.5 %copy-start.4 = (bf16[6,320,1536]{2,1,0:T(8,128)(2,1)}, bf16[6,320,1536]{2,1,0:T(8,128)(2,1)S(1)}, u32[]{:S(2)}) copy-start(bf16[6,320,1536]{2,1,0:T(8,128)(2,1)S(1)} %units_rest.1) | copy-start | bytes 17694724
  199.1 12.7 %copy-start.23 = (bf16[4,128,768]{2,1,0:T(8,128)(2,1)S(1)}, bf16[4,128,768]{2,1,0:T(8,128)(2,1)}, u32[]{:S(2)}) copy-start(bf16[4,128,768]{2,1,0:T(8,128)(2,1)} %copy-done.22) | copy-start | bytes 2359300
  208.6 30.2 %collective-permute-start.5 = (bf16[320,1536]{1,0:T(8,128)(2,1)}, bf16[320,1536]{1,0:T(8,128)(2,1)S(1)}, u32[]{:S(2)}, u32[]{:S(2)}) collective-permute-start(bf16[320,1536]{1,0:T(8,128)(2,1)} %get-tuple-element.64), channel_id=1, source_target_pairs={{0,32},{16,48},{32,64},{48,80},{64,96},{80,112},{96,0},{112,16},{1... | collective-permute-start | bytes 2949128 | tf_op jit(solution)/shard_map/ppermute | solution.py:381
  209.0 29.8 %collective-permute-start.8 = (bf16[320,1536]{1,0:T(8,128)(2,1)S(1)}, bf16[320,1536]{1,0:T(8,128)(2,1)}, u32[]{:S(2)}, u32[]{:S(2)}) collective-permute-start(bf16[320,1536]{1,0:T(8,128)(2,1)S(1)} %get-tuple-element.65), channel_id=1, source_target_pairs={{0,96},{16,112},{32,0},{48,16},{64,32},{80,48},{96,64},{112,80},{1... | collective-permute-start | bytes 2949128 | tf_op jit(solution)/shard_map/ppermute | solution.py:381
  212.5 25.2 %collective-permute-start.10 = (bf16[128,768]{1,0:T(8,128)(2,1)}, bf16[128,768]{1,0:T(8,128)(2,1)}, u32[]{:S(2)}, u32[]{:S(2)}) collective-permute-start(bf16[128,768]{1,0:T(8,128)(2,1)} %slice_bitcast_fusion.7), channel_id=1, source_target_pairs={{0,32},{16,48},{32,64},{48,80},{64,96},{80,112},{96,0},{112,16},{1... | collective-permute-start | bytes 589832 | tf_op jit(solution)/shard_map/ppermute | solution.py:381
  225.7 7.3 %copy-start.21 = (bf16[4,128,768]{2,1,0:T(8,128)(2,1)S(1)}, bf16[4,128,768]{2,1,0:T(8,128)(2,1)}, u32[]{:S(2)}) copy-start(bf16[4,128,768]{2,1,0:T(8,128)(2,1)} %copy-done.20) | copy-start | bytes 2359300
  225.7 70.2 %all-to-all-start.2 = ((bf16[16,32,4224]{2,1,0:T(8,128)(2,1)}), bf16[16,32,4224]{2,1,0:T(8,128)(2,1)}, u32[]{:S(2)}, u32[]{:S(2)}) async-start(bf16[16,32,4224]{2,1,0:T(8,128)(2,1)} %bitcast.82), calls=%async_computation.2 | async-start | bytes 8650752 | tf_op jit(solution)/shard_map/all_to_all | solution.py:398
  233.1 11.4 %collective-permute-start.13 = (bf16[128,768]{1,0:T(8,128)(2,1)S(1)}, bf16[128,768]{1,0:T(8,128)(2,1)S(1)}, u32[]{:S(2)}, u32[]{:S(2)}) collective-permute-start(bf16[128,768]{1,0:T(8,128)(2,1)S(1)} %slice_bitcast_fusion.6), channel_id=1, source_target_pairs={{0,96},{16,112},{32,0},{48,16},{64,32},{80,48},{96,64},{112,80},{1... | collective-permute-start | bytes 589832 | tf_op jit(solution)/shard_map/ppermute | solution.py:381
  238.7 8.8 %collective-permute-start.11 = (bf16[128,768]{1,0:T(8,128)(2,1)S(1)}, bf16[128,768]{1,0:T(8,128)(2,1)S(1)}, u32[]{:S(2)}, u32[]{:S(2)}) collective-permute-start(bf16[128,768]{1,0:T(8,128)(2,1)S(1)} %fusion.11), channel_id=1, source_target_pairs={{0,32},{16,48},{32,64},{48,80},{64,96},{80,112},{96,0},{112,16},{1... | collective-permute-start | bytes 589832 | tf_op jit(solution)/shard_map/ppermute | solution.py:381
  241.1 34.4 %collective-permute-start.6 = (bf16[320,1536]{1,0:T(8,128)(2,1)S(1)}, bf16[320,1536]{1,0:T(8,128)(2,1)S(1)}, u32[]{:S(2)}, u32[]{:S(2)}) collective-permute-start(bf16[320,1536]{1,0:T(8,128)(2,1)S(1)} %get-tuple-element.62), channel_id=1, source_target_pairs={{0,32},{16,48},{32,64},{48,80},{64,96},{80,112},{96,0},{112,16},{1... | collective-permute-start | bytes 2949128 | tf_op jit(solution)/shard_map/ppermute | solution.py:381
  241.3 34.2 %collective-permute-start.9 = (bf16[320,1536]{1,0:T(8,128)(2,1)S(1)}, bf16[320,1536]{1,0:T(8,128)(2,1)S(1)}, u32[]{:S(2)}, u32[]{:S(2)}) collective-permute-start(bf16[320,1536]{1,0:T(8,128)(2,1)S(1)} %get-tuple-element.63), channel_id=1, source_target_pairs={{0,96},{16,112},{32,0},{48,16},{64,32},{80,48},{96,64},{112,80},{1... | collective-permute-start | bytes 2949128 | tf_op jit(solution)/shard_map/ppermute | solution.py:381
  244.5 23.9 %collective-permute-start.14 = (bf16[128,768]{1,0:T(8,128)(2,1)S(1)}, bf16[128,768]{1,0:T(8,128)(2,1)S(1)}, u32[]{:S(2)}, u32[]{:S(2)}) collective-permute-start(bf16[128,768]{1,0:T(8,128)(2,1)S(1)} %fusion.8), channel_id=1, source_target_pairs={{0,96},{16,112},{32,0},{48,16},{64,32},{80,48},{96,64},{112,80},{1... | collective-permute-start | bytes 589832 | tf_op jit(solution)/shard_map/ppermute | solution.py:381
  247.6 24.7 %collective-permute-start.12 = (bf16[128,768]{1,0:T(8,128)(2,1)S(1)}, bf16[128,768]{1,0:T(8,128)(2,1)S(1)}, u32[]{:S(2)}, u32[]{:S(2)}) collective-permute-start(bf16[128,768]{1,0:T(8,128)(2,1)S(1)} %fusion.10), channel_id=1, source_target_pairs={{0,32},{16,48},{32,64},{48,80},{64,96},{80,112},{96,0},{112,16},{1... | collective-permute-start | bytes 589832 | tf_op jit(solution)/shard_map/ppermute | solution.py:381
  268.5 6.9 %collective-permute-start.15 = (bf16[128,768]{1,0:T(8,128)(2,1)S(1)}, bf16[128,768]{1,0:T(8,128)(2,1)S(1)}, u32[]{:S(2)}, u32[]{:S(2)}) collective-permute-start(bf16[128,768]{1,0:T(8,128)(2,1)S(1)} %fusion.7), channel_id=1, source_target_pairs={{0,96},{16,112},{32,0},{48,16},{64,32},{80,48},{96,64},{112,80},{1... | collective-permute-start | bytes 589832 | tf_op jit(solution)/shard_map/ppermute | solution.py:381
  277.5 0.9 copy-start.28
  278.6 17.4 %copy-start.26 = (bf16[512,128]{1,0:T(8,128)(2,1)S(1)}, bf16[512,128]{1,0:T(8,128)(2,1)}, u32[]{:S(2)}) copy-start(bf16[512,128]{1,0:T(8,128)(2,1)} %get-tuple-element.30.hot_ref) | copy-start | bytes 393220
  278.6 17.4 %copy-start.27 = (s32[128,2]{0,1:T(2,128)S(1)}, s32[128,2]{0,1:T(2,128)}, u32[]{:S(2)}) copy-start(s32[128,2]{0,1:T(2,128)} %param.8) | copy-start | bytes 3076
  281.8 19.1 %copy-start.30 = (bf16[512,768]{1,0:T(8,128)(2,1)}, bf16[512,768]{1,0:T(8,128)(2,1)S(1)}, u32[]{:S(2)}) copy-start(bf16[512,768]{1,0:T(8,128)(2,1)S(1)} %slice_dynamic-update-slice_fusion) | copy-start | bytes 2359300
  (5 other events, 4.5 us)

commit v3 on v2

--- a/solution.py
+++ b/solution.py
@@ -16,6 +16,10 @@
 SLICES = 8
 CAP = 32
 LANES = 128
+PACK_STEPS = 4
+PRE_PER = 2
+INPUT_BLOCK = 512
+HIDDEN_BLOCK = 256
 
 
 def params(mib):
@@ -71,7 +75,7 @@
 
 
 def pack(ids, gates, tokens_in, out_grad, slots):
-    steps = 4
+    steps = PACK_STEPS
     tok_dev, width = tokens_in.shape
     rows = slots // steps
     wide = SLICES * GROUP + LANES
@@ -134,7 +138,7 @@
 def pre(first, w, wd):
     slots = first.shape[0]
     ff = wd.shape[3]
-    per = 2
+    per = PRE_PER
     whole = pl.BlockSpec((slots, ff), lambda q: (0, 0))
     return pl.pallas_call(
         functools.partial(pre_kernel, per=per),
@@ -147,16 +151,16 @@
         ],
         out_specs=[whole] * 5,
         out_shape=[
-            jax.ShapeDtypeStruct((slots, ff), F32),
-            jax.ShapeDtypeStruct((slots, ff), F32),
-            jax.ShapeDtypeStruct((slots, ff), F32),
-            jax.ShapeDtypeStruct((slots, ff), BF),
-            jax.ShapeDtypeStruct((slots, ff), BF),
+            pltpu.HBM((slots, ff), F32),
+            pltpu.HBM((slots, ff), F32),
+            pltpu.HBM((slots, ff), F32),
+            pltpu.HBM((slots, ff), BF),
+            pltpu.HBM((slots, ff), BF),
         ],
         scratch_shapes=[pltpu.VMEM((slots, ff), F32)] * 2,
         compiler_params=params(36),
         name="pre",
-    )(first, first, w, wd)
+    )(*map(in_hbm, (first, first, w, wd)))
 
 
 def hidden_kernel(dy_ref, wd_ref, u_ref, c1_ref, c2_ref, p_ref, h_ref, gate_ref, u_acc, gate_acc):
@@ -189,9 +193,9 @@
         gate_ref[...] = jnp.broadcast_to(total, gate_ref.shape).astype(BF)
 
 
-def hidden(second, wd, u_a, c1, c2, p):
+def hidden(second, wd, u_a, c1, c2, p, gate_at):
     slots, ff = p.shape
-    blk = 256
+    blk = HIDDEN_BLOCK
     col = pl.BlockSpec((slots, blk), lambda j: (0, j))
     depth = second.shape[1]
     return pl.pallas_call(
@@ -205,40 +209,45 @@
             col,
             col,
         ],
-        out_specs=[pl.BlockSpec((2, slots, blk), lambda j: (0, 0, j)), pl.BlockSpec((slots, LANES), lambda j: (0, 0))],
-        out_shape=[jax.ShapeDtypeStruct((2, slots, ff), BF), jax.ShapeDtypeStruct((slots, LANES), BF)],
+        out_specs=[pl.BlockSpec((2, slots, blk), lambda j: (0, 0, j)), pl.BlockSpec((slots, LANES), lambda j: (0, gate_at // LANES))],
+        out_shape=[pltpu.HBM((2, slots, ff), BF), pltpu.HBM((slots, gate_at + LANES), BF)],
         scratch_shapes=[pltpu.VMEM((slots, blk), F32), pltpu.VMEM((slots, LANES), F32)],
         compiler_params=params(24),
         name="hidden",
-    )(second, wd, u_a, c1, c2, p)
-
-
-def input_kernel(h_ref, w_ref, gate_ref, out_ref):
+    )(*map(in_hbm, (second, wd, u_a, c1, c2, p)))
+
+
+def input_kernel(h_ref, w_ref, *refs):
+    out_ref = refs[-1]
     out_ref[...] = (dot_nt(h_ref[0], w_ref[0]) + dot_nt(h_ref[1], w_ref[1])).astype(BF)
 
-    @pl.when(pl.program_id(0) == pl.num_programs(0) - 1)
-    def _():
-        out_ref[:, out_ref.shape[1] - LANES :] = gate_ref[...]
-
-
-def input_rows(h, w, gate):
+
+def input_rows(h, w, begin, cols, into=None):
     _, slots, ff = h.shape
-    wide = w.shape[1] + LANES
-    steps = 11
-    blk = wide // steps
+    blk = INPUT_BLOCK
+    first = begin // blk
+    in_specs = [
+        pl.BlockSpec((2, slots, ff), lambda j: (0, 0, 0)),
+        pl.BlockSpec((2, blk, ff), lambda j: (0, first + j, 0)),
+    ]
+    args = [in_hbm(h), in_hbm(w)]
+    shape = (slots, cols)
+    alias = {}
+    if into is not None:
+        in_specs.append(pl.BlockSpec(memory_space=pltpu.HBM))
+        args.append(in_hbm(into))
+        shape = into.shape
+        alias = {2: 0}
     return pl.pallas_call(
         input_kernel,
-        grid=(steps,),
-        in_specs=[
-            pl.BlockSpec((2, slots, ff), lambda j: (0, 0, 0)),
-            pl.BlockSpec((2, blk, ff), lambda j: (0, j, 0)),
-            pl.BlockSpec((slots, LANES), lambda j: (0, 0)),
-        ],
+        grid=(cols // blk,),
+        in_specs=in_specs,
         out_specs=pl.BlockSpec((slots, blk), lambda j: (0, j)),
-        out_shape=pltpu.HBM((slots, wide), BF),
+        out_shape=pltpu.HBM(shape, BF),
+        input_output_aliases=alias,
         compiler_params=params(24),
         name="input_rows",
-    )(h, w, gate)
+    )(*args)
 
 
 def down_kernel(me_ref, own_ref, mate_ref, gp_ref, gp_mate_ref, up_ref, dn_ref):
@@ -263,10 +272,10 @@
         grid_spec=pltpu.PrefetchScalarGridSpec(
             num_scalar_prefetch=1, grid=(4,), in_specs=[rows, rows, whole, whole], out_specs=[out, out]
         ),
-        out_shape=[jax.ShapeDtypeStruct((4, PART_A // 2, ff), BF)] * 2,
+        out_shape=[pltpu.HBM((4, PART_A // 2, ff), BF)] * 2,
         compiler_params=params(16),
         name="down_parts",
-    )(me, own, mate, gp, gp_mate)
+    )(me, *map(in_hbm, (own, mate, gp, gp_mate)))
 
 
 UNIT = SLICE // 2
@@ -319,11 +328,11 @@
     if head:
         steps = 2
         out_specs = [pl.BlockSpec(shape, lambda i, me: (0, 0))] * 2
-        out_shape = [jax.ShapeDtypeStruct(shape, BF)] * 2
+        out_shape = [pltpu.HBM(shape, BF)] * 2
     else:
         steps = 6
         out_specs = pl.BlockSpec((1,) + shape, lambda i, me: (i, 0, 0))
-        out_shape = jax.ShapeDtypeStruct((6,) + shape, BF)
+        out_shape = pltpu.HBM((6,) + shape, BF)
     return pl.pallas_call(
         head_kernel if head else rest_kernel,
         grid_spec=pltpu.PrefetchScalarGridSpec(
@@ -335,11 +344,15 @@
         out_shape=out_shape,
         compiler_params=params(24),
         name="units_head" if head else "units_rest",
-    )(me, first, mate_first, second, mate_second, h, h_mate, gp, gp_mate)
-
-
-def unpack_kernel(hot_ref, ids_ref, rows_ref, gates_ref, out_ref, gate_ref):
+    )(me, *map(in_hbm, (first, mate_first, second, mate_second, h, h_mate, gp, gp_mate)))
+
+
+def unpack_kernel(hot_ref, rows_ref, out_ref):
     out_ref[...] = dot_tn(hot_ref[...], rows_ref[...]).astype(BF)
+
+
+def unpack_gate_kernel(hot_ref, rows_ref, ids_ref, gates_ref, out_ref, gate_ref):
+    unpack_kernel(hot_ref, rows_ref, out_ref)
 
     @pl.when(pl.program_id(0) == 0)
     def _():
@@ -352,22 +365,48 @@
 
 def unpack(hot, ids, back, width):
     slots, tok_dev = hot.shape
-    steps = 4
+    blk = 512
+    half = width // 2
     whole = lambda shape: pl.BlockSpec(shape, lambda i: (0, 0))
     return pl.pallas_call(
-        unpack_kernel,
+        unpack_gate_kernel,
+        grid=(half // blk,),
+        in_specs=[
+            whole((slots, tok_dev)),
+            pl.BlockSpec((slots, blk), lambda i: (0, i)),
+            whole((2, tok_dev)),
+            pl.BlockSpec((slots, LANES), lambda i: (0, half // LANES)),
+        ],
+        out_specs=[pl.BlockSpec((tok_dev, blk), lambda i: (0, i)), whole((2, tok_dev))],
+        out_shape=[pltpu.HBM((tok_dev, width), BF), pltpu.HBM((2, tok_dev), BF)],
+        compiler_params=params(16),
+        name="unpack",
+    )(*map(in_hbm, (hot, back, ids, back)))
+
+
+def unpack_tail_kernel(hot_ref, rows_ref, whole_ref, out_ref):
+    del whole_ref
+    unpack_kernel(hot_ref, rows_ref, out_ref)
+
+
+def unpack_tail(hot, back, into):
+    slots, tok_dev = hot.shape
+    blk = 512
+    steps = back.shape[1] // blk
+    return pl.pallas_call(
+        unpack_tail_kernel,
         grid=(steps,),
         in_specs=[
-            whole((slots, tok_dev)),
-            whole((2, tok_dev)),
-            pl.BlockSpec((slots, width // steps), lambda i: (0, i)),
-            pl.BlockSpec((slots, LANES), lambda i: (0, width // LANES)),
-        ],
-        out_specs=[pl.BlockSpec((tok_dev, width // steps), lambda i: (0, i)), whole((2, tok_dev))],
-        out_shape=[jax.ShapeDtypeStruct((tok_dev, width), BF), jax.ShapeDtypeStruct((2, tok_dev), BF)],
+            pl.BlockSpec((slots, tok_dev), lambda i: (0, 0)),
+            pl.BlockSpec((slots, blk), lambda i: (0, i)),
+            pl.BlockSpec(memory_space=pltpu.HBM),
+        ],
+        out_specs=pl.BlockSpec((tok_dev, blk), lambda i: (0, steps + i)),
+        out_shape=pltpu.HBM(into.shape, BF),
+        input_output_aliases={2: 0},
         compiler_params=params(16),
-        name="unpack",
-    )(hot, ids, in_hbm(back), in_hbm(back))
+        name="unpack_tail",
+    )(*map(in_hbm, (hot, back, into)))
 
 
 UP = [(i, (i + 2) % 8) for i in range(8)]
@@ -401,27 +440,41 @@
     def swap(x):
         return lax.ppermute(x, "dp", SWAP)
 
-    first, gate_up, down_proj, me = lax.optimization_barrier((exchange(first), gate_up, down_proj, me))
+    me = me.reshape(1).astype(jnp.int32)
+    first, me = lax.optimization_barrier((first, me))
+    first, gate_up, down_proj = lax.optimization_barrier((exchange(first), gate_up, down_proj))
     second = exchange(second)
-    me = me.reshape(1).astype(jnp.int32)
     mate_first = swap(first)
     w = jnp.transpose(gate_up[:, :, 0], (1, 0, 2))
     wd = down_proj.reshape(SLICES, 2, PART_A, ff)
     u_a, c1, c2, p, gp = pre(first, w, wd)
     gp_mate = swap(gp)
     down_up, down_dn = down_parts(me, first, mate_first, gp, gp_mate)
-    second, down_up, down_dn = lax.optimization_barrier((second, down_up, down_dn))
+    arrived_up = lax.ppermute(down_up[0], "dp", UP)
+    arrived_dn = lax.ppermute(down_dn[2], "dp", DOWN)
+    second, _, _ = lax.optimization_barrier((second, down_up, down_dn))
+
+    half = width // 2
+    mate_second = swap(second)
+    h, rows_1 = hidden(second, wd, u_a, c1, c2, p, half)
+    h_mate = swap(h)
+    rows_1 = input_rows(h, w, 0, half, rows_1)
+    h_mate, rows_1 = lax.optimization_barrier((h_mate, rows_1))
+    back_1 = exchange(rows_1)
+    head_up, head_dn = units(me, first, mate_first, second, mate_second, h, h_mate, gp, gp_mate, True)
+    h, head_up, head_dn, arrived_up, arrived_dn = lax.optimization_barrier((h, head_up, head_dn, arrived_up, arrived_dn))
+    rows_2 = input_rows(h, w, half, half)
+    h, rows_2 = lax.optimization_barrier((h, rows_2))
+    rest = units(me, first, mate_first, second, mate_second, h, h_mate, gp, gp_mate, False)
+    back_2 = exchange(rows_2)
+    total = lambda a, b: (a.astype(F32) + b.astype(F32)).astype(BF)
     grad_a = jnp.concatenate(
-        [ring([down_up[j] for j in (0, 1, 2, 3)], UP), ring([down_dn[j] for j in (2, 1, 0, 3)], DOWN)], axis=0
+        [
+            ring([total(arrived_up, down_up[1]), down_up[2], down_up[3]], UP),
+            ring([total(arrived_dn, down_dn[1]), down_dn[0], down_dn[3]], DOWN),
+        ],
+        axis=0,
     )
-
-    mate_second = swap(second)
-    h, gate_rows = hidden(second, wd, u_a, c1, c2, p)
-    h_mate = swap(h)
-    head_up, head_dn = units(me, first, mate_first, second, mate_second, h, h_mate, gp, gp_mate, True)
-    h, head_up, head_dn = lax.optimization_barrier((h, head_up, head_dn))
-    back = exchange(input_rows(h, w, gate_rows))
-    rest = units(me, first, mate_first, second, mate_second, h, h_mate, gp, gp_mate, False)
     sum_up = ring([head_up, rest[0], rest[2], rest[4]], UP)
     sum_dn = ring([head_dn, rest[1], rest[3], rest[5]], DOWN)
 
@@ -430,7 +483,8 @@
     down_b = [t[UNIT:, k * ff : (k + 1) * ff] for t in (sum_up, sum_dn) for k in range(2)]
     down_grad = jnp.concatenate([grad_a] + down_b, axis=0)[:, None, :]
 
-    input_grad, gate_grad = unpack(hot, ids, back, width)
+    input_grad, gate_grad = unpack(hot, ids, back_1, width)
+    input_grad = unpack_tail(hot, back_2, input_grad)
     return (input_grad, gate_grad.T, gate_up_grad, down_grad)
 
 

time: 302 us -> 273 us (0.904)
  waiting for transfers between devices: 146 us -> 46.3 us
  blocking collectives: 0 us -> 82 us
  local copies, waits for them, and re-layouts: 43.3 us -> 24.9 us
  Pallas kernels: 60.5 us -> 77.6 us
  starting transfers between devices: 41 us -> 30.6 us
    all_to_all x3, waiting for transfers between devices: 109 us -> 7.56 us  [exchange(): lax.all_to_all(rows.reshape(owners, CAP, wide), 'expert', split_axis=0, c...]
    all_to_all x0 -> x1, blocking collectives: none -> 82 us  [exchange(): lax.all_to_all(rows.reshape(owners, CAP, wide), 'expert', split_axis=0, c...]
    unnamed x71 -> x21, local copies, waits for them, and re-layouts: 29.3 us -> 9.06 us
    ppermute x12 -> x10, starting transfers between devices: 20.1 us -> 10.1 us  [ring(): arrived = lax.ppermute(total, 'dp', perm)]
    pallas_call x2 -> x4, Pallas kernels: 18 us -> 23.3 us  [the longest x2 15.1 us: input_rows(): pl.pallas_call(input_kernel, grid=(cols // blk,), in_specs=in_specs, out_...]
    all_to_all x3, starting transfers between devices: 20.1 us -> 15 us  [exchange(): lax.all_to_all(rows.reshape(owners, CAP, wide), 'expert', split_axis=0, c...]
    ppermute x12 -> x10, waiting for transfers between devices: 31.8 us -> 36.6 us  [ring(): arrived = lax.ppermute(total, 'dp', perm)]
    ppermute x0 -> x2, starting transfers between devices: none -> 4.17 us  [the longest x1 2.18 us: body(): arrived_dn = lax.ppermute(down_dn[2], 'dp', DOWN)]
  transfers between devices with their start and end apart: 19 -> 19, of which waited for: 9 -> 6; matrix products, arithmetic and copies ran while one was open for 7% -> 8% of each run, Pallas kernels for 14% -> 26%
where the time goes in v3:
time: 273 us; the launch traced here: 272 us
  blocking collectives  82 us (30%)
  Pallas kernels  77.6 us (28%)
  waiting for transfers between devices  46.3 us (17%)
  starting transfers between devices  30.6 us (11%)
  local copies, waits for them, and re-layouts  24.9 us (9%)
  other arithmetic  10.2 us (4%)
    all_to_all x1, blocking collectives, exchange(): lax.all_to_all(rows.reshape(owners, CAP, wide), 'expert', split_axis=0, c...  82 us
    ppermute x10, waiting for transfers between devices, ring(): arrived = lax.ppermute(total, 'dp', perm)  36.6 us
    pallas_call x2, Pallas kernels, units(): pl.pallas_call(head_kernel if head else rest_kernel, grid_spec=pltpu.Pref...  18.2 us
    pallas_call x1, Pallas kernels, pre(): pl.pallas_call(functools.partial(pre_kernel, per=per), grid=(SLICES // pe...  16.4 us
    pallas_call x2, Pallas kernels, input_rows(): pl.pallas_call(input_kernel, grid=(cols // blk,), in_specs=in_specs, out_...  15.1 us
    all_to_all x3, starting transfers between devices, exchange(): lax.all_to_all(rows.reshape(owners, CAP, wide), 'expert', split_axis=0, c...  15 us
    optimization_barrier x1, local copies, waits for them, and re-layouts, body(): lax.optimization_barrier((exchange(first), gate_up, down_proj))  11.9 us
    ppermute x10, starting transfers between devices, ring(): arrived = lax.ppermute(total, 'dp', perm)  10.1 us
  transfers between devices with their start and end apart: 19, of which 6 were waited for; matrix products, arithmetic and copies ran while one was open for 8% of the time, Pallas kernels for 26%

profile of v3, /device:TPU:0, one launch (start us, length us, event | category | flops | bytes accessed | tf_op | source)
XLA Modules:
  0.0 272.4 jit_solution(5876555937822547226)
XLA Ops:
  0.6 6.8 %pack.1 = (bf16[512,6272]{1,0:T(8,128)(2,1)}, bf16[512,2048]{1,0:T(8,128)(2,1)}, bf16[512,128]{1,0:T(8,128)(2,1)}) custom-call(s32[2,128]{1,0:T(2,128)} %bitcast.89, bf16[2,128]{1,0:T(2,128)(2,1)} %bitcast.91, bf16[128,4096]{1,0:T(8,128)(2,1)} %tok_ref.1, bf16[128,4096]{1,0:T(8,128)(2,1)} %dy_ref.1), custom_call_target="tpu_custom_call" | custom-call | tf_op jit(solution)/shard_map/pack/pallas_call | solution.py:83
  7.5 82.0 %all_to_all.20 = bf16[16,32,6272]{2,1,0:T(8,128)(2,1)} all-to-all(bf16[16,32,6272]{2,1,0:T(8,128)(2,1)} %bitcast.85), channel_id=1, replica_groups=mesh['dp'=8,'expert'=16] {'expert'}, dimensions={0} | all-to-all | bytes 12845056 | tf_op jit(solution)/shard_map/all_to_all | solution.py:437
  89.5 3.7 %all-to-all-start = ((bf16[16,32,2048]{2,1,0:T(8,128)(2,1)}), bf16[16,32,2048]{2,1,0:T(8,128)(2,1)S(1)}, u32[]{:S(2)}, u32[]{:S(2)}) async-start(bf16[16,32,2048]{2,1,0:T(8,128)(2,1)} %bitcast.86), calls=%async_computation | async-start | bytes 4194304 | tf_op jit(solution)/shard_map/all_to_all | solution.py:437
  93.2 11.9 %copy.15 = bf16[4096,2,1,768]{3,0,1,2:T(8,128)(2,1)} copy(bf16[4096,2,1,768]{3,1,2,0:T(2,128)(2,1)} %param.10) | data formatting | bytes 25165824 | tf_op jit(solution)/shard_map/optimization_barrier | solution.py:445
  105.1 16.4 %pre.1 = (f32[512,768]{1,0:T(8,128)}, f32[512,768]{1,0:T(8,128)}, f32[512,768]{1,0:T(8,128)}, bf16[512,768]{1,0:T(8,128)(2,1)}, bf16[512,768]{1,0:T(8,128)(2,1)}) custom-call(bf16[512,6272]{1,0:T(8,128)(2,1)} %bitcast.6.rows_ref.gate_ref.own_ref.refs_0_, bf16[512,6272]{1,0:T(8,128)(2,1)} %bitcast.6.rows_ref.gate_ref.own_ref.refs_0_, ...), custom_call_target="tpu_custom_call" | custom-call | tf_op jit(solution)/shard_map/pre/pallas_call | solution.py:143
  121.9 2.1 collective-permute-done.1.gp_mate_ref.refs_7_
  124.1 0.9 copy-done.3
  124.9 5.4 %down_parts.1 = (bf16[4,128,768]{2,1,0:T(8,128)(2,1)}, bf16[4,128,768]{2,1,0:T(8,128)(2,1)}) custom-call(s32[1]{0:T(128)} %bitcast.4.me_ref, bf16[512,6272]{1,0:T(8,128)(2,1)} %bitcast.6.rows_ref.gate_ref.own_ref.refs_0_, bf16[512,6272]{1,0:T(8,128)(2,1)} %collective-permute-done.mate_ref.refs_1_, bf16[512,768]{1,0:T(8,128)(2,1)} %get-tuple-element.43.gp_ref.refs_6_, ...), custom_call_target="tpu_custom_call" | custom-call | tf_op jit(solution)/shard_map/down_parts/pallas_call | solution.py:270
  130.7 0.8 copy-done
  131.6 7.5 %hidden.1 = (bf16[2,512,768]{2,1,0:T(8,128)(2,1)}, bf16[512,2176]{1,0:T(8,128)(2,1)}) custom-call(bf16[512,2048]{1,0:T(8,128)(2,1)} %bitcast.76, bf16[8,2,256,768]{3,2,1,0:T(8,128)(2,1)} %bitcast.80, f32[512,768]{1,0:T(8,128)} %get-tuple-element.47.u_ref, f32[512,768]{1,0:T(8,128)} %get-tuple-element.48.c1_ref, f32[512,768]{1,0:T(8,128)} %get-tuple-element.49.c2_ref, ...), custom_call_target="tpu_custom_call" | custom-call | tf_op jit(solution)/shard_map/hidden/pallas_call | solution.py:201
  139.4 0.9 slice_bitcast_fusion.7
  140.4 0.9 slice_bitcast_fusion.6
  141.3 2.0 collective-permute-start.4
  143.3 2.2 collective-permute-start.5
  145.5 7.5 %input_rows.2 = bf16[512,2176]{1,0:T(8,128)(2,1)} custom-call(bf16[2,512,768]{2,1,0:T(8,128)(2,1)} %get-tuple-element.62.h_ref.refs_4_, bf16[2,4096,768]{2,1,0:T(8,128)(2,1)} %bitcast.73, bf16[512,2176]{1,0:T(8,128)(2,1)} %get-tuple-element.52.refs_0_), custom_call_target="tpu_custom_call", output_to_operand_aliasing={{}: (2, {})} | custom-call | tf_op jit(solution)/shard_map/input_rows/pallas_call | solution.py:241
  153.0 1.1 copy-done.4
  154.2 1.3 copy-done.2
  155.5 6.4 %units_head.1 = (bf16[320,1536]{1,0:T(8,128)(2,1)}, bf16[320,1536]{1,0:T(8,128)(2,1)}) custom-call(s32[1]{0:T(128)} %bitcast.4.me_ref, bf16[512,6272]{1,0:T(8,128)(2,1)} %bitcast.6.rows_ref.gate_ref.own_ref.refs_0_, bf16[512,6272]{1,0:T(8,128)(2,1)} %collective-permute-done.mate_ref.refs_1_, bf16[512,2048]{1,0:T(8,128)(2,1)} %bitcast.77, ...), custom_call_target="tpu_custom_call" | custom-call | tf_op jit(solution)/shard_map/units_head/pallas_call | solution.py:336
  162.0 0.7 copy-done.7
  162.6 3.2 %collective-permute-start.9 = (bf16[320,1536]{1,0:T(8,128)(2,1)}, bf16[320,1536]{1,0:T(8,128)(2,1)}, u32[]{:S(2)}, u32[]{:S(2)}) collective-permute-start(bf16[320,1536]{1,0:T(8,128)(2,1)} %get-tuple-element.63), channel_id=1, source_target_pairs={{0,96},{16,112},{32,0},{48,16},{64,32},{80,48},{96,64},{112,80},{1... | collective-permute-start | bytes 2949128 | tf_op jit(solution)/shard_map/ppermute | solution.py:420
  165.8 6.9 %all-to-all-start.3 = ((bf16[16,32,2176]{2,1,0:T(8,128)(2,1)}), bf16[16,32,2176]{2,1,0:T(8,128)(2,1)S(1)}, u32[]{:S(2)}, u32[]{:S(2)}) async-start(bf16[16,32,2176]{2,1,0:T(8,128)(2,1)} %bitcast.83), calls=%async_computation.3 | async-start | bytes 4456448 | tf_op jit(solution)/shard_map/all_to_all | solution.py:437
  172.7 7.5 %input_rows.3 = bf16[512,2048]{1,0:T(8,128)(2,1)} custom-call(bf16[2,512,768]{2,1,0:T(8,128)(2,1)} %get-tuple-element.62.h_ref.refs_4_, bf16[2,4096,768]{2,1,0:T(8,128)(2,1)} %bitcast.74), custom_call_target="tpu_custom_call" | custom-call | tf_op jit(solution)/shard_map/input_rows/pallas_call | solution.py:241
  180.2 11.8 %units_rest.1 = bf16[6,320,1536]{2,1,0:T(8,128)(2,1)} custom-call(s32[1]{0:T(128)} %bitcast.4.me_ref, bf16[512,6272]{1,0:T(8,128)(2,1)} %bitcast.6.rows_ref.gate_ref.own_ref.refs_0_, bf16[512,6272]{1,0:T(8,128)(2,1)} %collective-permute-done.mate_ref.refs_1_, bf16[512,2048]{1,0:T(8,128)(2,1)} %bitcast.78, bf16[512,2048]{1,0:T(8,128)(2,1)} %copy-done.2, ...), custom_call_target="tpu_custom_call" | custom-call | tf_op jit(solution)/shard_map/units_rest/pallas_call | solution.py:336
  192.1 3.6 %fusion.5 = (bf16[320,1536]{1,0:T(8,128)(2,1)}, bf16[320,1536]{1,0:T(8,128)(2,1)}) fusion(bf16[320,1536]{1,0:T(8,128)(2,1)S(1)} %collective-permute-done.6, bf16[6,320,1536]{2,1,0:T(8,128)(2,1)} %units_rest.1, bf16[320,1536]{1,0:T(8,128)(2,1)} %collective-permute-done.9), kind=kLoop, calls=%fused_computation.12 | loop fusion | flops 3932160 | bytes 5898240 | tf_op jit(solution)/shard_map/convert_element_type | solution.py:421
  195.6 0.7 collective-permute-start.10
  196.3 1.3 collective-permute-start.7
  197.6 7.6 %all-to-all-done.3 = bf16[16,32,2176]{2,1,0:T(8,128)(2,1)S(1)} async-done(((bf16[16,32,2176]{2,1,0:T(8,128)(2,1)}), bf16[16,32,2176]{2,1,0:T(8,128)(2,1)S(1)}, u32[]{:S(2)}, u32[]{:S(2)}) %all-to-all-start.3) | async-done | bytes 2228256 | tf_op jit(solution)/shard_map/all_to_all | solution.py:437
  205.2 1.4 copy-done.1
  206.6 4.4 %all-to-all-start.2 = ((bf16[16,32,2048]{2,1,0:T(8,128)(2,1)}), bf16[16,32,2048]{2,1,0:T(8,128)(2,1)}, u32[]{:S(2)}, u32[]{:S(2)}) async-start(bf16[16,32,2048]{2,1,0:T(8,128)(2,1)} %bitcast.84), calls=%async_computation.2 | async-start | bytes 4194304 | tf_op jit(solution)/shard_map/all_to_all | solution.py:437
  211.0 1.1 fusion.11
  212.2 6.4 %collective-permute-done.10 = bf16[320,1536]{1,0:T(8,128)(2,1)S(1)} collective-permute-done((bf16[320,1536]{1,0:T(8,128)(2,1)}, bf16[320,1536]{1,0:T(8,128)(2,1)S(1)}, u32[]{:S(2)}, u32[]{:S(2)}) %collective-permute-start.10) | collective-permute-done | bytes 983072 | tf_op jit(solution)/shard_map/ppermute | solution.py:420
  218.6 3.6 %collective-permute-done.7 = bf16[320,1536]{1,0:T(8,128)(2,1)} collective-permute-done((bf16[320,1536]{1,0:T(8,128)(2,1)}, bf16[320,1536]{1,0:T(8,128)(2,1)}, u32[]{:S(2)}, u32[]{:S(2)}) %collective-permute-start.7) | collective-permute-done | bytes 983072 | tf_op jit(solution)/shard_map/ppermute | solution.py:420
  222.2 3.2 %fusion.4 = (bf16[320,1536]{1,0:T(8,128)(2,1)S(1)}, bf16[320,1536]{1,0:T(8,128)(2,1)}) fusion(bf16[320,1536]{1,0:T(8,128)(2,1)} %collective-permute-done.7, bf16[6,320,1536]{2,1,0:T(8,128)(2,1)} %units_rest.1, bf16[320,1536]{1,0:T(8,128)(2,1)S(1)} %collective-permute-done.10), kind=kLoop, calls=%fused_computation.10 | loop fusion | flops 3932160 | bytes 5898240 | tf_op jit(solution)/shard_map/convert_element_type | solution.py:421
  225.5 2.0 collective-permute-start.8
  227.6 1.3 collective-permute-start.14
  228.9 0.9 collective-permute-start.13
  229.8 21.5 %collective-permute-done.14 = bf16[128,768]{1,0:T(8,128)(2,1)S(1)} collective-permute-done((bf16[128,768]{1,0:T(8,128)(2,1)S(1)}, bf16[128,768]{1,0:T(8,128)(2,1)S(1)}, u32[]{:S(2)}, u32[]{:S(2)}) %collective-permute-start.14) | collective-permute-done | bytes 196640 | tf_op jit(solution)/shard_map/ppermute | solution.py:420
  251.3 0.5 collective-permute-start.15
  251.9 5.1 %collective-permute-done.15 = bf16[128,768]{1,0:T(8,128)(2,1)S(1)} collective-permute-done((bf16[128,768]{1,0:T(8,128)(2,1)S(1)}, bf16[128,768]{1,0:T(8,128)(2,1)S(1)}, u32[]{:S(2)}, u32[]{:S(2)}) %collective-permute-start.15) | collective-permute-done | bytes 196640 | tf_op jit(solution)/shard_map/ppermute | solution.py:420
  257.1 0.9 copy-done.8
  258.0 4.3 %unpack.1 = (bf16[128,4096]{1,0:T(8,128)(2,1)}, bf16[2,128]{1,0:T(2,128)(2,1)}) custom-call(bf16[512,128]{1,0:T(8,128)(2,1)} %get-tuple-element.35.hot_ref, bf16[512,2176]{1,0:T(8,128)(2,1)} %bitcast.81, s32[2,128]{1,0:T(2,128)} %bitcast.90, bf16[512,2176]{1,0:T(8,128)(2,1)} %bitcast.82), custom_call_target="tpu_custom_call" | custom-call | tf_op jit(solution)/shard_map/unpack/pallas_call | solution.py:371
  262.3 4.0 %unpack_tail.1 = bf16[128,4096]{1,0:T(8,128)(2,1)} custom-call(bf16[512,128]{1,0:T(8,128)(2,1)} %get-tuple-element.35.hot_ref, bf16[512,2048]{1,0:T(8,128)(2,1)} %bitcast.14.rows_ref, bf16[128,4096]{1,0:T(8,128)(2,1)} %get-tuple-element.59.whole_ref), custom_call_target="tpu_custom_call", output_to_operand_aliasing={{}: (2, {})} | custom-call | tf_op jit(solution)/shard_map/unpack_tail/pallas_call | solution.py:396
  266.3 2.0 fusion.3
  268.3 0.7 slice_dynamic-update-slice_fusion.3
  269.0 0.6 slice_dynamic-update-slice_fusion.2
  269.7 0.7 slice_dynamic-update-slice_fusion.1
  270.3 0.6 slice_dynamic-update-slice_fusion
  271.1 1.3 reshape.75
  (39 shorter events, 1.9 us)
Async XLA Ops:
  89.5 34.6 %collective-permute-start = (bf16[512,6272]{1,0:T(8,128)(2,1)}, bf16[512,6272]{1,0:T(8,128)(2,1)}, u32[]{:S(2)}, u32[]{:S(2)}) collective-permute-start(bf16[512,6272]{1,0:T(8,128)(2,1)} %bitcast.6.rows_ref.gate_ref.own_ref.refs_0_), channel_id=1, source_target_pairs={{0,16},{16,0},{32,48},{48,32},{64,80},{80,64},{96,112},{112,96},{1... | collective-permute-start | bytes 19267592 | tf_op jit(solution)/shard_map/ppermute | solution.py:441
  89.5 40.8 %all-to-all-start = ((bf16[16,32,2048]{2,1,0:T(8,128)(2,1)}), bf16[16,32,2048]{2,1,0:T(8,128)(2,1)S(1)}, u32[]{:S(2)}, u32[]{:S(2)}) async-start(bf16[16,32,2048]{2,1,0:T(8,128)(2,1)} %bitcast.86), calls=%async_computation | async-start | bytes 4194304 | tf_op jit(solution)/shard_map/all_to_all | solution.py:437
  121.4 2.6 collective-permute-start.1
  124.1 0.9 copy-start.3
  130.3 1.3 copy-start
  130.3 22.7 %collective-permute-start.2 = (bf16[512,2048]{1,0:T(8,128)(2,1)S(1)}, bf16[512,2048]{1,0:T(8,128)(2,1)S(1)}, u32[]{:S(2)}, u32[]{:S(2)}) collective-permute-start(bf16[512,2048]{1,0:T(8,128)(2,1)S(1)} %bitcast.75), channel_id=1, source_target_pairs={{0,16},{16,0},{32,48},{48,32},{64,80},{80,64},{96,112},{112,96},{1... | collective-permute-start | bytes 6291464 | tf_op jit(solution)/shard_map/ppermute | solution.py:441
  139.1 14.0 %collective-permute-start.3 = (bf16[2,512,768]{2,1,0:T(8,128)(2,1)}, bf16[2,512,768]{2,1,0:T(8,128)(2,1)S(1)}, u32[]{:S(2)}, u32[]{:S(2)}) collective-permute-start(bf16[2,512,768]{2,1,0:T(8,128)(2,1)} %get-tuple-element.62.h_ref.refs_4_), channel_id=1, source_target_pairs={{0,16},{16,0},{32,48},{48,32},{64,80},{80,64},{96,112},{112,96},{1... | collective-permute-start | bytes 4718600 | tf_op jit(solution)/shard_map/ppermute | solution.py:441
  141.3 20.6 %collective-permute-start.4 = (bf16[128,768]{1,0:T(8,128)(2,1)S(1)}, bf16[128,768]{1,0:T(8,128)(2,1)S(1)}, u32[]{:S(2)}, u32[]{:S(2)}) collective-permute-start(bf16[128,768]{1,0:T(8,128)(2,1)S(1)} %slice_bitcast_fusion.7), channel_id=1, source_target_pairs={{0,32},{16,48},{32,64},{48,80},{64,96},{80,112},{96,0},{112,16},{1... | collective-permute-start | bytes 589832 | tf_op jit(solution)/shard_map/ppermute | solution.py:453
  143.3 18.6 %collective-permute-start.5 = (bf16[128,768]{1,0:T(8,128)(2,1)S(1)}, bf16[128,768]{1,0:T(8,128)(2,1)S(1)}, u32[]{:S(2)}, u32[]{:S(2)}) collective-permute-start(bf16[128,768]{1,0:T(8,128)(2,1)S(1)} %slice_bitcast_fusion.6), channel_id=1, source_target_pairs={{0,96},{16,112},{32,0},{48,16},{64,32},{80,48},{96,64},{112,80},{1... | collective-permute-start | bytes 589832 | tf_op jit(solution)/shard_map/ppermute | solution.py:454
  153.0 1.1 copy-start.4
  154.2 1.3 copy-start.2
  161.9 0.7 copy-start.7
  162.6 29.4 %collective-permute-start.6 = (bf16[320,1536]{1,0:T(8,128)(2,1)}, bf16[320,1536]{1,0:T(8,128)(2,1)S(1)}, u32[]{:S(2)}, u32[]{:S(2)}) collective-permute-start(bf16[320,1536]{1,0:T(8,128)(2,1)} %get-tuple-element.61), channel_id=1, source_target_pairs={{0,32},{16,48},{32,64},{48,80},{64,96},{80,112},{96,0},{112,16},{1... | collective-permute-start | bytes 2949128 | tf_op jit(solution)/shard_map/ppermute | solution.py:420
  162.6 29.4 %collective-permute-start.9 = (bf16[320,1536]{1,0:T(8,128)(2,1)}, bf16[320,1536]{1,0:T(8,128)(2,1)}, u32[]{:S(2)}, u32[]{:S(2)}) collective-permute-start(bf16[320,1536]{1,0:T(8,128)(2,1)} %get-tuple-element.63), channel_id=1, source_target_pairs={{0,96},{16,112},{32,0},{48,16},{64,32},{80,48},{96,64},{112,80},{1... | collective-permute-start | bytes 2949128 | tf_op jit(solution)/shard_map/ppermute | solution.py:420
  165.8 39.4 %all-to-all-start.3 = ((bf16[16,32,2176]{2,1,0:T(8,128)(2,1)}), bf16[16,32,2176]{2,1,0:T(8,128)(2,1)S(1)}, u32[]{:S(2)}, u32[]{:S(2)}) async-start(bf16[16,32,2176]{2,1,0:T(8,128)(2,1)} %bitcast.83), calls=%async_computation.3 | async-start | bytes 4456448 | tf_op jit(solution)/shard_map/all_to_all | solution.py:437
  195.6 23.0 %collective-permute-start.10 = (bf16[320,1536]{1,0:T(8,128)(2,1)}, bf16[320,1536]{1,0:T(8,128)(2,1)S(1)}, u32[]{:S(2)}, u32[]{:S(2)}) collective-permute-start(bf16[320,1536]{1,0:T(8,128)(2,1)} %get-tuple-element.75), channel_id=1, source_target_pairs={{0,96},{16,112},{32,0},{48,16},{64,32},{80,48},{96,64},{112,80},{1... | collective-permute-start | bytes 2949128 | tf_op jit(solution)/shard_map/ppermute | solution.py:420
  196.3 25.9 %collective-permute-start.7 = (bf16[320,1536]{1,0:T(8,128)(2,1)}, bf16[320,1536]{1,0:T(8,128)(2,1)}, u32[]{:S(2)}, u32[]{:S(2)}) collective-permute-start(bf16[320,1536]{1,0:T(8,128)(2,1)} %get-tuple-element.74), channel_id=1, source_target_pairs={{0,32},{16,48},{32,64},{48,80},{64,96},{80,112},{96,0},{112,16},{1... | collective-permute-start | bytes 2949128 | tf_op jit(solution)/shard_map/ppermute | solution.py:420
  205.2 1.4 copy-start.1
  206.6 55.7 %all-to-all-start.2 = ((bf16[16,32,2048]{2,1,0:T(8,128)(2,1)}), bf16[16,32,2048]{2,1,0:T(8,128)(2,1)}, u32[]{:S(2)}, u32[]{:S(2)}) async-start(bf16[16,32,2048]{2,1,0:T(8,128)(2,1)} %bitcast.84), calls=%async_computation.2 | async-start | bytes 4194304 | tf_op jit(solution)/shard_map/all_to_all | solution.py:437
  212.1 15.4 %copy-start.5 = (bf16[4,128,768]{2,1,0:T(8,128)(2,1)S(1)}, bf16[4,128,768]{2,1,0:T(8,128)(2,1)}, u32[]{:S(2)}) copy-start(bf16[4,128,768]{2,1,0:T(8,128)(2,1)} %get-tuple-element.45) | copy-start | bytes 2359300
  212.1 16.7 %copy-start.6 = (bf16[4,128,768]{2,1,0:T(8,128)(2,1)S(1)}, bf16[4,128,768]{2,1,0:T(8,128)(2,1)}, u32[]{:S(2)}) copy-start(bf16[4,128,768]{2,1,0:T(8,128)(2,1)} %get-tuple-element.44) | copy-start | bytes 2359300
  212.1 16.7 %collective-permute-start.12 = (bf16[128,768]{1,0:T(8,128)(2,1)S(1)}, bf16[128,768]{1,0:T(8,128)(2,1)S(1)}, u32[]{:S(2)}, u32[]{:S(2)}) collective-permute-start(bf16[128,768]{1,0:T(8,128)(2,1)S(1)} %fusion.11), channel_id=1, source_target_pairs={{0,32},{16,48},{32,64},{48,80},{64,96},{80,112},{96,0},{112,16},{1... | collective-permute-start | bytes 589832 | tf_op jit(solution)/shard_map/ppermute | solution.py:420
  225.5 40.8 %collective-permute-start.11 = (bf16[320,1536]{1,0:T(8,128)(2,1)}, bf16[320,1536]{1,0:T(8,128)(2,1)S(1)}, u32[]{:S(2)}, u32[]{:S(2)}) collective-permute-start(bf16[320,1536]{1,0:T(8,128)(2,1)} %get-tuple-element.73), channel_id=1, source_target_pairs={{0,96},{16,112},{32,0},{48,16},{64,32},{80,48},{96,64},{112,80},{1... | collective-permute-start | bytes 2949128 | tf_op jit(solution)/shard_map/ppermute | solution.py:420
  225.5 40.8 %collective-permute-start.8 = (bf16[320,1536]{1,0:T(8,128)(2,1)S(1)}, bf16[320,1536]{1,0:T(8,128)(2,1)S(1)}, u32[]{:S(2)}, u32[]{:S(2)}) collective-permute-start(bf16[320,1536]{1,0:T(8,128)(2,1)S(1)} %get-tuple-element.72), channel_id=1, source_target_pairs={{0,32},{16,48},{32,64},{48,80},{64,96},{80,112},{96,0},{112,16},{1... | collective-permute-start | bytes 2949128 | tf_op jit(solution)/shard_map/ppermute | solution.py:420
  227.6 23.7 %collective-permute-start.14 = (bf16[128,768]{1,0:T(8,128)(2,1)S(1)}, bf16[128,768]{1,0:T(8,128)(2,1)S(1)}, u32[]{:S(2)}, u32[]{:S(2)}) collective-permute-start(bf16[128,768]{1,0:T(8,128)(2,1)S(1)} %fusion.8), channel_id=1, source_target_pairs={{0,96},{16,112},{32,0},{48,16},{64,32},{80,48},{96,64},{112,80},{1... | collective-permute-start | bytes 589832 | tf_op jit(solution)/shard_map/ppermute | solution.py:420
  228.9 22.9 %collective-permute-start.13 = (bf16[128,768]{1,0:T(8,128)(2,1)S(1)}, bf16[128,768]{1,0:T(8,128)(2,1)S(1)}, u32[]{:S(2)}, u32[]{:S(2)}) collective-permute-start(bf16[128,768]{1,0:T(8,128)(2,1)S(1)} %fusion.10), channel_id=1, source_target_pairs={{0,32},{16,48},{32,64},{48,80},{64,96},{80,112},{96,0},{112,16},{1... | collective-permute-start | bytes 589832 | tf_op jit(solution)/shard_map/ppermute | solution.py:420
  251.3 5.7 %collective-permute-start.15 = (bf16[128,768]{1,0:T(8,128)(2,1)S(1)}, bf16[128,768]{1,0:T(8,128)(2,1)S(1)}, u32[]{:S(2)}, u32[]{:S(2)}) collective-permute-start(bf16[128,768]{1,0:T(8,128)(2,1)S(1)} %fusion.7), channel_id=1, source_target_pairs={{0,96},{16,112},{32,0},{48,16},{64,32},{80,48},{96,64},{112,80},{1... | collective-permute-start | bytes 589832 | tf_op jit(solution)/shard_map/ppermute | solution.py:420
  257.1 0.9 copy-start.8

commit v4 on v2

v4 whole, which is shorter than its diff:
```python
import functools

import jax
import jax.numpy as jnp
from jax import lax
from jax.experimental import pallas as pl
from jax.experimental.pallas import tpu as pltpu
from jax.sharding import PartitionSpec as P

BF = jnp.bfloat16
F32 = jnp.float32
SLICE = 512
PART_A = 256
PART_B = SLICE - PART_A
SLICES = 8
GRADS = SLICES * SLICE
FIRST = GRADS + SLICES * PART_A
CAP = 32
LANES = 128
PACK_STEPS = 2
PRE_PER = 2
INPUT_BLOCK = 1024


def params(mib):
    return pltpu.CompilerParams(vmem_limit_bytes=mib * 1024 * 1024)


def in_hbm(x):
    return pltpu.with_memory_space_constraint(x, pltpu.HBM)


def in_vmem(x):
    return pltpu.with_memory_space_constraint(x, pltpu.VMEM)


def held(shape):
    return pl.BlockSpec(shape, lambda *_: (0,) * len(shape), pipeline_mode=pl.Buffered(1))


def left_in_hbm():
    return pl.BlockSpec(memory_space=pltpu.HBM)


def dot_nn(a, b):
    return lax.dot_general(a, b, (((1,), (0,)), ((), ())), preferred_element_type=F32)


def dot_nt(a, b):
    return lax.dot_general(a, b, (((1,), (1,)), ((), ())), preferred_element_type=F32)


def dot_tn(a, b):
    return lax.dot_general(a, b, (((0,), (0,)), ((), ())), preferred_element_type=F32)


def pack_kernel(ids_ref, gates_ref, tok_ref, dy_ref, first_ref, second_ref, hot_ref, *, step_experts):
    tokens = ids_ref.shape[1]
    base = pl.program_id(0) * step_experts
    expert = lax.broadcasted_iota(jnp.int32, (8, tokens), 0) + base
    zero = jnp.zeros((8, tokens), F32)
    is_0 = ids_ref[0:1, :] == expert
    is_1 = ids_ref[1:2, :] == expert
    named = is_0 | is_1
    member = jnp.where(named, 1.0, 0.0).astype(BF)
    row = lax.broadcasted_iota(jnp.int32, (tokens, tokens), 0)
    col = lax.broadcasted_iota(jnp.int32, (tokens, tokens), 1)
    earlier = jnp.where(row < col, 1.0, 0.0).astype(BF)
    place = jnp.where(named, dot_nn(member, earlier), -1.0)
    gates = gates_ref[...].astype(F32)
    weight = jnp.where(is_0, gates[0:1, :], zero) + jnp.where(is_1, gates[1:2, :], zero)
    rows = step_experts * CAP
    place_all = jnp.broadcast_to(place[:step_experts, None, :], (step_experts, CAP, tokens)).reshape(rows, tokens)
    weight_all = jnp.broadcast_to(weight[:step_experts, None, :], (step_experts, CAP, tokens)).reshape(rows, tokens)
    slot = (lax.broadcasted_iota(jnp.int32, (rows, tokens), 0) % CAP).astype(F32)
    hot = jnp.where(place_all == slot, 1.0, 0.0)
    slot_gate = jnp.sum(hot * weight_all, axis=1, keepdims=True)
    first_ref[:, FIRST:] = jnp.broadcast_to(slot_gate, (rows, LANES)).astype(BF)
    hot = hot.astype(BF)
    hot_ref[...] = hot
    for q in range(SLICES):
        cols = slice(q * SLICE, (q + 1) * SLICE)
        first_ref[:, cols] = dot_nn(hot, tok_ref[:, cols]).astype(BF)
        grads = dot_nn(hot, dy_ref[:, cols]).astype(BF)
        first_ref[:, GRADS + q * PART_A : GRADS + (q + 1) * PART_A] = grads[:, :PART_A]
        second_ref[:, q * PART_B : (q + 1) * PART_B] = grads[:, PART_A:]


def pack(ids, gates, tokens_in, out_grad, slots):
    steps = PACK_STEPS
    tok_dev, width = tokens_in.shape
    rows = slots // steps
    wide = FIRST + LANES
    whole = lambda shape: pl.BlockSpec(shape, lambda i: (0, 0))
    return pl.pallas_call(
        functools.partial(pack_kernel, step_experts=rows // CAP),
        grid=(steps,),
        in_specs=[whole((2, tok_dev)), whole((2, tok_dev)), whole((tok_dev, width)), whole((tok_dev, width))],
        out_specs=[
            pl.BlockSpec((rows, wide), lambda i: (i, 0)),
            pl.BlockSpec((rows, SLICES * PART_B), lambda i: (i, 0)),
            pl.BlockSpec((rows, tok_dev), lambda i: (i, 0)),
        ],
        out_shape=[
            pltpu.HBM((slots, wide), BF),
            pltpu.HBM((slots, SLICES * PART_B), BF),
            pltpu.HBM((slots, tok_dev), BF),
        ],
        compiler_params=params(24),
        name="pack",
    )(in_hbm(ids), in_hbm(gates), in_hbm(tokens_in), in_hbm(out_grad))


def pre_kernel(rows_ref, dy_ref, gate_ref, w_ref, wd_ref, *refs, per):
    outs, (u_acc, pg_acc, pu_acc, p_buf, gp_buf, sems) = refs[:5], refs[5:]
    step = pl.program_id(0)

    @pl.when(step == 0)
    def _():
        pg_acc[...] = jnp.zeros_like(pg_acc)
        pu_acc[...] = jnp.zeros_like(pu_acc)
        u_acc[...] = jnp.zeros_like(u_acc)

    depth = pl.ds(pl.multiple_of(step * per * SLICE, SLICE), per * SLICE)
    u_acc[...] += dot_nn(dy_ref[...], wd_ref[...].reshape(per * PART_A, wd_ref.shape[3]))
    x = rows_ref[...]
    pg_acc[...] += dot_nn(x, w_ref[0, depth, :])
    pu_acc[...] += dot_nn(x, w_ref[1, depth, :])

    @pl.when(step == pl.num_programs(0) - 1)
    def _():
        slots = pg_acc.shape[0]
        chunk, part = 32, slots // 4
        copies = [pltpu.make_async_copy(u_acc, outs[0], sems.at[4, 0])]
        copies[0].start()
        for k in range(4):

            def one(i, carry):
                at = pl.ds(pl.multiple_of(k * part + i * chunk, chunk), chunk)
                pg = pg_acc[at, :]
                pu = pu_acc[at, :]
                g = gate_ref[at, :].astype(F32)[:, :1]
                s = jax.nn.sigmoid(pg)
                a = pg * s
                product = a * pu
                p_buf[at, :] = product.astype(BF)
                gp_buf[at, :] = (g * product).astype(BF)
                pg_acc[at, :] = g * (pu * s * (1.0 + pg * (1.0 - s)))
                pu_acc[at, :] = g * a
                return carry

            lax.fori_loop(0, part // chunk, one, 0)
            for j, (buf, out) in enumerate(zip((pg_acc, pu_acc, p_buf, gp_buf), outs[1:])):
                at = pl.ds(k * part, part)
                copies.append(pltpu.make_async_copy(buf.at[at], out.at[at], sems.at[j, k]))
                copies[-1].start()
        for copy in copies:
            copy.wait()


def pre(first, w, wd):
    slots = first.shape[0]
    ff = wd.shape[3]
    per = PRE_PER
    return pl.pallas_call(
        functools.partial(pre_kernel, per=per),
        grid=(SLICES // per,),
        in_specs=[
            pl.BlockSpec((slots, per * SLICE), lambda q: (0, q)),
            pl.BlockSpec((slots, per * PART_A), lambda q: (0, GRADS // (per * PART_A) + q)),
            pl.BlockSpec((slots, LANES), lambda q: (0, FIRST // LANES)),
            pl.BlockSpec(memory_space=pltpu.VMEM),
            pl.BlockSpec((per, 1, PART_A, ff), lambda q: (q, 0, 0, 0)),
        ],
        out_specs=[left_in_hbm()] * 5,
        out_shape=[pltpu.HBM((slots, ff), t) for t in (F32, F32, F32, BF, BF)],
        scratch_shapes=[pltpu.VMEM((slots, ff), t) for t in (F32, F32, F32, BF, BF)]
        + [pltpu.SemaphoreType.DMA((5, 4))],
        compiler_params=params(24),
        name="pre",
    )(in_hbm(first), in_hbm(first), in_hbm(first), in_vmem(w), in_hbm(wd))


def hidden_kernel(dy_hbm, wd_hbm, u_hbm, c1_hbm, c2_hbm, p_hbm, h_ref, gate_ref, *scratch):
    dy, wd, u_acc, c1, c2, p, gate_acc, sems = scratch
    half = SLICES // 2
    depth = half * PART_B
    wanted = [
        (dy_hbm, dy),
        (wd_hbm.at[:half, 1], wd.at[:half]),
        (wd_hbm.at[half:, 1], wd.at[half:]),
        (u_hbm, u_acc),
        (c1_hbm, c1),
        (c2_hbm, c2),
        (p_hbm, p),
    ]
    copies = [pltpu.make_async_copy(src, dst, sems.at[k]) for k, (src, dst) in enumerate(wanted)]
    for copy in copies:
        copy.start()
    copies[0].wait()
    copies[1].wait()
    copies[3].wait()
    u_acc[...] += dot_nn(dy[:, :depth], wd[:half].reshape(depth, wd.shape[2]))
    copies[2].wait()
    u_acc[...] += dot_nn(dy[:, depth:], wd[half:].reshape(depth, wd.shape[2]))
    for copy in copies[4:]:
        copy.wait()
    chunk = 32

    def one(i, carry):
        at = pl.ds(pl.multiple_of(i * chunk, chunk), chunk)
        u = u_acc[at, :]
        h_ref[0, at, :] = (u * c1[at, :]).astype(BF)
        h_ref[1, at, :] = (u * c2[at, :]).astype(BF)
        both = u * p[at, :].astype(F32)
        folded = both[:, :LANES]
        for k in range(1, both.shape[1] // LANES):
            folded += both[:, k * LANES : (k + 1) * LANES]
        gate_acc[at, :] = folded
        return carry

    lax.fori_loop(0, u_acc.shape[0] // chunk, one, 0)
    total = jnp.sum(gate_acc[...], axis=1, keepdims=True)
    gate_ref[...] = jnp.broadcast_to(total, gate_ref.shape).astype(BF)


def hidden(second, wd, u_a, c1, c2, p, gate_at):
    slots, ff = p.shape
    return pl.pallas_call(
        hidden_kernel,
        grid=(1,),
        in_specs=[pl.BlockSpec(memory_space=pl.ANY)] + [left_in_hbm()] * 5,
        out_specs=[held((2, slots, ff)), pl.BlockSpec((slots, LANES), lambda j: (0, gate_at // LANES))],
        out_shape=[pltpu.HBM((2, slots, ff), BF), pltpu.HBM((slots, gate_at + LANES), BF)],
        scratch_shapes=[
            pltpu.VMEM(second.shape, BF),
            pltpu.VMEM((SLICES, PART_B, ff), BF),
            pltpu.VMEM((slots, ff), F32),
            pltpu.VMEM((slots, ff), F32),
            pltpu.VMEM((slots, ff), F32),
            pltpu.VMEM((slots, ff), BF),
            pltpu.VMEM((slots, LANES), F32),
            pltpu.SemaphoreType.DMA((7,)),
        ],
        compiler_params=params(24),
        name="hidden",
    )(second, *map(in_hbm, (wd, u_a, c1, c2, p)))


def input_kernel(h_ref, w_ref, into_ref, out_ref):
    del into_ref
    out_ref[...] = (dot_nt(h_ref[0], w_ref[0]) + dot_nt(h_ref[1], w_ref[1])).astype(BF)


def input_rows(h, w, begin, cols, into):
    _, slots, ff = h.shape
    blk = INPUT_BLOCK
    first = begin // blk
    return pl.pallas_call(
        input_kernel,
        grid=(cols // blk,),
        in_specs=[held((2, slots, ff)), pl.BlockSpec((2, blk, ff), lambda j: (0, first + j, 0)), left_in_hbm()],
        out_specs=pl.BlockSpec((slots, blk), lambda j: (0, first + j)),
        out_shape=pltpu.HBM(into.shape, BF),
        input_output_aliases={2: 0},
        compiler_params=params(24),
        name="input_rows",
    )(in_hbm(h), in_hbm(w), in_hbm(into))


def down_kernel(rows_ref, gp_ref, out_ref):
    for k in range(2):
        part = dot_tn(rows_ref[:, k * PART_A : (k + 1) * PART_A], gp_ref[...])
        out_ref[k * PART_A : (k + 1) * PART_A] = part.astype(BF)


def down_parts(own, gp):
    slots, ff = gp.shape
    return pl.pallas_call(
        down_kernel,
        grid=(SLICES // 2,),
        in_specs=[pl.BlockSpec((slots, 2 * PART_A), lambda i: (0, GRADS // (2 * PART_A) + i)), held((slots, ff))],
        out_specs=pl.BlockSpec((2 * PART_A, ff), lambda i: (i, 0)),
        out_shape=pltpu.HBM((SLICES * PART_A, ff), BF),
        compiler_params=params(16),
        name="down_parts",
    )(in_hbm(own), in_hbm(gp))


EXTRA = PART_B // 2


def unit_kernel(me_ref, own_ref, mate_ref, dy_ref, dy_mate_ref, h_ref, h_mate_ref, gp_ref, gp_mate_ref, out_ref):
    del me_ref
    ff = gp_ref.shape[1]
    own = own_ref[...]
    mate = mate_ref[...]
    for k in range(2):
        part = dot_tn(own, h_ref[k]) + dot_tn(mate, h_mate_ref[k])
        out_ref[:SLICE, k * ff : (k + 1) * ff] = part.astype(BF)
    down = (dot_tn(dy_ref[...], gp_ref[...]) + dot_tn(dy_mate_ref[...], gp_mate_ref[...])).astype(BF)
    out_ref[SLICE:, :ff] = down[:EXTRA]
    out_ref[SLICE:, ff:] = down[EXTRA:]


def units(me, first, mate_first, second, mate_second, h, h_mate, gp, gp_mate):
    _, slots, ff = h.shape
    rows = pl.BlockSpec((slots, SLICE), lambda i, me: (0, 2 * i + me[0] % 2))
    grads = pl.BlockSpec((slots, PART_B), lambda i, me: (0, 2 * i + me[0] % 2))
    deep = SLICE + EXTRA
    return pl.pallas_call(
        unit_kernel,
        grid_spec=pltpu.PrefetchScalarGridSpec(
            num_scalar_prefetch=1,
            grid=(4,),
            in_specs=[rows, rows, grads, grads] + [held((2, slots, ff))] * 2 + [held((slots, ff))] * 2,
            out_specs=pl.BlockSpec((deep, 2 * ff), lambda i, me: (i, 0)),
        ),
        out_shape=pltpu.HBM((4 * deep, 2 * ff), BF),
        compiler_params=params(20),
        name="units",
    )(me, in_hbm(first), in_hbm(mate_first), second, mate_second, in_hbm(h), h_mate, in_hbm(gp), gp_mate)


def unpack_kernel(hot_ref, rows_ref, ids_ref, gates_ref, out_ref, gate_ref):
    out_ref[...] = dot_tn(hot_ref[...], rows_ref[...]).astype(BF)

    @pl.when(pl.program_id(0) == 0)
    def _():
        hot = hot_ref[...]
        expert = lax.broadcasted_iota(jnp.int32, hot.shape, 0) // CAP
        for k in range(2):
            chosen = jnp.where(expert == ids_ref[k : k + 1, :], hot.astype(F32), 0.0).astype(BF)
            gate_ref[k : k + 1, :] = dot_tn(gates_ref[...], chosen)[0:1, :].astype(BF)


def unpack(hot, ids, back, width):
    slots, tok_dev = hot.shape
    blk = 1024
    whole = lambda shape: pl.BlockSpec(shape, lambda i: (0, 0))
    return pl.pallas_call(
        unpack_kernel,
        grid=(width // blk,),
        in_specs=[
            whole((slots, tok_dev)),
            pl.BlockSpec((slots, blk), lambda i: (0, i)),
            whole((2, tok_dev)),
            pl.BlockSpec((slots, LANES), lambda i: (0, width // LANES)),
        ],
        out_specs=[pl.BlockSpec((tok_dev, blk), lambda i: (0, i)), whole((2, tok_dev))],
        out_shape=[pltpu.HBM((tok_dev, width), BF), pltpu.HBM((2, tok_dev), BF)],
        compiler_params=params(16),
        name="unpack",
    )(*map(in_hbm, (hot, back, ids, back)))


SWAP = [(i, i ^ 1) for i in range(8)]
CHIPS = [[0, 2, 4, 6], [1, 3, 5, 7]]


def body(tokens_in, out_grad, expert_ids, gate_probs, gate_up, down_proj):
    width = tokens_in.shape[1]
    owners = lax.axis_size("expert")
    ff = gate_up.shape[3]
    slots = owners * CAP
    me = lax.axis_index("dp")

    ids = expert_ids.T
    first, second, hot = pack(ids, gate_probs.T, tokens_in, out_grad, slots)

    def exchange(rows):
        wide = rows.shape[1]
        got = lax.all_to_all(rows.reshape(owners, CAP, wide), "expert", split_axis=0, concat_axis=0, tiled=True)
        return got.reshape(slots, wide)

    def swap(x):
        return lax.ppermute(x, "dp", SWAP)

    me = me.reshape(1).astype(jnp.int32)
    first, me = lax.optimization_barrier((first, me))
    first, gate_up, down_proj = lax.optimization_barrier((exchange(first), gate_up, down_proj))
    second = exchange(second)
    mate_first = swap(first)
    w = jnp.transpose(gate_up[:, :, 0], (1, 0, 2))
    wd = down_proj.reshape(SLICES, 2, PART_A, ff)
    u_a, c1, c2, p, gp = pre(first, w, wd)
    gp_mate = swap(gp)

    down_a = down_parts(first, gp)
    second, down_a = lax.optimization_barrier((second, down_a))
    grad_a = lax.psum_scatter(down_a, "dp", scatter_dimension=0, tiled=True)

    mate_second = swap(second)
    h, rows = hidden(second, wd, u_a, c1, c2, p, width)
    h_mate = swap(h)
    parts = units(me, first, mate_first, second, mate_second, h, h_mate, gp, gp_mate)
    parts, grad_a, rows = lax.optimization_barrier((parts, grad_a, rows))
    sums = lax.psum_scatter(parts, "dp", scatter_dimension=0, tiled=True, axis_index_groups=CHIPS)
    back = exchange(input_rows(h, w, 0, width, rows))

    gate_up_grad = sums[:SLICE].reshape(SLICE, 2, 1, ff)
    down_grad = jnp.concatenate([grad_a, sums[SLICE:, :ff], sums[SLICE:, ff:]], axis=0)[:, None, :]
    input_grad, gate_grad = unpack(hot, ids, back, width)
    return (input_grad, gate_grad.T, gate_up_grad, down_grad)


def solution(mesh):
    placed = (
        P(("dp", "expert"), None),
        P(("dp", "expert"), None),
        P(("dp", "expert"), None),
        P(("dp", "expert"), None),
        P(None, None, "expert", None),
        P(None, "expert", None),
    )
    return jax.shard_map(
        body,
        mesh=mesh,
        in_specs=placed,
        out_specs=(
            P(("dp", "expert"), None),
            P(("dp", "expert"), None),
            P("dp", None, "expert", None),
            P("dp", "expert", None),
        ),
        check_vma=False,
    )
```

time: 302 us -> 259 us (0.86)
  blocking collectives: 0 us -> 138 us
  waiting for transfers between devices: 146 us -> 24.4 us
  starting transfers between devices: 41 us -> 4.62 us
  local copies, waits for them, and re-layouts: 43.3 us -> 11.2 us
  between operations: 0.99 us -> 14.1 us
  other arithmetic: 8.61 us -> 1.93 us
    all_to_all x0 -> x2, blocking collectives: none -> 138 us  [exchange(): lax.all_to_all(rows.reshape(owners, CAP, wide), 'expert', split_axis=0, c...]
    all_to_all x3 -> x1, waiting for transfers between devices: 109 us -> 0.6 us  [exchange(): lax.all_to_all(rows.reshape(owners, CAP, wide), 'expert', split_axis=0, c...]
    ppermute x12 -> x0, waiting for transfers between devices: 31.8 us -> none  [ring(): arrived = lax.ppermute(total, 'dp', perm)]
    unnamed x71 -> x6, local copies, waits for them, and re-layouts: 29.3 us -> 0.81 us
    ppermute x12 -> x0, starting transfers between devices: 20.1 us -> none  [ring(): arrived = lax.ppermute(total, 'dp', perm)]
    reduce_scatter x0 -> x2, waiting for transfers between devices: none -> 19.4 us  [the longest x1 13.5 us: body(): grad_a = lax.psum_scatter(down_a, 'dp', scatter_dimension=0, tiled=True)]
    all_to_all x3 -> x1, starting transfers between devices: 20.1 us -> 3.72 us  [exchange(): lax.all_to_all(rows.reshape(owners, CAP, wide), 'expert', split_axis=0, c...]
    convert_element_type x7 -> x0, other arithmetic: 8.39 us -> none  [ring(): total = (arrived.astype(F32) + part.astype(F32)).astype(BF)]
  transfers between devices with their start and end apart: 19 -> 7, of which waited for: 9 -> 5; matrix products, arithmetic and copies ran while one was open for 7% -> 3% of each run, Pallas kernels for 14% -> 22%
where the time goes in v4:
time: 259 us; the launch traced here: 257 us
  blocking collectives  138 us (53%)
  Pallas kernels  63 us (24%)
  waiting for transfers between devices  24.4 us (9%)
  between operations  14.1 us (5%)
  local copies, waits for them, and re-layouts  11.2 us (4%)
  starting transfers between devices  4.62 us (2%)
    all_to_all x2, blocking collectives, exchange(): lax.all_to_all(rows.reshape(owners, CAP, wide), 'expert', split_axis=0, c...  138 us
    pallas_call x1, Pallas kernels, pre(): pl.pallas_call(functools.partial(pre_kernel, per=per), grid=(SLICES // pe...  15.5 us
    reduce_scatter x1, waiting for transfers between devices, body(): grad_a = lax.psum_scatter(down_a, 'dp', scatter_dimension=0, tiled=True)  13.5 us
    pallas_call x1, Pallas kernels, units(): pl.pallas_call(unit_kernel, grid_spec=pltpu.PrefetchScalarGridSpec(num_sc...  12.7 us
    pallas_call x1, Pallas kernels, input_rows(): pl.pallas_call(input_kernel, grid=(cols // blk,), in_specs=[held((2, slot...  11.3 us
    optimization_barrier x1, local copies, waits for them, and re-layouts, body(): lax.optimization_barrier((exchange(first), gate_up, down_proj))  7.68 us
    pallas_call x1, Pallas kernels, hidden(): pl.pallas_call(hidden_kernel, grid=(1,), in_specs=[pl.BlockSpec(memory_sp...  6.66 us
    pallas_call x1, Pallas kernels, pack(): pl.pallas_call(functools.partial(pack_kernel, step_experts=rows // CAP),...  6.48 us
  transfers between devices with their start and end apart: 7, of which 5 were waited for; matrix products, arithmetic and copies ran while one was open for 3% of the time, Pallas kernels for 22%

profile of v4, /device:TPU:0, one launch (start us, length us, event | category | flops | bytes accessed | tf_op | source)
XLA Modules:
  0.0 257.3 jit_solution(10887767875475786340)
XLA Ops:
  7.2 6.5 %pack.1 = (bf16[512,6272]{1,0:T(8,128)(2,1)}, bf16[512,2048]{1,0:T(8,128)(2,1)}, bf16[512,128]{1,0:T(8,128)(2,1)}) custom-call(s32[2,128]{1,0:T(2,128)} %bitcast.38, bf16[2,128]{1,0:T(2,128)(2,1)} %bitcast.40, bf16[128,4096]{1,0:T(8,128)(2,1)} %tok_ref.1, bf16[128,4096]{1,0:T(8,128)(2,1)} %dy_ref.1), custom_call_target="tpu_custom_call" | custom-call | tf_op jit(solution)/shard_map/pack/pallas_call | solution.py:95
  13.7 82.0 %all_to_all.15 = bf16[16,32,6272]{2,1,0:T(8,128)(2,1)} all-to-all(bf16[16,32,6272]{2,1,0:T(8,128)(2,1)} %bitcast.35), channel_id=1, replica_groups=mesh['dp'=8,'expert'=16] {'expert'}, dimensions={0} | all-to-all | bytes 12845056 | tf_op jit(solution)/shard_map/all_to_all | solution.py:373
  95.6 3.7 %all-to-all-start = ((bf16[16,32,2048]{2,1,0:T(8,128)(2,1)}), bf16[16,32,2048]{2,1,0:T(8,128)(2,1)S(1)}, u32[]{:S(2)}, u32[]{:S(2)}) async-start(bf16[16,32,2048]{2,1,0:T(8,128)(2,1)} %bitcast.36), calls=%async_computation | async-start | bytes 4194304 | tf_op jit(solution)/shard_map/all_to_all | solution.py:373
  99.3 0.0 reduce-scatter.3.cloned.1.call-start
  99.4 0.1 collective-permute-start
  99.5 7.7 %copy.14 = bf16[4096,2,1,768]{3,0,1,2:T(8,128)(2,1)S(1)} copy(bf16[4096,2,1,768]{3,1,2,0:T(2,128)(2,1)} %param.10) | data formatting | bytes 25165824 | tf_op jit(solution)/shard_map/optimization_barrier | solution.py:381
  107.2 0.0 copy-start
  107.2 15.5 %pre.1 = (f32[512,768]{1,0:T(8,128)}, f32[512,768]{1,0:T(8,128)}, f32[512,768]{1,0:T(8,128)}, bf16[512,768]{1,0:T(8,128)(2,1)}, bf16[512,768]{1,0:T(8,128)(2,1)}) custom-call(bf16[512,6272]{1,0:T(8,128)(2,1)} %bitcast.25, bf16[512,6272]{1,0:T(8,128)(2,1)} %bitcast.26, bf16[512,6272]{1,0:T(8,128)(2,1)} %bitcast.27, bf16[2,4096,768]{2,1,0:T(8,128)(2,1)S(1)} %bitcast.19, ...), custom_call_target="tpu_custom_call" | custom-call | tf_op jit(solution)/shard_map/pre/pallas_call | solution.py:165
  122.7 0.0 copy-done
  122.7 5.4 %down_parts.1 = bf16[2048,768]{1,0:T(8,128)(2,1)} custom-call(bf16[512,6272]{1,0:T(8,128)(2,1)} %bitcast.28, bf16[512,768]{1,0:T(8,128)(2,1)} %get-tuple-element.33.gp_ref), custom_call_target="tpu_custom_call" | custom-call | tf_op jit(solution)/shard_map/down_parts/pallas_call | solution.py:279
  128.1 0.6 all-to-all-done
  128.7 0.0 reduce-scatter.3.cloned.1.call-update
  128.7 0.0 reduce-scatter.5.cloned.1.call-start
  128.8 0.1 collective-permute-start.1
  128.9 0.0 copy-start.2
  128.9 6.7 %hidden.1 = (bf16[2,512,768]{2,1,0:T(8,128)(2,1)}, bf16[512,4224]{1,0:T(8,128)(2,1)}) custom-call(bf16[512,2048]{1,0:T(8,128)(2,1)S(1)} %bitcast.22, bf16[8,2,256,768]{3,2,1,0:T(8,128)(2,1)} %bitcast.33, f32[512,768]{1,0:T(8,128)} %get-tuple-element.35.u_hbm, f32[512,768]{1,0:T(8,128)} %get-tuple-element.36.c1_hbm, f32[512,768]{1,0:T(8,128)} %get-tuple-element.37.c2_hbm, ...), custom_call_target="tpu_custom_call" | custom-call | tf_op jit(solution)/shard_map/hidden/pallas_call | solution.py:229
  135.6 0.6 collective-permute-start.2
  136.1 0.0 copy-done.2
  136.1 0.1 collective-permute-start.3
  136.2 4.0 %collective-permute-done.3.gp_mate_ref = bf16[512,768]{1,0:T(8,128)(2,1)S(1)} collective-permute-done((bf16[512,768]{1,0:T(8,128)(2,1)S(1)}, bf16[512,768]{1,0:T(8,128)(2,1)S(1)}, u32[]{:S(2)}, u32[]{:S(2)}) %collective-permute-start.3) | collective-permute-done | bytes 786464 | tf_op jit(solution)/shard_map/ppermute | solution.py:377
  140.2 0.4 collective-permute-done.2.h_mate_ref
  140.6 0.0 collective-permute-done.1.dy_mate_ref
  140.6 0.0 collective-permute-done.mate_ref
  140.6 12.7 %units.1 = bf16[2560,1536]{1,0:T(8,128)(2,1)} custom-call(s32[1]{0:T(128)} %bitcast.4.me_ref, bf16[512,6272]{1,0:T(8,128)(2,1)} %bitcast.29, bf16[512,6272]{1,0:T(8,128)(2,1)} %collective-permute-done.mate_ref, bf16[512,2048]{1,0:T(8,128)(2,1)S(1)} %bitcast.23, bf16[512,2048]{1,0:T(8,128)(2,1)S(1)} %collective-permute-done.1.dy_mate_ref, ...), custom_call_target="tpu_custom_call" | custom-call | tf_op jit(solution)/shard_map/units/pallas_call | solution.py:311
  153.3 13.5 %reduce-scatter.3.cloned.1.call-done = bf16[256,768]{1,0:T(8,128)(2,1)} async-done(((bf16[2048,768]{1,0:T(8,128)(2,1)}), bf16[256,768]{1,0:T(8,128)(2,1)}) %reduce-scatter.3.cloned.1.call-update) | async-done | bytes 393232 | tf_op jit(solution)/shard_map/reduce_scatter | solution.py:391
  166.8 0.0 reduce-scatter.5.cloned.1.call-update
  166.9 11.3 %input_rows.1 = bf16[512,4224]{1,0:T(8,128)(2,1)} custom-call(bf16[2,512,768]{2,1,0:T(8,128)(2,1)} %get-tuple-element.39.h_ref, bf16[2,4096,768]{2,1,0:T(8,128)(2,1)} %bitcast.20, bf16[512,4224]{1,0:T(8,128)(2,1)} %get-tuple-element.43.into_ref), custom_call_target="tpu_custom_call", output_to_operand_aliasing={{}: (2, {})} | custom-call | tf_op jit(solution)/shard_map/input_rows/pallas_call | solution.py:259
  178.2 56.0 %all_to_all.16 = bf16[16,32,4224]{2,1,0:T(8,128)(2,1)} all-to-all(bf16[16,32,4224]{2,1,0:T(8,128)(2,1)} %bitcast.34), channel_id=1, replica_groups=mesh['dp'=8,'expert'=16] {'expert'}, dimensions={0} | all-to-all | bytes 8650752 | tf_op jit(solution)/shard_map/all_to_all | solution.py:373
  234.1 5.0 %unpack.1 = (bf16[128,4096]{1,0:T(8,128)(2,1)}, bf16[2,128]{1,0:T(2,128)(2,1)}) custom-call(bf16[512,128]{1,0:T(8,128)(2,1)} %get-tuple-element.26.hot_ref, bf16[512,4224]{1,0:T(8,128)(2,1)} %bitcast.30, s32[2,128]{1,0:T(2,128)} %bitcast.39, bf16[512,4224]{1,0:T(8,128)(2,1)} %bitcast.31), custom_call_target="tpu_custom_call" | custom-call | tf_op jit(solution)/shard_map/unpack/pallas_call | solution.py:341
  239.1 5.8 %reduce-scatter.5.cloned.1.call-done = bf16[640,1536]{1,0:T(8,128)(2,1)} async-done(((bf16[2560,1536]{1,0:T(8,128)(2,1)}), bf16[640,1536]{1,0:T(8,128)(2,1)}) %reduce-scatter.5.cloned.1.call-update) | async-done | bytes 1966096 | tf_op jit(solution)/shard_map/reduce_scatter | solution.py:398
  244.9 0.0 slice-start
  244.9 1.4 slice-done
  246.3 0.0 copy-start.1
  246.3 1.3 reshape.43
  247.7 0.8 copy-done.1
  248.5 1.9 maximum_bitcast_fusion
  (1 shorter events, 0.0 us)
Async XLA Ops:
  95.6 33.1 %all-to-all-start = ((bf16[16,32,2048]{2,1,0:T(8,128)(2,1)}), bf16[16,32,2048]{2,1,0:T(8,128)(2,1)S(1)}, u32[]{:S(2)}, u32[]{:S(2)}) async-start(bf16[16,32,2048]{2,1,0:T(8,128)(2,1)} %bitcast.36), calls=%async_computation | async-start | bytes 4194304 | tf_op jit(solution)/shard_map/all_to_all | solution.py:373
  99.3 67.5 %reduce-scatter.3.cloned.1.call-start = ((), (), s32[]{:S(2)}) async-start(), calls=%async_computation.5 | async-start | bytes 3538944 | tf_op jit(solution)/shard_map/reduce_scatter | solution.py:391
  99.4 41.2 %collective-permute-start = (bf16[512,6272]{1,0:T(8,128)(2,1)}, bf16[512,6272]{1,0:T(8,128)(2,1)}, u32[]{:S(2)}, u32[]{:S(2)}) collective-permute-start(bf16[512,6272]{1,0:T(8,128)(2,1)} %bitcast.24), channel_id=1, source_target_pairs={{0,16},{16,0},{32,48},{48,32},{64,80},{80,64},{96,112},{112,96},{1... | collective-permute-start | bytes 19267592 | tf_op jit(solution)/shard_map/ppermute | solution.py:377
  107.2 15.5 %copy-start = (bf16[4096,2,1,768]{3,0,1,2:T(8,128)(2,1)}, bf16[4096,2,1,768]{3,0,1,2:T(8,128)(2,1)S(1)}, u32[]{:S(2)}) copy-start(bf16[4096,2,1,768]{3,0,1,2:T(8,128)(2,1)S(1)} %copy.14) | copy-start | bytes 37748740
  128.7 116.2 %reduce-scatter.5.cloned.1.call-start = ((), (), s32[]{:S(2)}) async-start(), calls=%async_computation.6 | async-start | bytes 9830400 | tf_op jit(solution)/shard_map/reduce_scatter | solution.py:398
  128.8 11.8 %collective-permute-start.1 = (bf16[512,2048]{1,0:T(8,128)(2,1)S(1)}, bf16[512,2048]{1,0:T(8,128)(2,1)S(1)}, u32[]{:S(2)}, u32[]{:S(2)}) collective-permute-start(bf16[512,2048]{1,0:T(8,128)(2,1)S(1)} %bitcast.21), channel_id=1, source_target_pairs={{0,16},{16,0},{32,48},{48,32},{64,80},{80,64},{96,112},{112,96},{1... | collective-permute-start | bytes 6291464 | tf_op jit(solution)/shard_map/ppermute | solution.py:377
  128.9 7.2 %copy-start.2 = (bf16[512,768]{1,0:T(8,128)(2,1)S(1)}, bf16[512,768]{1,0:T(8,128)(2,1)}, u32[]{:S(2)}) copy-start(bf16[512,768]{1,0:T(8,128)(2,1)} %get-tuple-element.33.gp_ref) | copy-start | bytes 2359300
  135.6 5.0 %collective-permute-start.2 = (bf16[2,512,768]{2,1,0:T(8,128)(2,1)}, bf16[2,512,768]{2,1,0:T(8,128)(2,1)S(1)}, u32[]{:S(2)}, u32[]{:S(2)}) collective-permute-start(bf16[2,512,768]{2,1,0:T(8,128)(2,1)} %get-tuple-element.39.h_ref), channel_id=1, source_target_pairs={{0,16},{16,0},{32,48},{48,32},{64,80},{80,64},{96,112},{112,96},{1... | collective-permute-start | bytes 4718600 | tf_op jit(solution)/shard_map/ppermute | solution.py:377
  136.1 4.1 %collective-permute-start.3 = (bf16[512,768]{1,0:T(8,128)(2,1)S(1)}, bf16[512,768]{1,0:T(8,128)(2,1)S(1)}, u32[]{:S(2)}, u32[]{:S(2)}) collective-permute-start(bf16[512,768]{1,0:T(8,128)(2,1)S(1)} %copy-done.2), channel_id=1, source_target_pairs={{0,16},{16,0},{32,48},{48,32},{64,80},{80,64},{96,112},{112,96},{1... | collective-permute-start | bytes 2359304 | tf_op jit(solution)/shard_map/ppermute | solution.py:377
  244.9 1.4 slice-start
  246.3 2.1 copy-start.1
Sparse Core Ops, SparseCore 0:
  128.9 37.9 reduce-scatter.2
  169.3 75.6 reduce-scatter.4

commit v5 on v4

--- a/solution.py
+++ b/solution.py
@@ -108,6 +108,7 @@
         ],
         compiler_params=params(24),
         name="pack",
+        cost_estimate=pl.CostEstimate(flops=3000000000, transcendentals=0, bytes_accessed=14000000),
     )(in_hbm(ids), in_hbm(gates), in_hbm(tokens_in), in_hbm(out_grad))
 
 
@@ -178,6 +179,7 @@
         + [pltpu.SemaphoreType.DMA((5, 4))],
         compiler_params=params(24),
         name="pre",
+        cost_estimate=pl.CostEstimate(flops=17000000000, transcendentals=0, bytes_accessed=40000000),
     )(in_hbm(first), in_hbm(first), in_hbm(first), in_vmem(w), in_hbm(wd))
 
 
@@ -244,6 +246,7 @@
         ],
         compiler_params=params(24),
         name="hidden",
+        cost_estimate=pl.CostEstimate(flops=4000000000, transcendentals=0, bytes_accessed=14000000),
     )(second, *map(in_hbm, (wd, u_a, c1, c2, p)))
 
 
@@ -265,60 +268,98 @@
         input_output_aliases={2: 0},
         compiler_params=params(24),
         name="input_rows",
+        cost_estimate=pl.CostEstimate(flops=13000000000, transcendentals=0, bytes_accessed=24000000),
     )(in_hbm(h), in_hbm(w), in_hbm(into))
 
 
-def down_kernel(rows_ref, gp_ref, out_ref):
-    for k in range(2):
-        part = dot_tn(rows_ref[:, k * PART_A : (k + 1) * PART_A], gp_ref[...])
-        out_ref[k * PART_A : (k + 1) * PART_A] = part.astype(BF)
-
-
-def down_parts(own, gp):
+def chip_at(me, hop, up):
+    return jnp.where(up, me // 2 + 3 - hop, me // 2 + 1 + hop) % 4
+
+
+def down_kernel(me_ref, own_ref, mate_ref, gp_ref, gp_mate_ref, up_ref, dn_ref, up_rest_ref, dn_rest_ref):
+    del me_ref
+    step = pl.program_id(0)
+    part = (dot_tn(own_ref[...], gp_ref[...]) + dot_tn(mate_ref[...], gp_mate_ref[...])).astype(BF)
+    half = PART_A // 2
+
+    @pl.when(step == 0)
+    def _():
+        up_ref[...] = part[:half]
+
+    @pl.when(step == 2)
+    def _():
+        dn_ref[...] = part[half:]
+
+    up_rest_ref[0] = part[:half]
+    dn_rest_ref[0] = part[half:]
+
+
+def down_parts(me, own, mate, gp, gp_mate):
     slots, ff = gp.shape
+    rows = pl.BlockSpec(
+        (slots, PART_A), lambda i, me: (0, GRADS // PART_A + 2 * chip_at(me[0], i, True) + me[0] % 2)
+    )
+    half = PART_A // 2
     return pl.pallas_call(
         down_kernel,
-        grid=(SLICES // 2,),
-        in_specs=[pl.BlockSpec((slots, 2 * PART_A), lambda i: (0, GRADS // (2 * PART_A) + i)), held((slots, ff))],
-        out_specs=pl.BlockSpec((2 * PART_A, ff), lambda i: (i, 0)),
-        out_shape=pltpu.HBM((SLICES * PART_A, ff), BF),
+        grid_spec=pltpu.PrefetchScalarGridSpec(
+            num_scalar_prefetch=1,
+            grid=(4,),
+            in_specs=[rows, rows, held((slots, ff)), held((slots, ff))],
+            out_specs=[pl.BlockSpec((half, ff), lambda i, me: (0, 0))] * 2
+            + [pl.BlockSpec((1, half, ff), lambda i, me: (i, 0, 0))] * 2,
+        ),
+        out_shape=[pltpu.HBM((half, ff), BF)] * 2 + [pltpu.HBM((4, half, ff), BF)] * 2,
         compiler_params=params(16),
         name="down_parts",
-    )(in_hbm(own), in_hbm(gp))
-
-
-EXTRA = PART_B // 2
-
-
-def unit_kernel(me_ref, own_ref, mate_ref, dy_ref, dy_mate_ref, h_ref, h_mate_ref, gp_ref, gp_mate_ref, out_ref):
-    del me_ref
+        cost_estimate=pl.CostEstimate(flops=4000000000, transcendentals=0, bytes_accessed=12000000),
+    )(me, in_hbm(own), in_hbm(mate), in_hbm(gp), gp_mate)
+
+
+UNIT = SLICE // 2
+EXTRA = PART_B // 4
+
+
+def unit_part(own_ref, mate_ref, dy_ref, dy_mate_ref, h_ref, h_mate_ref, gp_ref, gp_mate_ref, out_ref):
     ff = gp_ref.shape[1]
     own = own_ref[...]
     mate = mate_ref[...]
     for k in range(2):
         part = dot_tn(own, h_ref[k]) + dot_tn(mate, h_mate_ref[k])
-        out_ref[:SLICE, k * ff : (k + 1) * ff] = part.astype(BF)
+        out_ref[:UNIT, k * ff : (k + 1) * ff] = part.astype(BF)
     down = (dot_tn(dy_ref[...], gp_ref[...]) + dot_tn(dy_mate_ref[...], gp_mate_ref[...])).astype(BF)
-    out_ref[SLICE:, :ff] = down[:EXTRA]
-    out_ref[SLICE:, ff:] = down[EXTRA:]
-
-
-def units(me, first, mate_first, second, mate_second, h, h_mate, gp, gp_mate):
+    out_ref[UNIT:, :ff] = down[:EXTRA]
+    out_ref[UNIT:, ff:] = down[EXTRA:]
+
+
+def units_kernel(me_ref, *refs):
+    del me_ref
+    ins, outs = refs[:8], refs[8:]
+    for k, out in enumerate(outs):
+
+        @pl.when(pl.program_id(0) == k)
+        def _():
+            unit_part(*ins, out)
+
+
+def units(me, first, mate_first, second, mate_second, h, h_mate, gp, gp_mate, hop, hops):
     _, slots, ff = h.shape
-    rows = pl.BlockSpec((slots, SLICE), lambda i, me: (0, 2 * i + me[0] % 2))
-    grads = pl.BlockSpec((slots, PART_B), lambda i, me: (0, 2 * i + me[0] % 2))
-    deep = SLICE + EXTRA
-    return pl.pallas_call(
-        unit_kernel,
+    at = lambda i, me: 2 * (2 * chip_at(me[0], hop + i // 2, i % 2 == 0) + me[0] % 2) + i % 2
+    rows = pl.BlockSpec((slots, UNIT), lambda i, me: (0, at(i, me)))
+    grads = pl.BlockSpec((slots, PART_B // 2), lambda i, me: (0, at(i, me)))
+    shape = (UNIT + EXTRA, 2 * ff)
+    return pl.pallas_call(
+        units_kernel,
         grid_spec=pltpu.PrefetchScalarGridSpec(
             num_scalar_prefetch=1,
-            grid=(4,),
+            grid=(2 * hops,),
             in_specs=[rows, rows, grads, grads] + [held((2, slots, ff))] * 2 + [held((slots, ff))] * 2,
-            out_specs=pl.BlockSpec((deep, 2 * ff), lambda i, me: (i, 0)),
+            out_specs=[pl.BlockSpec(shape, lambda i, me: (0, 0))] * (2 * hops),
         ),
-        out_shape=pltpu.HBM((4 * deep, 2 * ff), BF),
-        compiler_params=params(20),
+        out_shape=[pltpu.HBM(shape, BF)] * (2 * hops),
+        compiler_params=params(28),
         name="units",
+        cost_estimate=pl.CostEstimate(flops=4000000000, transcendentals=0, bytes_accessed=12000000),
     )(me, in_hbm(first), in_hbm(mate_first), second, mate_second, in_hbm(h), h_mate, in_hbm(gp), gp_mate)
 
 
@@ -351,11 +392,21 @@
         out_shape=[pltpu.HBM((tok_dev, width), BF), pltpu.HBM((2, tok_dev), BF)],
         compiler_params=params(16),
         name="unpack",
+        cost_estimate=pl.CostEstimate(flops=1000000000, transcendentals=0, bytes_accessed=10000000),
     )(*map(in_hbm, (hot, back, ids, back)))
 
 
 SWAP = [(i, i ^ 1) for i in range(8)]
-CHIPS = [[0, 2, 4, 6], [1, 3, 5, 7]]
+UP = [(i, (i + 2) % 8) for i in range(8)]
+DOWN = [(i, (i - 2) % 8) for i in range(8)]
+
+
+def pass_on(up, dn):
+    return lax.ppermute(up, "dp", UP), lax.ppermute(dn, "dp", DOWN)
+
+
+def added(arrived, parts):
+    return tuple((a.astype(F32) + b.astype(F32)).astype(BF) for a, b in zip(arrived, parts))
 
 
 def body(tokens_in, out_grad, expert_ids, gate_probs, gate_up, down_proj):
@@ -385,21 +436,37 @@
     wd = down_proj.reshape(SLICES, 2, PART_A, ff)
     u_a, c1, c2, p, gp = pre(first, w, wd)
     gp_mate = swap(gp)
-
-    down_a = down_parts(first, gp)
-    second, down_a = lax.optimization_barrier((second, down_a))
-    grad_a = lax.psum_scatter(down_a, "dp", scatter_dimension=0, tiled=True)
-
+    down_up, down_dn, rest_up, rest_dn = down_parts(me, first, mate_first, gp, gp_mate)
+    down_sum = pass_on(down_up, down_dn)
+    second, rest_up, rest_dn = lax.optimization_barrier((second, rest_up, rest_dn))
     mate_second = swap(second)
     h, rows = hidden(second, wd, u_a, c1, c2, p, width)
     h_mate = swap(h)
-    parts = units(me, first, mate_first, second, mate_second, h, h_mate, gp, gp_mate)
-    parts, grad_a, rows = lax.optimization_barrier((parts, grad_a, rows))
-    sums = lax.psum_scatter(parts, "dp", scatter_dimension=0, tiled=True, axis_index_groups=CHIPS)
-    back = exchange(input_rows(h, w, 0, width, rows))
-
-    gate_up_grad = sums[:SLICE].reshape(SLICE, 2, 1, ff)
-    down_grad = jnp.concatenate([grad_a, sums[SLICE:, :ff], sums[SLICE:, ff:]], axis=0)[:, None, :]
+    h_mate, down_sum = lax.optimization_barrier((h_mate, down_sum))
+    args = (me, first, mate_first, second, mate_second)
+    total = units(*args, h, h_mate, gp, gp_mate, 0, 1)
+    down_sum = pass_on(*added(down_sum, (rest_up[1], rest_dn[1])))
+    h, total = lax.optimization_barrier((h, total))
+    total = pass_on(*total)
+    rows = input_rows(h, w, 0, width, rows)
+    h, rows, down_sum = lax.optimization_barrier((h, rows, down_sum))
+    back = exchange(rows)
+    parts = units(*args, h, h_mate, gp, gp_mate, 1, 1)
+    down_sum = pass_on(*added(down_sum, (rest_up[2], rest_dn[0])))
+    total = added(total, parts)
+    h, total = lax.optimization_barrier((h, total))
+    total = pass_on(*total)
+    parts = units(*args, h, h_mate, gp, gp_mate, 2, 2)
+    total, down_sum = lax.optimization_barrier((total, down_sum))
+    total = pass_on(*added(total, parts[:2]))
+    total, back = lax.optimization_barrier((total, back))
+    down_sum = added(down_sum, (rest_up[3], rest_dn[3]))
+    sum_up, sum_dn = added(total, parts[2:])
+
+    sums = jnp.concatenate([sum_up[:UNIT], sum_dn[:UNIT]], axis=0)
+    gate_up_grad = sums.reshape(SLICE, 2, 1, ff)
+    down_b = [t[UNIT:, k * ff : (k + 1) * ff] for t in (sum_up, sum_dn) for k in range(2)]
+    down_grad = jnp.concatenate(list(down_sum) + down_b, axis=0)[:, None, :]
     input_grad, gate_grad = unpack(hot, ids, back, width)
     return (input_grad, gate_grad.T, gate_up_grad, down_grad)
 

time: 259 us -> 255 us (0.985)
  blocking collectives: 138 us -> 82 us
  starting transfers between devices: 4.62 us -> 29.1 us
  waiting for transfers between devices: 24.4 us -> 44.8 us
  between operations: 14.1 us -> 0.89 us
  Pallas kernels: 63 us -> 71.4 us
  other arithmetic: 1.93 us -> 10.1 us
  local copies, waits for them, and re-layouts: 11.2 us -> 15.7 us
    all_to_all x2 -> x1, blocking collectives: 138 us -> 82 us  [exchange(): lax.all_to_all(rows.reshape(owners, CAP, wide), 'expert', split_axis=0, c...]
    ppermute x0 -> x12, waiting for transfers between devices: none -> 39.4 us  [pass_on(): return (lax.ppermute(up, 'dp', UP), lax.ppermute(dn, 'dp', DOWN))]
    ppermute x0 -> x12, starting transfers between devices: none -> 19.6 us  [pass_on(): return (lax.ppermute(up, 'dp', UP), lax.ppermute(dn, 'dp', DOWN))]
    reduce_scatter x2 -> x0, waiting for transfers between devices: 19.4 us -> none  [the longest x1 13.5 us: body(): grad_a = lax.psum_scatter(down_a, 'dp', scatter_dimension=0, tiled=True)]
    convert_element_type x0 -> x9, other arithmetic: none -> 9.92 us  [added(): (a.astype(F32) + b.astype(F32)).astype(BF)]
    pallas_call x2 -> x4, Pallas kernels: 18.1 us -> 26.7 us  [the longest x3 21.2 us: units(): pl.pallas_call(units_kernel, grid_spec=pltpu.PrefetchScalarGridSpec(num_s...]
    unnamed x6 -> x31, local copies, waits for them, and re-layouts: 0.81 us -> 5.92 us
    all_to_all x1 -> x2, starting transfers between devices: 3.72 us -> 8.28 us  [exchange(): lax.all_to_all(rows.reshape(owners, CAP, wide), 'expert', split_axis=0, c...]
  transfers between devices with their start and end apart: 7 -> 18, of which waited for: 5 -> 7; matrix products, arithmetic and copies ran while one was open for 3% -> 6% of each run, Pallas kernels for 22% -> 24%
where the time goes in v5:
time: 255 us; the launch traced here: 254 us
  blocking collectives  82 us (32%)
  Pallas kernels  71.4 us (28%)
  waiting for transfers between devices  44.8 us (18%)
  starting transfers between devices  29.1 us (11%)
  local copies, waits for them, and re-layouts  15.7 us (6%)
  other arithmetic  10.1 us (4%)
    all_to_all x1, blocking collectives, exchange(): lax.all_to_all(rows.reshape(owners, CAP, wide), 'expert', split_axis=0, c...  82 us
    ppermute x12, waiting for transfers between devices, pass_on(): return (lax.ppermute(up, 'dp', UP), lax.ppermute(dn, 'dp', DOWN))  39.4 us
    pallas_call x3, Pallas kernels, units(): pl.pallas_call(units_kernel, grid_spec=pltpu.PrefetchScalarGridSpec(num_s...  21.2 us
    ppermute x12, starting transfers between devices, pass_on(): return (lax.ppermute(up, 'dp', UP), lax.ppermute(dn, 'dp', DOWN))  19.6 us
    pallas_call x1, Pallas kernels, pre(): pl.pallas_call(functools.partial(pre_kernel, per=per), grid=(SLICES // pe...  15.5 us
    pallas_call x1, Pallas kernels, input_rows(): pl.pallas_call(input_kernel, grid=(cols // blk,), in_specs=[held((2, slot...  11.3 us
    convert_element_type x9, other arithmetic, added(): (a.astype(F32) + b.astype(F32)).astype(BF)  9.92 us
    all_to_all x2, starting transfers between devices, exchange(): lax.all_to_all(rows.reshape(owners, CAP, wide), 'expert', split_axis=0, c...  8.28 us
  transfers between devices with their start and end apart: 18, of which 7 were waited for; matrix products, arithmetic and copies ran while one was open for 6% of the time, Pallas kernels for 24%

profile of v5, /device:TPU:0, one launch (start us, length us, event | category | flops | bytes accessed | tf_op | source)
XLA Modules:
  0.0 254.0 jit_solution(13741610108074503027)
XLA Ops:
  0.6 6.5 %pack.1 = (bf16[512,6272]{1,0:T(8,128)(2,1)}, bf16[512,2048]{1,0:T(8,128)(2,1)}, bf16[512,128]{1,0:T(8,128)(2,1)}) custom-call(s32[2,128]{1,0:T(2,128)} %bitcast.48, bf16[2,128]{1,0:T(2,128)(2,1)} %bitcast.52, bf16[128,4096]{1,0:T(8,128)(2,1)} %tok_ref.1, bf16[128,4096]{1,0:T(8,128)(2,1)} %dy_ref.1), custom_call_target="tpu_custom_call" | custom-call | flops 3000000000 | bytes 14000000 | tf_op jit(solution)/shard_map/pack/pallas_call | solution.py:95
  7.1 82.0 %all_to_all.15 = bf16[16,32,6272]{2,1,0:T(8,128)(2,1)} all-to-all(bf16[16,32,6272]{2,1,0:T(8,128)(2,1)} %bitcast.43), channel_id=1, replica_groups=mesh['dp'=8,'expert'=16] {'expert'}, dimensions={0} | all-to-all | bytes 12845056 | tf_op jit(solution)/shard_map/all_to_all | solution.py:424
  89.0 3.7 %all-to-all-start = ((bf16[16,32,2048]{2,1,0:T(8,128)(2,1)}), bf16[16,32,2048]{2,1,0:T(8,128)(2,1)S(1)}, u32[]{:S(2)}, u32[]{:S(2)}) async-start(bf16[16,32,2048]{2,1,0:T(8,128)(2,1)} %bitcast.45), calls=%async_computation | async-start | bytes 4194304 | tf_op jit(solution)/shard_map/all_to_all | solution.py:424
  92.8 7.7 %copy.14 = bf16[4096,2,1,768]{3,0,1,2:T(8,128)(2,1)S(1)} copy(bf16[4096,2,1,768]{3,1,2,0:T(2,128)(2,1)} %param.10) | data formatting | bytes 25165824 | tf_op jit(solution)/shard_map/optimization_barrier | solution.py:432
  100.5 15.5 %pre.1 = (f32[512,768]{1,0:T(8,128)}, f32[512,768]{1,0:T(8,128)}, f32[512,768]{1,0:T(8,128)}, bf16[512,768]{1,0:T(8,128)(2,1)}, bf16[512,768]{1,0:T(8,128)(2,1)}) custom-call(bf16[512,6272]{1,0:T(8,128)(2,1)} %bitcast.6.rows_ref.dy_ref.gate_ref.own_ref.refs_0_, bf16[512,6272]{1,0:T(8,128)(2,1)} %bitcast.6.rows_ref.dy_ref.gate_ref.own_ref.refs_0_, ...), custom_call_target="tpu_custom_call" | custom-call | flops 16999999488 | bytes 40000000 | tf_op jit(solution)/shard_map/pre/pallas_call | solution.py:166
  116.0 0.6 collective-permute-start.1
  116.6 2.1 collective-permute-done.1.gp_mate_ref.refs_7_
  118.7 5.5 %down_parts.1 = (bf16[128,768]{1,0:T(8,128)(2,1)}, bf16[128,768]{1,0:T(8,128)(2,1)}, bf16[4,128,768]{2,1,0:T(8,128)(2,1)}, bf16[4,128,768]{2,1,0:T(8,128)(2,1)}) custom-call(s32[1]{0:T(128)} %bitcast.4.me_ref, bf16[512,6272]{1,0:T(8,128)(2,1)} %bitcast.6.rows_ref.dy_ref.gate_ref.own_ref.refs_0_, bf16[512,6272]{1,0:T(8,128)(2,1)} %collective-permute-done.mate_ref.refs_1_, ...), custom_call_target="tpu_custom_call" | custom-call | flops 4000000000 | bytes 12000000 | tf_op jit(solution)/shard_map/down_parts/pallas_call | solution.py:303
  124.2 3.3 %all-to-all-done = bf16[16,32,2048]{2,1,0:T(8,128)(2,1)S(1)} async-done(((bf16[16,32,2048]{2,1,0:T(8,128)(2,1)}), bf16[16,32,2048]{2,1,0:T(8,128)(2,1)S(1)}, u32[]{:S(2)}, u32[]{:S(2)}) %all-to-all-start) | async-done | bytes 2097184 | tf_op jit(solution)/shard_map/all_to_all | solution.py:424
  127.5 6.6 %hidden.1 = (bf16[2,512,768]{2,1,0:T(8,128)(2,1)}, bf16[512,4224]{1,0:T(8,128)(2,1)}) custom-call(bf16[512,2048]{1,0:T(8,128)(2,1)S(1)} %bitcast.37, bf16[8,2,256,768]{3,2,1,0:T(8,128)(2,1)} %bitcast.51, f32[512,768]{1,0:T(8,128)} %get-tuple-element.68.u_hbm, f32[512,768]{1,0:T(8,128)} %get-tuple-element.69.c1_hbm, f32[512,768]{1,0:T(8,128)} %get-tuple-element.70.c2_hbm, ...), custom_call_target="tpu_custom_call" | custom-call | flops 4000000000 | bytes 14000000 | tf_op jit(solution)/shard_map/hidden/pallas_call | solution.py:231
  134.1 0.6 collective-permute-start.3
  134.7 1.9 collective-permute-start.4
  136.6 2.2 collective-permute-start.5
  138.8 5.1 %collective-permute-done.4 = bf16[128,768]{1,0:T(8,128)(2,1)S(1)} collective-permute-done((bf16[128,768]{1,0:T(8,128)(2,1)S(1)}, bf16[128,768]{1,0:T(8,128)(2,1)S(1)}, u32[]{:S(2)}, u32[]{:S(2)}) %collective-permute-start.4) | collective-permute-done | bytes 196640 | tf_op jit(solution)/shard_map/ppermute | solution.py:405
  143.9 1.2 fusion.4
  145.1 3.1 %collective-permute-start.7 = (bf16[128,768]{1,0:T(8,128)(2,1)S(1)}, bf16[128,768]{1,0:T(8,128)(2,1)S(1)}, u32[]{:S(2)}, u32[]{:S(2)}) collective-permute-start(bf16[128,768]{1,0:T(8,128)(2,1)S(1)} %fusion.4), channel_id=1, source_target_pairs={{0,96},{16,112},{32,0},{48,16},{64,32},{80,48},{96,64},{112,80},{1... | collective-permute-start | bytes 589832 | tf_op jit(solution)/shard_map/ppermute | solution.py:405
  148.2 1.0 fusion.5
  149.2 0.3 collective-permute-start.6
  149.5 6.3 %units.3 = (bf16[320,1536]{1,0:T(8,128)(2,1)}, bf16[320,1536]{1,0:T(8,128)(2,1)}) custom-call(s32[1]{0:T(128)} %bitcast.4.me_ref, bf16[512,6272]{1,0:T(8,128)(2,1)} %bitcast.6.rows_ref.dy_ref.gate_ref.own_ref.refs_0_, bf16[512,6272]{1,0:T(8,128)(2,1)} %collective-permute-done.mate_ref.refs_1_, bf16[512,2048]{1,0:T(8,128)(2,1)S(1)} %bitcast.38, ...), custom_call_target="tpu_custom_call" | custom-call | flops 4000000000 | bytes 12000000 | tf_op jit(solution)/shard_map/units/pallas_call | solution.py:351
  155.8 0.3 collective-permute-start.8
  156.1 3.1 %collective-permute-start.9 = (bf16[320,1536]{1,0:T(8,128)(2,1)}, bf16[320,1536]{1,0:T(8,128)(2,1)}, u32[]{:S(2)}, u32[]{:S(2)}) collective-permute-start(bf16[320,1536]{1,0:T(8,128)(2,1)} %get-tuple-element.87), channel_id=1, source_target_pairs={{0,96},{16,112},{32,0},{48,16},{64,32},{80,48},{96,64},{112,80},{1... | collective-permute-start | bytes 2949128 | tf_op jit(solution)/shard_map/ppermute | solution.py:405
  159.2 11.3 %input_rows.1 = bf16[512,4224]{1,0:T(8,128)(2,1)} custom-call(bf16[2,512,768]{2,1,0:T(8,128)(2,1)} %get-tuple-element.94.refs_4_.h_ref, bf16[2,4096,768]{2,1,0:T(8,128)(2,1)} %bitcast.42, bf16[512,4224]{1,0:T(8,128)(2,1)} %get-tuple-element.79.into_ref), custom_call_target="tpu_custom_call", output_to_operand_aliasing={{}: (2, {})} | custom-call | flops 12999999488 | bytes 24000000 | tf_op jit(solution)/shard_map/input_rows/pallas_call | solution.py:262
  170.4 4.6 %all-to-all-start.2 = ((bf16[16,32,4224]{2,1,0:T(8,128)(2,1)}), bf16[16,32,4224]{2,1,0:T(8,128)(2,1)}, u32[]{:S(2)}, u32[]{:S(2)}) async-start(bf16[16,32,4224]{2,1,0:T(8,128)(2,1)} %bitcast.44), calls=%async_computation.2 | async-start | bytes 8650752 | tf_op jit(solution)/shard_map/all_to_all | solution.py:424
  175.0 1.6 copy-done.1
  176.6 1.4 copy-done.3
  178.0 5.6 %units.4 = (bf16[320,1536]{1,0:T(8,128)(2,1)}, bf16[320,1536]{1,0:T(8,128)(2,1)}) custom-call(s32[1]{0:T(128)} %bitcast.4.me_ref, bf16[512,6272]{1,0:T(8,128)(2,1)} %bitcast.6.rows_ref.dy_ref.gate_ref.own_ref.refs_0_, bf16[512,6272]{1,0:T(8,128)(2,1)} %collective-permute-done.mate_ref.refs_1_, bf16[512,2048]{1,0:T(8,128)(2,1)S(1)} %bitcast.39, ...), custom_call_target="tpu_custom_call" | custom-call | flops 4000000000 | bytes 12000000 | tf_op jit(solution)/shard_map/units/pallas_call | solution.py:351
  183.6 1.8 add_convert_fusion.5
  185.5 1.5 add_convert_fusion.4
  187.1 3.2 %collective-permute-start.11 = (bf16[320,1536]{1,0:T(8,128)(2,1)S(1)}, bf16[320,1536]{1,0:T(8,128)(2,1)S(1)}, u32[]{:S(2)}, u32[]{:S(2)}) collective-permute-start(bf16[320,1536]{1,0:T(8,128)(2,1)S(1)} %add_convert_fusion.4), channel_id=1, source_target_pairs={{0,96},{16,112},{32,0},{48,16},{64,32},{80,48},{96,64},{112,80},{1... | collective-permute-start | bytes 2949128 | tf_op jit(solution)/shard_map/ppermute | solution.py:405
  190.4 0.8 collective-permute-start.13
  191.3 1.6 collective-permute-start.12
  192.8 9.3 %units.5 = (bf16[320,1536]{1,0:T(8,128)(2,1)}, bf16[320,1536]{1,0:T(8,128)(2,1)}, bf16[320,1536]{1,0:T(8,128)(2,1)}, bf16[320,1536]{1,0:T(8,128)(2,1)}) custom-call(s32[1]{0:T(128)} %bitcast.4.me_ref, bf16[512,6272]{1,0:T(8,128)(2,1)} %bitcast.6.rows_ref.dy_ref.gate_ref.own_ref.refs_0_, bf16[512,6272]{1,0:T(8,128)(2,1)} %collective-permute-done.mate_ref.refs_1_, ...), custom_call_target="tpu_custom_call" | custom-call | flops 4000000000 | bytes 12000000 | tf_op jit(solution)/shard_map/units/pallas_call | solution.py:351
  202.1 11.8 %collective-permute-done.13 = bf16[128,768]{1,0:T(8,128)(2,1)S(1)} collective-permute-done((bf16[128,768]{1,0:T(8,128)(2,1)S(1)}, bf16[128,768]{1,0:T(8,128)(2,1)S(1)}, u32[]{:S(2)}, u32[]{:S(2)}) %collective-permute-start.13) | collective-permute-done | bytes 196640 | tf_op jit(solution)/shard_map/ppermute | solution.py:405
  213.9 0.7 collective-permute-done.12
  214.6 1.4 add_convert_fusion.2
  216.1 3.0 %collective-permute-start.15 = (bf16[320,1536]{1,0:T(8,128)(2,1)S(1)}, bf16[320,1536]{1,0:T(8,128)(2,1)S(1)}, u32[]{:S(2)}, u32[]{:S(2)}) collective-permute-start(bf16[320,1536]{1,0:T(8,128)(2,1)S(1)} %add_convert_fusion.2), channel_id=1, source_target_pairs={{0,96},{16,112},{32,0},{48,16},{64,32},{80,48},{96,64},{112,80},{1... | collective-permute-start | bytes 2949128 | tf_op jit(solution)/shard_map/ppermute | solution.py:405
  219.1 0.2 add_convert_fusion.3
  219.6 18.1 %collective-permute-done.15 = bf16[320,1536]{1,0:T(8,128)(2,1)S(1)} collective-permute-done((bf16[320,1536]{1,0:T(8,128)(2,1)S(1)}, bf16[320,1536]{1,0:T(8,128)(2,1)S(1)}, u32[]{:S(2)}, u32[]{:S(2)}) %collective-permute-start.15) | collective-permute-done | bytes 983072 | tf_op jit(solution)/shard_map/ppermute | solution.py:405
  237.6 3.7 %collective-permute-done.14 = bf16[320,1536]{1,0:T(8,128)(2,1)S(1)} collective-permute-done((bf16[320,1536]{1,0:T(8,128)(2,1)S(1)}, bf16[320,1536]{1,0:T(8,128)(2,1)S(1)}, u32[]{:S(2)}, u32[]{:S(2)}) %collective-permute-start.14) | collective-permute-done | bytes 983072 | tf_op jit(solution)/shard_map/ppermute | solution.py:405
  241.4 0.9 copy-done.7
  242.3 2.6 %add_convert_fusion = (bf16[320,1536]{1,0:T(8,128)(2,1)S(1)}, bf16[320,1536]{1,0:T(8,128)(2,1)S(1)}) fusion(bf16[320,1536]{1,0:T(8,128)(2,1)} %get-tuple-element.105, bf16[320,1536]{1,0:T(8,128)(2,1)} %copy-done.6, bf16[320,1536]{1,0:T(8,128)(2,1)} %get-tuple-element.103, bf16[320,1536]{1,0:T(8,128)(2,1)} %copy-done.7), kind=kLoop, calls=%fused_computation.1 | loop fusion | flops 3932160 | bytes 5898240 | tf_op jit(solution)/shard_map/convert_element_type | solution.py:409
  244.9 0.7 slice_dynamic-update-slice_fusion.3
  245.6 0.6 slice_dynamic-update-slice_fusion.2
  246.3 0.7 slice_dynamic-update-slice_fusion.1
  247.0 0.6 slice_dynamic-update-slice_fusion
  247.6 0.1 pad_maximum_fusion
  247.7 1.3 reshape.55
  249.0 4.9 %unpack.1 = (bf16[128,4096]{1,0:T(8,128)(2,1)}, bf16[2,128]{1,0:T(2,128)(2,1)}) custom-call(bf16[512,128]{1,0:T(8,128)(2,1)} %get-tuple-element.56.hot_ref, bf16[512,4224]{1,0:T(8,128)(2,1)} %bitcast.16.rows_ref.gates_ref, s32[2,128]{1,0:T(2,128)} %bitcast.49, bf16[512,4224]{1,0:T(8,128)(2,1)} %bitcast.16.rows_ref.gates_ref), custom_call_target="tpu_custom_call" | custom-call | flops 1000000000 | bytes 10000000 | tf_op jit(solution)/shard_map/unpack/pallas_call | solution.py:382
  (46 shorter events, 0.5 us)
Async XLA Ops:
  89.0 29.7 %collective-permute-start = (bf16[512,6272]{1,0:T(8,128)(2,1)}, bf16[512,6272]{1,0:T(8,128)(2,1)}, u32[]{:S(2)}, u32[]{:S(2)}) collective-permute-start(bf16[512,6272]{1,0:T(8,128)(2,1)} %bitcast.6.rows_ref.dy_ref.gate_ref.own_ref.refs_0_), channel_id=1, source_target_pairs={{0,16},{16,0},{32,48},{48,32},{64,80},{80,64},{96,112},{112,96},{1... | collective-permute-start | bytes 19267592 | tf_op jit(solution)/shard_map/ppermute | solution.py:428
  89.0 38.4 %all-to-all-start = ((bf16[16,32,2048]{2,1,0:T(8,128)(2,1)}), bf16[16,32,2048]{2,1,0:T(8,128)(2,1)S(1)}, u32[]{:S(2)}, u32[]{:S(2)}) async-start(bf16[16,32,2048]{2,1,0:T(8,128)(2,1)} %bitcast.45), calls=%async_computation | async-start | bytes 4194304 | tf_op jit(solution)/shard_map/all_to_all | solution.py:424
  100.5 15.5 %copy-start.4 = (bf16[4096,2,1,768]{3,0,1,2:T(8,128)(2,1)}, bf16[4096,2,1,768]{3,0,1,2:T(8,128)(2,1)S(1)}, u32[]{:S(2)}) copy-start(bf16[4096,2,1,768]{3,0,1,2:T(8,128)(2,1)S(1)} %copy.14) | copy-start | bytes 37748740
  116.0 2.7 %collective-permute-start.1 = (bf16[512,768]{1,0:T(8,128)(2,1)}, bf16[512,768]{1,0:T(8,128)(2,1)S(1)}, u32[]{:S(2)}, u32[]{:S(2)}) collective-permute-start(bf16[512,768]{1,0:T(8,128)(2,1)} %get-tuple-element.64.gp_ref.refs_6_), channel_id=1, source_target_pairs={{0,16},{16,0},{32,48},{48,32},{64,80},{80,64},{96,112},{112,96},{1... | collective-permute-start | bytes 2359304 | tf_op jit(solution)/shard_map/ppermute | solution.py:428
  127.5 22.0 %collective-permute-start.2 = (bf16[512,2048]{1,0:T(8,128)(2,1)S(1)}, bf16[512,2048]{1,0:T(8,128)(2,1)S(1)}, u32[]{:S(2)}, u32[]{:S(2)}) collective-permute-start(bf16[512,2048]{1,0:T(8,128)(2,1)S(1)} %bitcast.36), channel_id=1, source_target_pairs={{0,16},{16,0},{32,48},{48,32},{64,80},{80,64},{96,112},{112,96},{1... | collective-permute-start | bytes 6291464 | tf_op jit(solution)/shard_map/ppermute | solution.py:428
  127.5 7.2 %copy-start.13 = (bf16[128,768]{1,0:T(8,128)(2,1)S(1)}, bf16[128,768]{1,0:T(8,128)(2,1)}, u32[]{:S(2)}) copy-start(bf16[128,768]{1,0:T(8,128)(2,1)} %get-tuple-element.73) | copy-start | bytes 589828
  127.5 9.1 %copy-start.12 = (bf16[128,768]{1,0:T(8,128)(2,1)S(1)}, bf16[128,768]{1,0:T(8,128)(2,1)}, u32[]{:S(2)}) copy-start(bf16[128,768]{1,0:T(8,128)(2,1)} %get-tuple-element.74) | copy-start | bytes 589828
  134.1 9.8 %collective-permute-start.3 = (bf16[2,512,768]{2,1,0:T(8,128)(2,1)}, bf16[2,512,768]{2,1,0:T(8,128)(2,1)S(1)}, u32[]{:S(2)}, u32[]{:S(2)}) collective-permute-start(bf16[2,512,768]{2,1,0:T(8,128)(2,1)} %get-tuple-element.94.refs_4_.h_ref), channel_id=1, source_target_pairs={{0,16},{16,0},{32,48},{48,32},{64,80},{80,64},{96,112},{112,96},{1... | collective-permute-start | bytes 4718600 | tf_op jit(solution)/shard_map/ppermute | solution.py:428
  134.7 9.2 %collective-permute-start.4 = (bf16[128,768]{1,0:T(8,128)(2,1)S(1)}, bf16[128,768]{1,0:T(8,128)(2,1)S(1)}, u32[]{:S(2)}, u32[]{:S(2)}) collective-permute-start(bf16[128,768]{1,0:T(8,128)(2,1)S(1)} %copy-done.13), channel_id=1, source_target_pairs={{0,32},{16,48},{32,64},{48,80},{64,96},{80,112},{96,0},{112,16},{1... | collective-permute-start | bytes 589832 | tf_op jit(solution)/shard_map/ppermute | solution.py:405
  136.6 7.3 %collective-permute-start.5 = (bf16[128,768]{1,0:T(8,128)(2,1)S(1)}, bf16[128,768]{1,0:T(8,128)(2,1)S(1)}, u32[]{:S(2)}, u32[]{:S(2)}) collective-permute-start(bf16[128,768]{1,0:T(8,128)(2,1)S(1)} %copy-done.12), channel_id=1, source_target_pairs={{0,96},{16,112},{32,0},{48,16},{64,32},{80,48},{96,64},{112,80},{1... | collective-permute-start | bytes 589832 | tf_op jit(solution)/shard_map/ppermute | solution.py:405
  143.9 11.9 %copy-start.2 = (bf16[2,512,768]{2,1,0:T(8,128)(2,1)}, bf16[2,512,768]{2,1,0:T(8,128)(2,1)S(1)}, u32[]{:S(2)}) copy-start(bf16[2,512,768]{2,1,0:T(8,128)(2,1)S(1)} %collective-permute-done.3.refs_5_) | copy-start | bytes 4718596
  145.1 25.3 %collective-permute-start.7 = (bf16[128,768]{1,0:T(8,128)(2,1)S(1)}, bf16[128,768]{1,0:T(8,128)(2,1)S(1)}, u32[]{:S(2)}, u32[]{:S(2)}) collective-permute-start(bf16[128,768]{1,0:T(8,128)(2,1)S(1)} %fusion.4), channel_id=1, source_target_pairs={{0,96},{16,112},{32,0},{48,16},{64,32},{80,48},{96,64},{112,80},{1... | collective-permute-start | bytes 589832 | tf_op jit(solution)/shard_map/ppermute | solution.py:405
  149.2 21.3 %collective-permute-start.6 = (bf16[128,768]{1,0:T(8,128)(2,1)S(1)}, bf16[128,768]{1,0:T(8,128)(2,1)S(1)}, u32[]{:S(2)}, u32[]{:S(2)}) collective-permute-start(bf16[128,768]{1,0:T(8,128)(2,1)S(1)} %fusion.5), channel_id=1, source_target_pairs={{0,32},{16,48},{32,64},{48,80},{64,96},{80,112},{96,0},{112,16},{1... | collective-permute-start | bytes 589832 | tf_op jit(solution)/shard_map/ppermute | solution.py:405
  149.5 6.3 %copy-start = (bf16[512,2048]{1,0:T(8,128)(2,1)}, bf16[512,2048]{1,0:T(8,128)(2,1)S(1)}, u32[]{:S(2)}) copy-start(bf16[512,2048]{1,0:T(8,128)(2,1)S(1)} %collective-permute-done.2.refs_3_) | copy-start | bytes 6291460
  155.8 27.8 %collective-permute-start.8 = (bf16[320,1536]{1,0:T(8,128)(2,1)}, bf16[320,1536]{1,0:T(8,128)(2,1)}, u32[]{:S(2)}, u32[]{:S(2)}) collective-permute-start(bf16[320,1536]{1,0:T(8,128)(2,1)} %get-tuple-element.85), channel_id=1, source_target_pairs={{0,32},{16,48},{32,64},{48,80},{64,96},{80,112},{96,0},{112,16},{1... | collective-permute-start | bytes 2949128 | tf_op jit(solution)/shard_map/ppermute | solution.py:405
  156.1 29.4 %collective-permute-start.9 = (bf16[320,1536]{1,0:T(8,128)(2,1)}, bf16[320,1536]{1,0:T(8,128)(2,1)}, u32[]{:S(2)}, u32[]{:S(2)}) collective-permute-start(bf16[320,1536]{1,0:T(8,128)(2,1)} %get-tuple-element.87), channel_id=1, source_target_pairs={{0,96},{16,112},{32,0},{48,16},{64,32},{80,48},{96,64},{112,80},{1... | collective-permute-start | bytes 2949128 | tf_op jit(solution)/shard_map/ppermute | solution.py:405
  170.4 70.9 %all-to-all-start.2 = ((bf16[16,32,4224]{2,1,0:T(8,128)(2,1)}), bf16[16,32,4224]{2,1,0:T(8,128)(2,1)}, u32[]{:S(2)}, u32[]{:S(2)}) async-start(bf16[16,32,4224]{2,1,0:T(8,128)(2,1)} %bitcast.44), calls=%async_computation.2 | async-start | bytes 8650752 | tf_op jit(solution)/shard_map/all_to_all | solution.py:424
  175.0 1.6 copy-start.1
  176.6 1.4 copy-start.3
  183.6 1.9 copy-start.8
  185.4 4.9 %copy-start.9 = (bf16[4,128,768]{2,1,0:T(8,128)(2,1)S(1)}, bf16[4,128,768]{2,1,0:T(8,128)(2,1)}, u32[]{:S(2)}) copy-start(bf16[4,128,768]{2,1,0:T(8,128)(2,1)} %get-tuple-element.83) | copy-start | bytes 2359300
  185.5 5.7 %copy-start.10 = (bf16[4,128,768]{2,1,0:T(8,128)(2,1)S(1)}, bf16[4,128,768]{2,1,0:T(8,128)(2,1)}, u32[]{:S(2)}) copy-start(bf16[4,128,768]{2,1,0:T(8,128)(2,1)} %get-tuple-element.81) | copy-start | bytes 2359300
  187.0 27.6 %collective-permute-start.10 = (bf16[320,1536]{1,0:T(8,128)(2,1)S(1)}, bf16[320,1536]{1,0:T(8,128)(2,1)S(1)}, u32[]{:S(2)}, u32[]{:S(2)}) collective-permute-start(bf16[320,1536]{1,0:T(8,128)(2,1)S(1)} %add_convert_fusion.5), channel_id=1, source_target_pairs={{0,32},{16,48},{32,64},{48,80},{64,96},{80,112},{96,0},{112,16},{1... | collective-permute-start | bytes 2949128 | tf_op jit(solution)/shard_map/ppermute | solution.py:405
  187.1 27.5 %collective-permute-start.11 = (bf16[320,1536]{1,0:T(8,128)(2,1)S(1)}, bf16[320,1536]{1,0:T(8,128)(2,1)S(1)}, u32[]{:S(2)}, u32[]{:S(2)}) collective-permute-start(bf16[320,1536]{1,0:T(8,128)(2,1)S(1)} %add_convert_fusion.4), channel_id=1, source_target_pairs={{0,96},{16,112},{32,0},{48,16},{64,32},{80,48},{96,64},{112,80},{1... | collective-permute-start | bytes 2949128 | tf_op jit(solution)/shard_map/ppermute | solution.py:405
  190.4 23.5 %collective-permute-start.13 = (bf16[128,768]{1,0:T(8,128)(2,1)S(1)}, bf16[128,768]{1,0:T(8,128)(2,1)S(1)}, u32[]{:S(2)}, u32[]{:S(2)}) collective-permute-start(bf16[128,768]{1,0:T(8,128)(2,1)S(1)} %fusion.2), channel_id=1, source_target_pairs={{0,96},{16,112},{32,0},{48,16},{64,32},{80,48},{96,64},{112,80},{1... | collective-permute-start | bytes 589832 | tf_op jit(solution)/shard_map/ppermute | solution.py:405
  191.3 23.4 %collective-permute-start.12 = (bf16[128,768]{1,0:T(8,128)(2,1)S(1)}, bf16[128,768]{1,0:T(8,128)(2,1)S(1)}, u32[]{:S(2)}, u32[]{:S(2)}) collective-permute-start(bf16[128,768]{1,0:T(8,128)(2,1)S(1)} %fusion.3), channel_id=1, source_target_pairs={{0,32},{16,48},{32,64},{48,80},{64,96},{80,112},{96,0},{112,16},{1... | collective-permute-start | bytes 589832 | tf_op jit(solution)/shard_map/ppermute | solution.py:405
  202.1 17.0 %copy-start.5 = (bf16[320,1536]{1,0:T(8,128)(2,1)S(1)}, bf16[320,1536]{1,0:T(8,128)(2,1)}, u32[]{:S(2)}) copy-start(bf16[320,1536]{1,0:T(8,128)(2,1)} %get-tuple-element.95) | copy-start | bytes 2949124
  216.1 21.5 %collective-permute-start.15 = (bf16[320,1536]{1,0:T(8,128)(2,1)S(1)}, bf16[320,1536]{1,0:T(8,128)(2,1)S(1)}, u32[]{:S(2)}, u32[]{:S(2)}) collective-permute-start(bf16[320,1536]{1,0:T(8,128)(2,1)S(1)} %add_convert_fusion.2), channel_id=1, source_target_pairs={{0,96},{16,112},{32,0},{48,16},{64,32},{80,48},{96,64},{112,80},{1... | collective-permute-start | bytes 2949128 | tf_op jit(solution)/shard_map/ppermute | solution.py:405
  219.4 22.0 %collective-permute-start.14 = (bf16[320,1536]{1,0:T(8,128)(2,1)S(1)}, bf16[320,1536]{1,0:T(8,128)(2,1)S(1)}, u32[]{:S(2)}, u32[]{:S(2)}) collective-permute-start(bf16[320,1536]{1,0:T(8,128)(2,1)S(1)} %add_convert_fusion.3), channel_id=1, source_target_pairs={{0,32},{16,48},{32,64},{48,80},{64,96},{80,112},{96,0},{112,16},{1... | collective-permute-start | bytes 2949128 | tf_op jit(solution)/shard_map/ppermute | solution.py:405
  219.6 25.3 %copy-start.11 = (bf16[512,768]{1,0:T(8,128)(2,1)}, bf16[512,768]{1,0:T(8,128)(2,1)S(1)}, u32[]{:S(2)}) copy-start(bf16[512,768]{1,0:T(8,128)(2,1)S(1)} %fusion.7) | copy-start | bytes 2359300
  237.6 3.7 %copy-start.6 = (bf16[320,1536]{1,0:T(8,128)(2,1)}, bf16[320,1536]{1,0:T(8,128)(2,1)S(1)}, u32[]{:S(2)}) copy-start(bf16[320,1536]{1,0:T(8,128)(2,1)S(1)} %collective-permute-done.15) | copy-start | bytes 2949124
  241.3 0.9 copy-start.7

commit v6 on v5

--- a/solution.py
+++ b/solution.py
@@ -276,48 +276,8 @@
     return jnp.where(up, me // 2 + 3 - hop, me // 2 + 1 + hop) % 4
 
 
-def down_kernel(me_ref, own_ref, mate_ref, gp_ref, gp_mate_ref, up_ref, dn_ref, up_rest_ref, dn_rest_ref):
-    del me_ref
-    step = pl.program_id(0)
-    part = (dot_tn(own_ref[...], gp_ref[...]) + dot_tn(mate_ref[...], gp_mate_ref[...])).astype(BF)
-    half = PART_A // 2
-
-    @pl.when(step == 0)
-    def _():
-        up_ref[...] = part[:half]
-
-    @pl.when(step == 2)
-    def _():
-        dn_ref[...] = part[half:]
-
-    up_rest_ref[0] = part[:half]
-    dn_rest_ref[0] = part[half:]
-
-
-def down_parts(me, own, mate, gp, gp_mate):
-    slots, ff = gp.shape
-    rows = pl.BlockSpec(
-        (slots, PART_A), lambda i, me: (0, GRADS // PART_A + 2 * chip_at(me[0], i, True) + me[0] % 2)
-    )
-    half = PART_A // 2
-    return pl.pallas_call(
-        down_kernel,
-        grid_spec=pltpu.PrefetchScalarGridSpec(
-            num_scalar_prefetch=1,
-            grid=(4,),
-            in_specs=[rows, rows, held((slots, ff)), held((slots, ff))],
-            out_specs=[pl.BlockSpec((half, ff), lambda i, me: (0, 0))] * 2
-            + [pl.BlockSpec((1, half, ff), lambda i, me: (i, 0, 0))] * 2,
-        ),
-        out_shape=[pltpu.HBM((half, ff), BF)] * 2 + [pltpu.HBM((4, half, ff), BF)] * 2,
-        compiler_params=params(16),
-        name="down_parts",
-        cost_estimate=pl.CostEstimate(flops=4000000000, transcendentals=0, bytes_accessed=12000000),
-    )(me, in_hbm(own), in_hbm(mate), in_hbm(gp), gp_mate)
-
-
 UNIT = SLICE // 2
-EXTRA = PART_B // 4
+EXTRA = UNIT // 2
 
 
 def unit_part(own_ref, mate_ref, dy_ref, dy_mate_ref, h_ref, h_mate_ref, gp_ref, gp_mate_ref, out_ref):
@@ -334,33 +294,47 @@
 
 def units_kernel(me_ref, *refs):
     del me_ref
-    ins, outs = refs[:8], refs[8:]
+    own, mate, dy_a, dy_a_mate, dy_b, dy_b_mate = refs[:6]
+    hid, outs = refs[6:10], refs[10:]
     for k, out in enumerate(outs):
 
         @pl.when(pl.program_id(0) == k)
         def _():
-            unit_part(*ins, out)
+            dy = (dy_a, dy_a_mate) if k % 2 == 0 else (dy_b, dy_b_mate)
+            unit_part(own, mate, *dy, *hid, out)
 
 
 def units(me, first, mate_first, second, mate_second, h, h_mate, gp, gp_mate, hop, hops):
     _, slots, ff = h.shape
-    at = lambda i, me: 2 * (2 * chip_at(me[0], hop + i // 2, i % 2 == 0) + me[0] % 2) + i % 2
-    rows = pl.BlockSpec((slots, UNIT), lambda i, me: (0, at(i, me)))
-    grads = pl.BlockSpec((slots, PART_B // 2), lambda i, me: (0, at(i, me)))
+    at = lambda i, me: 2 * chip_at(me[0], hop + i // 2, i % 2 == 0) + me[0] % 2
+    rows = pl.BlockSpec((slots, UNIT), lambda i, me: (0, 2 * at(i, me) + i % 2))
+    grads_a = pl.BlockSpec((slots, PART_A), lambda i, me: (0, GRADS // PART_A + at(i - i % 2, me)))
+    grads_b = pl.BlockSpec((slots, PART_B), lambda i, me: (0, at(i - i % 2 + 1, me)))
     shape = (UNIT + EXTRA, 2 * ff)
+    free = (lambda x: x) if hop == 0 else in_hbm
     return pl.pallas_call(
         units_kernel,
         grid_spec=pltpu.PrefetchScalarGridSpec(
             num_scalar_prefetch=1,
             grid=(2 * hops,),
-            in_specs=[rows, rows, grads, grads] + [held((2, slots, ff))] * 2 + [held((slots, ff))] * 2,
+            in_specs=[rows, rows, grads_a, grads_a, grads_b, grads_b]
+            + [held((2, slots, ff))] * 2
+            + [held((slots, ff))] * 2,
             out_specs=[pl.BlockSpec(shape, lambda i, me: (0, 0))] * (2 * hops),
         ),
         out_shape=[pltpu.HBM(shape, BF)] * (2 * hops),
-        compiler_params=params(28),
+        compiler_params=params(30),
         name="units",
         cost_estimate=pl.CostEstimate(flops=4000000000, transcendentals=0, bytes_accessed=12000000),
-    )(me, in_hbm(first), in_hbm(mate_first), second, mate_second, in_hbm(h), h_mate, in_hbm(gp), gp_mate)
+    )(
+        me,
+        *map(in_hbm, (first, mate_first, first, mate_first)),
+        *map(free, (second, mate_second)),
+        in_hbm(h),
+        free(h_mate),
+        in_hbm(gp),
+        free(gp_mate),
+    )
 
 
 def unpack_kernel(hot_ref, rows_ref, ids_ref, gates_ref, out_ref, gate_ref):
@@ -436,38 +410,33 @@
     wd = down_proj.reshape(SLICES, 2, PART_A, ff)
     u_a, c1, c2, p, gp = pre(first, w, wd)
     gp_mate = swap(gp)
-    down_up, down_dn, rest_up, rest_dn = down_parts(me, first, mate_first, gp, gp_mate)
-    down_sum = pass_on(down_up, down_dn)
-    second, rest_up, rest_dn = lax.optimization_barrier((second, rest_up, rest_dn))
+    second, gp_mate = lax.optimization_barrier((second, gp_mate))
     mate_second = swap(second)
     h, rows = hidden(second, wd, u_a, c1, c2, p, width)
     h_mate = swap(h)
-    h_mate, down_sum = lax.optimization_barrier((h_mate, down_sum))
     args = (me, first, mate_first, second, mate_second)
     total = units(*args, h, h_mate, gp, gp_mate, 0, 1)
-    down_sum = pass_on(*added(down_sum, (rest_up[1], rest_dn[1])))
     h, total = lax.optimization_barrier((h, total))
     total = pass_on(*total)
+    parts = units(*args, h, h_mate, gp, gp_mate, 1, 1)
+    h, parts = lax.optimization_barrier((h, parts))
     rows = input_rows(h, w, 0, width, rows)
-    h, rows, down_sum = lax.optimization_barrier((h, rows, down_sum))
+    h, rows = lax.optimization_barrier((h, rows))
     back = exchange(rows)
-    parts = units(*args, h, h_mate, gp, gp_mate, 1, 1)
-    down_sum = pass_on(*added(down_sum, (rest_up[2], rest_dn[0])))
+    total, rows = lax.optimization_barrier((total, rows))
     total = added(total, parts)
     h, total = lax.optimization_barrier((h, total))
     total = pass_on(*total)
     parts = units(*args, h, h_mate, gp, gp_mate, 2, 2)
-    total, down_sum = lax.optimization_barrier((total, down_sum))
     total = pass_on(*added(total, parts[:2]))
-    total, back = lax.optimization_barrier((total, back))
-    down_sum = added(down_sum, (rest_up[3], rest_dn[3]))
+    input_grad, gate_grad = unpack(hot, ids, back, width)
+    total, input_grad = lax.optimization_barrier((total, input_grad))
     sum_up, sum_dn = added(total, parts[2:])
 
     sums = jnp.concatenate([sum_up[:UNIT], sum_dn[:UNIT]], axis=0)
     gate_up_grad = sums.reshape(SLICE, 2, 1, ff)
-    down_b = [t[UNIT:, k * ff : (k + 1) * ff] for t in (sum_up, sum_dn) for k in range(2)]
-    down_grad = jnp.concatenate(list(down_sum) + down_b, axis=0)[:, None, :]
-    input_grad, gate_grad = unpack(hot, ids, back, width)
+    down = [t[UNIT:, k * ff : (k + 1) * ff] for t in (sum_up, sum_dn) for k in range(2)]
+    down_grad = jnp.concatenate(down, axis=0)[:, None, :]
     return (input_grad, gate_grad.T, gate_up_grad, down_grad)
 
 

time: 255 us -> 251 us (0.984)
  waiting for transfers between devices: 44.8 us -> 56.8 us
  starting transfers between devices: 29.1 us -> 20.1 us
  local copies, waits for them, and re-layouts: 15.7 us -> 11.9 us
  other arithmetic: 10.1 us -> 6.45 us
    all_to_all x2, waiting for transfers between devices: 3.31 us -> 36.4 us  [exchange(): lax.all_to_all(rows.reshape(owners, CAP, wide), 'expert', split_axis=0, c...]
    ppermute x12 -> x6, waiting for transfers between devices: 39.4 us -> 16.8 us  [pass_on(): return (lax.ppermute(up, 'dp', UP), lax.ppermute(dn, 'dp', DOWN))]
    ppermute x12 -> x6, starting transfers between devices: 19.6 us -> 11 us  [pass_on(): return (lax.ppermute(up, 'dp', UP), lax.ppermute(dn, 'dp', DOWN))]
    pallas_call x1 -> x0, Pallas kernels: 5.49 us -> none  [down_parts(): pl.pallas_call(down_kernel, grid_spec=pltpu.PrefetchScalarGridSpec(num_sc...]
    pallas_call x3, Pallas kernels: 21.2 us -> 26.5 us  [units(): pl.pallas_call(units_kernel, grid_spec=pltpu.PrefetchScalarGridSpec(num_s...]
    convert_element_type x9 -> x5, other arithmetic: 9.92 us -> 5.42 us  [added(): (a.astype(F32) + b.astype(F32)).astype(BF)]
    unnamed x31 -> x20, local copies, waits for them, and re-layouts: 5.92 us -> 1.69 us
  transfers between devices with their start and end apart: 18 -> 12, of which waited for: 7 -> 5; matrix products, arithmetic and copies ran while one was open for 6% -> 5% of each run, Pallas kernels for 24% -> 23%
where the time goes in v6:
time: 251 us; the launch traced here: 250 us
  blocking collectives  82 us (33%)
  Pallas kernels  72.2 us (29%)
  waiting for transfers between devices  56.8 us (23%)
  starting transfers between devices  20.1 us (8%)
  local copies, waits for them, and re-layouts  11.9 us (5%)
  other arithmetic  6.45 us (3%)
    all_to_all x1, blocking collectives, exchange(): lax.all_to_all(rows.reshape(owners, CAP, wide), 'expert', split_axis=0, c...  82 us
    all_to_all x2, waiting for transfers between devices, exchange(): lax.all_to_all(rows.reshape(owners, CAP, wide), 'expert', split_axis=0, c...  36.4 us
    pallas_call x3, Pallas kernels, units(): pl.pallas_call(units_kernel, grid_spec=pltpu.PrefetchScalarGridSpec(num_s...  26.5 us
    ppermute x6, waiting for transfers between devices, pass_on(): return (lax.ppermute(up, 'dp', UP), lax.ppermute(dn, 'dp', DOWN))  16.8 us
    pallas_call x1, Pallas kernels, pre(): pl.pallas_call(functools.partial(pre_kernel, per=per), grid=(SLICES // pe...  15.5 us
    pallas_call x1, Pallas kernels, input_rows(): pl.pallas_call(input_kernel, grid=(cols // blk,), in_specs=[held((2, slot...  11.3 us
    ppermute x6, starting transfers between devices, pass_on(): return (lax.ppermute(up, 'dp', UP), lax.ppermute(dn, 'dp', DOWN))  11 us
    all_to_all x2, starting transfers between devices, exchange(): lax.all_to_all(rows.reshape(owners, CAP, wide), 'expert', split_axis=0, c...  8.39 us
  transfers between devices with their start and end apart: 12, of which 5 were waited for; matrix products, arithmetic and copies ran while one was open for 5% of the time, Pallas kernels for 23%

profile of v6, /device:TPU:0, one launch (start us, length us, event | category | flops | bytes accessed | tf_op | source)
XLA Modules:
  0.0 250.3 jit_solution(8185971885502546885)
XLA Ops:
  0.6 6.5 %pack.1 = (bf16[512,6272]{1,0:T(8,128)(2,1)}, bf16[512,2048]{1,0:T(8,128)(2,1)}, bf16[512,128]{1,0:T(8,128)(2,1)}) custom-call(s32[2,128]{1,0:T(2,128)} %bitcast.30, bf16[2,128]{1,0:T(2,128)(2,1)} %bitcast.34, bf16[128,4096]{1,0:T(8,128)(2,1)} %tok_ref.1, bf16[128,4096]{1,0:T(8,128)(2,1)} %dy_ref.1), custom_call_target="tpu_custom_call" | custom-call | flops 3000000000 | bytes 14000000 | tf_op jit(solution)/shard_map/pack/pallas_call | solution.py:95
  7.2 82.0 %all_to_all.15 = bf16[16,32,6272]{2,1,0:T(8,128)(2,1)} all-to-all(bf16[16,32,6272]{2,1,0:T(8,128)(2,1)} %bitcast.26), channel_id=1, replica_groups=mesh['dp'=8,'expert'=16] {'expert'}, dimensions={0} | all-to-all | bytes 12845056 | tf_op jit(solution)/shard_map/all_to_all | solution.py:398
  89.1 0.0 collective-permute-start.1
  89.1 3.7 %all-to-all-start = ((bf16[16,32,2048]{2,1,0:T(8,128)(2,1)}), bf16[16,32,2048]{2,1,0:T(8,128)(2,1)S(1)}, u32[]{:S(2)}, u32[]{:S(2)}) async-start(bf16[16,32,2048]{2,1,0:T(8,128)(2,1)} %bitcast.28), calls=%async_computation | async-start | bytes 4194304 | tf_op jit(solution)/shard_map/all_to_all | solution.py:398
  92.9 7.7 %copy.14 = bf16[4096,2,1,768]{3,0,1,2:T(8,128)(2,1)S(1)} copy(bf16[4096,2,1,768]{3,1,2,0:T(2,128)(2,1)} %param.10) | data formatting | bytes 25165824 | tf_op jit(solution)/shard_map/optimization_barrier | solution.py:406
  100.6 15.5 %pre.1 = (f32[512,768]{1,0:T(8,128)}, f32[512,768]{1,0:T(8,128)}, f32[512,768]{1,0:T(8,128)}, bf16[512,768]{1,0:T(8,128)(2,1)}, bf16[512,768]{1,0:T(8,128)(2,1)}) custom-call(bf16[512,6272]{1,0:T(8,128)(2,1)} %bitcast.6.rows_ref.dy_ref.gate_ref.refs_0_.refs_2_, bf16[512,6272]{1,0:T(8,128)(2,1)} %bitcast.6.rows_ref.dy_ref.gate_ref.refs_0_.refs_2_, ...), custom_call_target="tpu_custom_call" | custom-call | flops 16999999488 | bytes 40000000 | tf_op jit(solution)/shard_map/pre/pallas_call | solution.py:166
  116.1 0.6 collective-permute-start
  116.7 10.9 %all-to-all-done = bf16[16,32,2048]{2,1,0:T(8,128)(2,1)S(1)} async-done(((bf16[16,32,2048]{2,1,0:T(8,128)(2,1)}), bf16[16,32,2048]{2,1,0:T(8,128)(2,1)S(1)}, u32[]{:S(2)}, u32[]{:S(2)}) %all-to-all-start) | async-done | bytes 2097184 | tf_op jit(solution)/shard_map/all_to_all | solution.py:398
  127.6 0.0 collective-permute-done.refs_9_
  127.6 0.1 collective-permute-start.2
  127.7 7.3 %hidden.1 = (bf16[2,512,768]{2,1,0:T(8,128)(2,1)}, bf16[512,4224]{1,0:T(8,128)(2,1)}) custom-call(bf16[512,2048]{1,0:T(8,128)(2,1)S(1)} %bitcast.20, bf16[8,2,256,768]{3,2,1,0:T(8,128)(2,1)} %bitcast.33, f32[512,768]{1,0:T(8,128)} %get-tuple-element.55.u_hbm, f32[512,768]{1,0:T(8,128)} %get-tuple-element.56.c1_hbm, f32[512,768]{1,0:T(8,128)} %get-tuple-element.57.c2_hbm, ...), custom_call_target="tpu_custom_call" | custom-call | flops 4000000000 | bytes 14000000 | tf_op jit(solution)/shard_map/hidden/pallas_call | solution.py:231
  135.0 0.1 collective-permute-start.3
  135.1 3.6 %collective-permute-done.3.refs_7_ = bf16[2,512,768]{2,1,0:T(8,128)(2,1)S(1)} collective-permute-done((bf16[2,512,768]{2,1,0:T(8,128)(2,1)}, bf16[2,512,768]{2,1,0:T(8,128)(2,1)S(1)}, u32[]{:S(2)}, u32[]{:S(2)}) %collective-permute-start.3) | collective-permute-done | bytes 1572896 | tf_op jit(solution)/shard_map/ppermute | solution.py:402
  138.7 0.0 collective-permute-done.2.refs_5_
  138.7 0.0 collective-permute-done.1.refs_1_.refs_3_
  138.7 0.0 copy-done
  138.7 7.7 %units.3 = (bf16[384,1536]{1,0:T(8,128)(2,1)}, bf16[384,1536]{1,0:T(8,128)(2,1)}) custom-call(s32[1]{0:T(128)} %bitcast.4.me_ref, bf16[512,6272]{1,0:T(8,128)(2,1)} %bitcast.6.rows_ref.dy_ref.gate_ref.refs_0_.refs_2_, bf16[512,6272]{1,0:T(8,128)(2,1)} %collective-permute-done.1.refs_1_.refs_3_, ...), custom_call_target="tpu_custom_call" | custom-call | flops 4000000000 | bytes 12000000 | tf_op jit(solution)/shard_map/units/pallas_call | solution.py:315
  146.4 2.0 collective-permute-start.4
  148.4 2.4 collective-permute-start.5
  150.8 7.3 %units.4 = (bf16[384,1536]{1,0:T(8,128)(2,1)}, bf16[384,1536]{1,0:T(8,128)(2,1)}) custom-call(s32[1]{0:T(128)} %bitcast.4.me_ref, bf16[512,6272]{1,0:T(8,128)(2,1)} %bitcast.6.rows_ref.dy_ref.gate_ref.refs_0_.refs_2_, bf16[512,6272]{1,0:T(8,128)(2,1)} %collective-permute-done.1.refs_1_.refs_3_, ...), custom_call_target="tpu_custom_call" | custom-call | flops 4000000000 | bytes 12000000 | tf_op jit(solution)/shard_map/units/pallas_call | solution.py:315
  158.1 11.3 %input_rows.1 = bf16[512,4224]{1,0:T(8,128)(2,1)} custom-call(bf16[2,512,768]{2,1,0:T(8,128)(2,1)} %get-tuple-element.78.refs_6_.h_ref, bf16[2,4096,768]{2,1,0:T(8,128)(2,1)} %bitcast.25, bf16[512,4224]{1,0:T(8,128)(2,1)} %get-tuple-element.68.into_ref), custom_call_target="tpu_custom_call", output_to_operand_aliasing={{}: (2, {})} | custom-call | flops 12999999488 | bytes 24000000 | tf_op jit(solution)/shard_map/input_rows/pallas_call | solution.py:262
  169.4 4.7 %all-to-all-start.2 = ((bf16[16,32,4224]{2,1,0:T(8,128)(2,1)}), bf16[16,32,4224]{2,1,0:T(8,128)(2,1)}, u32[]{:S(2)}, u32[]{:S(2)}) async-start(bf16[16,32,4224]{2,1,0:T(8,128)(2,1)} %bitcast.27), calls=%async_computation.2 | async-start | bytes 8650752 | tf_op jit(solution)/shard_map/all_to_all | solution.py:398
  174.1 2.9 %collective-permute-done.4 = bf16[384,1536]{1,0:T(8,128)(2,1)S(1)} collective-permute-done((bf16[384,1536]{1,0:T(8,128)(2,1)}, bf16[384,1536]{1,0:T(8,128)(2,1)S(1)}, u32[]{:S(2)}, u32[]{:S(2)}) %collective-permute-start.4) | collective-permute-done | bytes 1179680 | tf_op jit(solution)/shard_map/ppermute | solution.py:379
  177.0 0.0 collective-permute-done.5
  177.0 1.9 add_convert_fusion.4
  178.9 1.3 collective-permute-start.6
  180.2 2.0 collective-permute-start.8
  182.2 11.5 %units.5 = (bf16[384,1536]{1,0:T(8,128)(2,1)}, bf16[384,1536]{1,0:T(8,128)(2,1)}, bf16[384,1536]{1,0:T(8,128)(2,1)}, bf16[384,1536]{1,0:T(8,128)(2,1)}) custom-call(s32[1]{0:T(128)} %bitcast.4.me_ref, bf16[512,6272]{1,0:T(8,128)(2,1)} %bitcast.6.rows_ref.dy_ref.gate_ref.refs_0_.refs_2_, bf16[512,6272]{1,0:T(8,128)(2,1)} %collective-permute-done.1.refs_1_.refs_3_, ...), custom_call_target="tpu_custom_call" | custom-call | flops 4000000000 | bytes 12000000 | tf_op jit(solution)/shard_map/units/pallas_call | solution.py:315
  193.7 13.9 %collective-permute-done.6 = bf16[384,1536]{1,0:T(8,128)(2,1)S(1)} collective-permute-done((bf16[384,1536]{1,0:T(8,128)(2,1)S(1)}, bf16[384,1536]{1,0:T(8,128)(2,1)S(1)}, u32[]{:S(2)}, u32[]{:S(2)}) %collective-permute-start.6) | collective-permute-done | bytes 1179680 | tf_op jit(solution)/shard_map/ppermute | solution.py:379
  207.7 1.6 add_convert_fusion.3
  209.3 0.1 collective-permute-start.7
  209.4 0.0 collective-permute-done.8
  209.4 1.3 add_convert_fusion.2
  210.7 3.2 %collective-permute-start.9 = (bf16[384,1536]{1,0:T(8,128)(2,1)}, bf16[384,1536]{1,0:T(8,128)(2,1)S(1)}, u32[]{:S(2)}, u32[]{:S(2)}) collective-permute-start(bf16[384,1536]{1,0:T(8,128)(2,1)} %add_convert_fusion.2), channel_id=1, source_target_pairs={{0,96},{16,112},{32,0},{48,16},{64,32},{80,48},{96,64},{112,80},{1... | collective-permute-start | bytes 3538952 | tf_op jit(solution)/shard_map/ppermute | solution.py:379
  213.9 25.5 %all-to-all-done.2 = bf16[16,32,4224]{2,1,0:T(8,128)(2,1)} async-done(((bf16[16,32,4224]{2,1,0:T(8,128)(2,1)}), bf16[16,32,4224]{2,1,0:T(8,128)(2,1)}, u32[]{:S(2)}, u32[]{:S(2)}) %all-to-all-start.2) | async-done | bytes 4325408 | tf_op jit(solution)/shard_map/all_to_all | solution.py:398
  239.4 5.0 %unpack.1 = (bf16[128,4096]{1,0:T(8,128)(2,1)}, bf16[2,128]{1,0:T(2,128)(2,1)}) custom-call(bf16[512,128]{1,0:T(8,128)(2,1)} %get-tuple-element.82.hot_ref, bf16[512,4224]{1,0:T(8,128)(2,1)} %bitcast.12.rows_ref.gates_ref, s32[2,128]{1,0:T(2,128)} %bitcast.31, bf16[512,4224]{1,0:T(8,128)(2,1)} %bitcast.12.rows_ref.gates_ref), custom_call_target="tpu_custom_call" | custom-call | flops 1000000000 | bytes 10000000 | tf_op jit(solution)/shard_map/unpack/pallas_call | solution.py:356
  244.5 0.0 collective-permute-done.7
  244.5 0.0 collective-permute-done.9
  244.5 0.3 add_convert_fusion.1
  244.8 0.0 copy-start.5
  244.8 1.7 copy-done.6
  246.5 0.3 add_convert_fusion
  246.8 0.0 slice-start
  246.8 0.1 slice.25
  246.9 1.1 slice-done
  248.0 0.1 pad_maximum_fusion
  248.1 1.3 reshape.43
  249.4 0.9 maximum_bitcast_fusion
  (19 shorter events, 0.1 us)
Async XLA Ops:
  89.1 49.6 %collective-permute-start.1 = (bf16[512,6272]{1,0:T(8,128)(2,1)}, bf16[512,6272]{1,0:T(8,128)(2,1)}, u32[]{:S(2)}, u32[]{:S(2)}) collective-permute-start(bf16[512,6272]{1,0:T(8,128)(2,1)} %bitcast.6.rows_ref.dy_ref.gate_ref.refs_0_.refs_2_), channel_id=1, source_target_pairs={{0,16},{16,0},{32,48},{48,32},{64,80},{80,64},{96,112},{112,96},{1... | collective-permute-start | bytes 19267592 | tf_op jit(solution)/shard_map/ppermute | solution.py:402
  89.1 38.4 %all-to-all-start = ((bf16[16,32,2048]{2,1,0:T(8,128)(2,1)}), bf16[16,32,2048]{2,1,0:T(8,128)(2,1)S(1)}, u32[]{:S(2)}, u32[]{:S(2)}) async-start(bf16[16,32,2048]{2,1,0:T(8,128)(2,1)} %bitcast.28), calls=%async_computation | async-start | bytes 4194304 | tf_op jit(solution)/shard_map/all_to_all | solution.py:398
  100.5 15.5 %copy-start.3 = (bf16[4096,2,1,768]{3,0,1,2:T(8,128)(2,1)}, bf16[4096,2,1,768]{3,0,1,2:T(8,128)(2,1)S(1)}, u32[]{:S(2)}) copy-start(bf16[4096,2,1,768]{3,0,1,2:T(8,128)(2,1)S(1)} %copy.14) | copy-start | bytes 37748740
  116.1 11.5 %collective-permute-start = (bf16[512,768]{1,0:T(8,128)(2,1)}, bf16[512,768]{1,0:T(8,128)(2,1)S(1)}, u32[]{:S(2)}, u32[]{:S(2)}) collective-permute-start(bf16[512,768]{1,0:T(8,128)(2,1)} %get-tuple-element.53.refs_8_), channel_id=1, source_target_pairs={{0,16},{16,0},{32,48},{48,32},{64,80},{80,64},{96,112},{112,96},{1... | collective-permute-start | bytes 2359304 | tf_op jit(solution)/shard_map/ppermute | solution.py:402
  127.6 11.1 %copy-start = (bf16[16,32,2048]{2,1,0:T(8,128)(2,1)}, bf16[16,32,2048]{2,1,0:T(8,128)(2,1)S(1)}, u32[]{:S(2)}) copy-start(bf16[16,32,2048]{2,1,0:T(8,128)(2,1)S(1)} %all-to-all-done) | copy-start | bytes 6291460
  127.6 11.1 %copy-start.4 = (bf16[512,768]{1,0:T(8,128)(2,1)}, bf16[512,768]{1,0:T(8,128)(2,1)S(1)}, u32[]{:S(2)}) copy-start(bf16[512,768]{1,0:T(8,128)(2,1)S(1)} %collective-permute-done.refs_9_) | copy-start | bytes 2359300
  127.6 11.1 %collective-permute-start.2 = (bf16[512,2048]{1,0:T(8,128)(2,1)S(1)}, bf16[512,2048]{1,0:T(8,128)(2,1)S(1)}, u32[]{:S(2)}, u32[]{:S(2)}) collective-permute-start(bf16[512,2048]{1,0:T(8,128)(2,1)S(1)} %bitcast.19), channel_id=1, source_target_pairs={{0,16},{16,0},{32,48},{48,32},{64,80},{80,64},{96,112},{112,96},{1... | collective-permute-start | bytes 6291464 | tf_op jit(solution)/shard_map/ppermute | solution.py:402
  135.0 3.7 %collective-permute-start.3 = (bf16[2,512,768]{2,1,0:T(8,128)(2,1)}, bf16[2,512,768]{2,1,0:T(8,128)(2,1)S(1)}, u32[]{:S(2)}, u32[]{:S(2)}) collective-permute-start(bf16[2,512,768]{2,1,0:T(8,128)(2,1)} %get-tuple-element.78.refs_6_.h_ref), channel_id=1, source_target_pairs={{0,16},{16,0},{32,48},{48,32},{64,80},{80,64},{96,112},{112,96},{1... | collective-permute-start | bytes 4718600 | tf_op jit(solution)/shard_map/ppermute | solution.py:402
  138.7 7.7 %copy-start.2 = (bf16[2,512,768]{2,1,0:T(8,128)(2,1)}, bf16[2,512,768]{2,1,0:T(8,128)(2,1)S(1)}, u32[]{:S(2)}) copy-start(bf16[2,512,768]{2,1,0:T(8,128)(2,1)S(1)} %collective-permute-done.3.refs_7_) | copy-start | bytes 4718596
  138.7 7.7 %copy-start.1 = (bf16[512,2048]{1,0:T(8,128)(2,1)}, bf16[512,2048]{1,0:T(8,128)(2,1)S(1)}, u32[]{:S(2)}) copy-start(bf16[512,2048]{1,0:T(8,128)(2,1)S(1)} %collective-permute-done.2.refs_5_) | copy-start | bytes 6291460
  146.4 30.6 %collective-permute-start.4 = (bf16[384,1536]{1,0:T(8,128)(2,1)}, bf16[384,1536]{1,0:T(8,128)(2,1)S(1)}, u32[]{:S(2)}, u32[]{:S(2)}) collective-permute-start(bf16[384,1536]{1,0:T(8,128)(2,1)} %get-tuple-element.70), channel_id=1, source_target_pairs={{0,32},{16,48},{32,64},{48,80},{64,96},{80,112},{96,0},{112,16},{1... | collective-permute-start | bytes 3538952 | tf_op jit(solution)/shard_map/ppermute | solution.py:379
  148.4 28.6 %collective-permute-start.5 = (bf16[384,1536]{1,0:T(8,128)(2,1)}, bf16[384,1536]{1,0:T(8,128)(2,1)S(1)}, u32[]{:S(2)}, u32[]{:S(2)}) collective-permute-start(bf16[384,1536]{1,0:T(8,128)(2,1)} %get-tuple-element.71), channel_id=1, source_target_pairs={{0,96},{16,112},{32,0},{48,16},{64,32},{80,48},{96,64},{112,80},{1... | collective-permute-start | bytes 3538952 | tf_op jit(solution)/shard_map/ppermute | solution.py:379
  169.4 7.6 %copy-start.9 = (bf16[384,1536]{1,0:T(8,128)(2,1)S(1)}, bf16[384,1536]{1,0:T(8,128)(2,1)}, u32[]{:S(2)}) copy-start(bf16[384,1536]{1,0:T(8,128)(2,1)} %get-tuple-element.74) | copy-start | bytes 3538948
  169.4 70.0 %all-to-all-start.2 = ((bf16[16,32,4224]{2,1,0:T(8,128)(2,1)}), bf16[16,32,4224]{2,1,0:T(8,128)(2,1)}, u32[]{:S(2)}, u32[]{:S(2)}) async-start(bf16[16,32,4224]{2,1,0:T(8,128)(2,1)} %bitcast.27), calls=%async_computation.2 | async-start | bytes 8650752 | tf_op jit(solution)/shard_map/all_to_all | solution.py:398
  178.9 28.8 %collective-permute-start.6 = (bf16[384,1536]{1,0:T(8,128)(2,1)S(1)}, bf16[384,1536]{1,0:T(8,128)(2,1)S(1)}, u32[]{:S(2)}, u32[]{:S(2)}) collective-permute-start(bf16[384,1536]{1,0:T(8,128)(2,1)S(1)} %get-tuple-element.77), channel_id=1, source_target_pairs={{0,32},{16,48},{32,64},{48,80},{64,96},{80,112},{96,0},{112,16},{1... | collective-permute-start | bytes 3538952 | tf_op jit(solution)/shard_map/ppermute | solution.py:379
  180.2 29.2 %collective-permute-start.8 = (bf16[384,1536]{1,0:T(8,128)(2,1)S(1)}, bf16[384,1536]{1,0:T(8,128)(2,1)S(1)}, u32[]{:S(2)}, u32[]{:S(2)}) collective-permute-start(bf16[384,1536]{1,0:T(8,128)(2,1)S(1)} %get-tuple-element.80), channel_id=1, source_target_pairs={{0,96},{16,112},{32,0},{48,16},{64,32},{80,48},{96,64},{112,80},{1... | collective-permute-start | bytes 3538952 | tf_op jit(solution)/shard_map/ppermute | solution.py:379
  207.6 1.8 copy-start.8
  209.3 35.2 %collective-permute-start.7 = (bf16[384,1536]{1,0:T(8,128)(2,1)S(1)}, bf16[384,1536]{1,0:T(8,128)(2,1)S(1)}, u32[]{:S(2)}, u32[]{:S(2)}) collective-permute-start(bf16[384,1536]{1,0:T(8,128)(2,1)S(1)} %add_convert_fusion.3), channel_id=1, source_target_pairs={{0,32},{16,48},{32,64},{48,80},{64,96},{80,112},{96,0},{112,16},{1... | collective-permute-start | bytes 3538952 | tf_op jit(solution)/shard_map/ppermute | solution.py:379
  210.7 33.8 %collective-permute-start.9 = (bf16[384,1536]{1,0:T(8,128)(2,1)}, bf16[384,1536]{1,0:T(8,128)(2,1)S(1)}, u32[]{:S(2)}, u32[]{:S(2)}) collective-permute-start(bf16[384,1536]{1,0:T(8,128)(2,1)} %add_convert_fusion.2), channel_id=1, source_target_pairs={{0,96},{16,112},{32,0},{48,16},{64,32},{80,48},{96,64},{112,80},{1... | collective-permute-start | bytes 3538952 | tf_op jit(solution)/shard_map/ppermute | solution.py:379
  239.4 5.0 %copy-start.7 = (bf16[384,1536]{1,0:T(8,128)(2,1)S(1)}, bf16[384,1536]{1,0:T(8,128)(2,1)}, u32[]{:S(2)}) copy-start(bf16[384,1536]{1,0:T(8,128)(2,1)} %get-tuple-element.87) | copy-start | bytes 3538948
  244.8 2.0 copy-start.5
  244.8 1.7 copy-start.6
  246.8 1.1 slice-start

commit v7 on v6

--- a/solution.py
+++ b/solution.py
@@ -418,12 +418,10 @@
     total = units(*args, h, h_mate, gp, gp_mate, 0, 1)
     h, total = lax.optimization_barrier((h, total))
     total = pass_on(*total)
-    parts = units(*args, h, h_mate, gp, gp_mate, 1, 1)
-    h, parts = lax.optimization_barrier((h, parts))
     rows = input_rows(h, w, 0, width, rows)
     h, rows = lax.optimization_barrier((h, rows))
     back = exchange(rows)
-    total, rows = lax.optimization_barrier((total, rows))
+    parts = units(*args, h, h_mate, gp, gp_mate, 1, 1)
     total = added(total, parts)
     h, total = lax.optimization_barrier((h, total))
     total = pass_on(*total)

time: 251 us -> 242 us (0.964)
  waiting for transfers between devices: 56.8 us -> 50.8 us
  local copies, waits for them, and re-layouts: 11.9 us -> 9.21 us
    all_to_all x2, waiting for transfers between devices: 36.4 us -> 28.7 us  [exchange(): lax.all_to_all(rows.reshape(owners, CAP, wide), 'expert', split_axis=0, c...]
  transfers between devices with their start and end apart: 12 -> 12, of which waited for: 5 -> 7; matrix products, arithmetic and copies ran while one was open for 5% -> 5% of each run, Pallas kernels for 23% -> 24%
where the time goes in v7:
time: 242 us
  blocking collectives  82 us (34%)
  Pallas kernels  72.4 us (30%)
  waiting for transfers between devices  50.8 us (21%)
  starting transfers between devices  19.9 us (8%)
  local copies, waits for them, and re-layouts  9.21 us (4%)
  other arithmetic  6.52 us (3%)
    all_to_all x1, blocking collectives, exchange(): lax.all_to_all(rows.reshape(owners, CAP, wide), 'expert', split_axis=0, c...  82 us
    all_to_all x2, waiting for transfers between devices, exchange(): lax.all_to_all(rows.reshape(owners, CAP, wide), 'expert', split_axis=0, c...  28.7 us
    pallas_call x3, Pallas kernels, units(): pl.pallas_call(units_kernel, grid_spec=pltpu.PrefetchScalarGridSpec(num_s...  26.7 us
    ppermute x6, waiting for transfers between devices, pass_on(): return (lax.ppermute(up, 'dp', UP), lax.ppermute(dn, 'dp', DOWN))  18.5 us
    pallas_call x1, Pallas kernels, pre(): pl.pallas_call(functools.partial(pre_kernel, per=per), grid=(SLICES // pe...  15.5 us
    pallas_call x1, Pallas kernels, input_rows(): pl.pallas_call(input_kernel, grid=(cols // blk,), in_specs=[held((2, slot...  11.2 us
    ppermute x6, starting transfers between devices, pass_on(): return (lax.ppermute(up, 'dp', UP), lax.ppermute(dn, 'dp', DOWN))  10.9 us
    all_to_all x2, starting transfers between devices, exchange(): lax.all_to_all(rows.reshape(owners, CAP, wide), 'expert', split_axis=0, c...  8.25 us
  transfers between devices with their start and end apart: 12, of which 7 were waited for; matrix products, arithmetic and copies ran while one was open for 5% of the time, Pallas kernels for 24%

profile of v7, /device:TPU:0, one launch (start us, length us, event | category | flops | bytes accessed | tf_op | source)
XLA Modules:
  0.0 241.7 jit_solution(459299092941155828)
XLA Ops:
  0.6 6.5 %pack.1 = (bf16[512,6272]{1,0:T(8,128)(2,1)}, bf16[512,2048]{1,0:T(8,128)(2,1)}, bf16[512,128]{1,0:T(8,128)(2,1)}) custom-call(s32[2,128]{1,0:T(2,128)} %bitcast.30, bf16[2,128]{1,0:T(2,128)(2,1)} %bitcast.34, bf16[128,4096]{1,0:T(8,128)(2,1)} %tok_ref.1, bf16[128,4096]{1,0:T(8,128)(2,1)} %dy_ref.1), custom_call_target="tpu_custom_call" | custom-call | flops 3000000000 | bytes 14000000 | tf_op jit(solution)/shard_map/pack/pallas_call | solution.py:95
  7.1 82.0 %all_to_all.15 = bf16[16,32,6272]{2,1,0:T(8,128)(2,1)} all-to-all(bf16[16,32,6272]{2,1,0:T(8,128)(2,1)} %bitcast.26), channel_id=1, replica_groups=mesh['dp'=8,'expert'=16] {'expert'}, dimensions={0} | all-to-all | bytes 12845056 | tf_op jit(solution)/shard_map/all_to_all | solution.py:398
  89.1 0.0 collective-permute-start.1
  89.1 3.7 %all-to-all-start = ((bf16[16,32,2048]{2,1,0:T(8,128)(2,1)}), bf16[16,32,2048]{2,1,0:T(8,128)(2,1)S(1)}, u32[]{:S(2)}, u32[]{:S(2)}) async-start(bf16[16,32,2048]{2,1,0:T(8,128)(2,1)} %bitcast.28), calls=%async_computation | async-start | bytes 4194304 | tf_op jit(solution)/shard_map/all_to_all | solution.py:398
  92.8 7.7 %copy.14 = bf16[4096,2,1,768]{3,0,1,2:T(8,128)(2,1)S(1)} copy(bf16[4096,2,1,768]{3,1,2,0:T(2,128)(2,1)} %param.10) | data formatting | bytes 25165824 | tf_op jit(solution)/shard_map/optimization_barrier | solution.py:406
  100.5 0.0 copy-start.3
  100.5 15.5 %pre.1 = (f32[512,768]{1,0:T(8,128)}, f32[512,768]{1,0:T(8,128)}, f32[512,768]{1,0:T(8,128)}, bf16[512,768]{1,0:T(8,128)(2,1)}, bf16[512,768]{1,0:T(8,128)(2,1)}) custom-call(bf16[512,6272]{1,0:T(8,128)(2,1)} %bitcast.6.rows_ref.dy_ref.gate_ref.refs_0_.refs_2_, bf16[512,6272]{1,0:T(8,128)(2,1)} %bitcast.6.rows_ref.dy_ref.gate_ref.refs_0_.refs_2_, ...), custom_call_target="tpu_custom_call" | custom-call | flops 16999999488 | bytes 40000000 | tf_op jit(solution)/shard_map/pre/pallas_call | solution.py:166
  116.0 0.0 copy-done.3
  116.0 0.6 collective-permute-start
  116.6 10.9 %all-to-all-done = bf16[16,32,2048]{2,1,0:T(8,128)(2,1)S(1)} async-done(((bf16[16,32,2048]{2,1,0:T(8,128)(2,1)}), bf16[16,32,2048]{2,1,0:T(8,128)(2,1)S(1)}, u32[]{:S(2)}, u32[]{:S(2)}) %all-to-all-start) | async-done | bytes 2097184 | tf_op jit(solution)/shard_map/all_to_all | solution.py:398
  127.5 0.0 collective-permute-done.refs_9_
  127.5 0.1 collective-permute-start.2
  127.6 7.3 %hidden.1 = (bf16[2,512,768]{2,1,0:T(8,128)(2,1)}, bf16[512,4224]{1,0:T(8,128)(2,1)}) custom-call(bf16[512,2048]{1,0:T(8,128)(2,1)S(1)} %bitcast.20, bf16[8,2,256,768]{3,2,1,0:T(8,128)(2,1)} %bitcast.33, f32[512,768]{1,0:T(8,128)} %get-tuple-element.50.u_hbm, f32[512,768]{1,0:T(8,128)} %get-tuple-element.51.c1_hbm, f32[512,768]{1,0:T(8,128)} %get-tuple-element.52.c2_hbm, ...), custom_call_target="tpu_custom_call" | custom-call | flops 4000000000 | bytes 14000000 | tf_op jit(solution)/shard_map/hidden/pallas_call | solution.py:231
  135.0 0.1 collective-permute-start.3
  135.1 3.6 %collective-permute-done.3.refs_7_ = bf16[2,512,768]{2,1,0:T(8,128)(2,1)S(1)} collective-permute-done((bf16[2,512,768]{2,1,0:T(8,128)(2,1)}, bf16[2,512,768]{2,1,0:T(8,128)(2,1)S(1)}, u32[]{:S(2)}, u32[]{:S(2)}) %collective-permute-start.3) | collective-permute-done | bytes 1572896 | tf_op jit(solution)/shard_map/ppermute | solution.py:402
  138.7 0.0 collective-permute-done.2.refs_5_
  138.7 0.0 collective-permute-done.1.refs_1_.refs_3_
  138.7 0.0 copy-done
  138.7 7.7 %units.3 = (bf16[384,1536]{1,0:T(8,128)(2,1)}, bf16[384,1536]{1,0:T(8,128)(2,1)}) custom-call(s32[1]{0:T(128)} %bitcast.4.me_ref, bf16[512,6272]{1,0:T(8,128)(2,1)} %bitcast.6.rows_ref.dy_ref.gate_ref.refs_0_.refs_2_, bf16[512,6272]{1,0:T(8,128)(2,1)} %collective-permute-done.1.refs_1_.refs_3_, ...), custom_call_target="tpu_custom_call" | custom-call | flops 4000000000 | bytes 12000000 | tf_op jit(solution)/shard_map/units/pallas_call | solution.py:315
  146.4 2.0 collective-permute-start.4
  148.4 2.4 collective-permute-start.5
  150.8 11.2 %input_rows.1 = bf16[512,4224]{1,0:T(8,128)(2,1)} custom-call(bf16[2,512,768]{2,1,0:T(8,128)(2,1)} %get-tuple-element.67.refs_6_.h_ref, bf16[2,4096,768]{2,1,0:T(8,128)(2,1)} %bitcast.25, bf16[512,4224]{1,0:T(8,128)(2,1)} %get-tuple-element.60.into_ref), custom_call_target="tpu_custom_call", output_to_operand_aliasing={{}: (2, {})} | custom-call | flops 12999999488 | bytes 24000000 | tf_op jit(solution)/shard_map/input_rows/pallas_call | solution.py:262
  162.0 4.5 %all-to-all-start.2 = ((bf16[16,32,4224]{2,1,0:T(8,128)(2,1)}), bf16[16,32,4224]{2,1,0:T(8,128)(2,1)}, u32[]{:S(2)}, u32[]{:S(2)}) async-start(bf16[16,32,4224]{2,1,0:T(8,128)(2,1)} %bitcast.27), calls=%async_computation.2 | async-start | bytes 8650752 | tf_op jit(solution)/shard_map/all_to_all | solution.py:398
  166.6 7.5 %units.4 = (bf16[384,1536]{1,0:T(8,128)(2,1)}, bf16[384,1536]{1,0:T(8,128)(2,1)}) custom-call(s32[1]{0:T(128)} %bitcast.4.me_ref, bf16[512,6272]{1,0:T(8,128)(2,1)} %bitcast.6.rows_ref.dy_ref.gate_ref.refs_0_.refs_2_, bf16[512,6272]{1,0:T(8,128)(2,1)} %collective-permute-done.1.refs_1_.refs_3_, ...), custom_call_target="tpu_custom_call" | custom-call | flops 4000000000 | bytes 12000000 | tf_op jit(solution)/shard_map/units/pallas_call | solution.py:315
  174.0 2.9 %collective-permute-done.4 = bf16[384,1536]{1,0:T(8,128)(2,1)S(1)} collective-permute-done((bf16[384,1536]{1,0:T(8,128)(2,1)}, bf16[384,1536]{1,0:T(8,128)(2,1)S(1)}, u32[]{:S(2)}, u32[]{:S(2)}) %collective-permute-start.4) | collective-permute-done | bytes 1179680 | tf_op jit(solution)/shard_map/ppermute | solution.py:379
  177.0 1.6 add_convert_fusion.5
  178.6 0.0 collective-permute-done.5
  178.7 0.3 add_convert_fusion.4
  178.9 0.1 collective-permute-start.6
  179.0 3.2 %collective-permute-start.8 = (bf16[384,1536]{1,0:T(8,128)(2,1)S(1)}, bf16[384,1536]{1,0:T(8,128)(2,1)S(1)}, u32[]{:S(2)}, u32[]{:S(2)}) collective-permute-start(bf16[384,1536]{1,0:T(8,128)(2,1)S(1)} %add_convert_fusion.4), channel_id=1, source_target_pairs={{0,96},{16,112},{32,0},{48,16},{64,32},{80,48},{96,64},{112,80},{1... | collective-permute-start | bytes 3538952 | tf_op jit(solution)/shard_map/ppermute | solution.py:379
  182.2 11.5 %units.5 = (bf16[384,1536]{1,0:T(8,128)(2,1)}, bf16[384,1536]{1,0:T(8,128)(2,1)}, bf16[384,1536]{1,0:T(8,128)(2,1)}, bf16[384,1536]{1,0:T(8,128)(2,1)}) custom-call(s32[1]{0:T(128)} %bitcast.4.me_ref, bf16[512,6272]{1,0:T(8,128)(2,1)} %bitcast.6.rows_ref.dy_ref.gate_ref.refs_0_.refs_2_, bf16[512,6272]{1,0:T(8,128)(2,1)} %collective-permute-done.1.refs_1_.refs_3_, ...), custom_call_target="tpu_custom_call" | custom-call | flops 4000000000 | bytes 12000000 | tf_op jit(solution)/shard_map/units/pallas_call | solution.py:315
  193.8 14.1 %collective-permute-done.6 = bf16[384,1536]{1,0:T(8,128)(2,1)S(1)} collective-permute-done((bf16[384,1536]{1,0:T(8,128)(2,1)S(1)}, bf16[384,1536]{1,0:T(8,128)(2,1)S(1)}, u32[]{:S(2)}, u32[]{:S(2)}) %collective-permute-start.6) | collective-permute-done | bytes 1179680 | tf_op jit(solution)/shard_map/ppermute | solution.py:379
  207.8 1.6 add_convert_fusion.3
  209.5 0.1 collective-permute-start.7
  209.6 0.0 collective-permute-done.8
  209.6 0.0 copy-done.7
  209.6 1.3 add_convert_fusion.2
  210.9 3.2 %collective-permute-start.9 = (bf16[384,1536]{1,0:T(8,128)(2,1)}, bf16[384,1536]{1,0:T(8,128)(2,1)S(1)}, u32[]{:S(2)}, u32[]{:S(2)}) collective-permute-start(bf16[384,1536]{1,0:T(8,128)(2,1)} %add_convert_fusion.2), channel_id=1, source_target_pairs={{0,96},{16,112},{32,0},{48,16},{64,32},{80,48},{96,64},{112,80},{1... | collective-permute-start | bytes 3538952 | tf_op jit(solution)/shard_map/ppermute | solution.py:379
  214.1 17.8 %all-to-all-done.2 = bf16[16,32,4224]{2,1,0:T(8,128)(2,1)} async-done(((bf16[16,32,4224]{2,1,0:T(8,128)(2,1)}), bf16[16,32,4224]{2,1,0:T(8,128)(2,1)}, u32[]{:S(2)}, u32[]{:S(2)}) %all-to-all-start.2) | async-done | bytes 4325408 | tf_op jit(solution)/shard_map/all_to_all | solution.py:398
  231.9 5.1 %unpack.1 = (bf16[128,4096]{1,0:T(8,128)(2,1)}, bf16[2,128]{1,0:T(2,128)(2,1)}) custom-call(bf16[512,128]{1,0:T(8,128)(2,1)} %get-tuple-element.71.hot_ref, bf16[512,4224]{1,0:T(8,128)(2,1)} %bitcast.12.rows_ref.gates_ref, s32[2,128]{1,0:T(2,128)} %bitcast.31, bf16[512,4224]{1,0:T(8,128)(2,1)} %bitcast.12.rows_ref.gates_ref), custom_call_target="tpu_custom_call" | custom-call | flops 1000000000 | bytes 10000000 | tf_op jit(solution)/shard_map/unpack/pallas_call | solution.py:356
  237.0 0.6 collective-permute-done.7
  237.6 0.9 collective-permute-done.9
  238.5 0.6 add_convert_fusion
  239.1 0.1 slice.25
  239.2 0.1 slice.24
  239.3 0.1 pad_maximum_fusion
  239.4 1.3 reshape.43
  240.7 0.9 maximum_bitcast_fusion
  (16 shorter events, 0.1 us)
Async XLA Ops:
  89.1 49.6 %collective-permute-start.1 = (bf16[512,6272]{1,0:T(8,128)(2,1)}, bf16[512,6272]{1,0:T(8,128)(2,1)}, u32[]{:S(2)}, u32[]{:S(2)}) collective-permute-start(bf16[512,6272]{1,0:T(8,128)(2,1)} %bitcast.6.rows_ref.dy_ref.gate_ref.refs_0_.refs_2_), channel_id=1, source_target_pairs={{0,16},{16,0},{32,48},{48,32},{64,80},{80,64},{96,112},{112,96},{1... | collective-permute-start | bytes 19267592 | tf_op jit(solution)/shard_map/ppermute | solution.py:402
  89.1 38.4 %all-to-all-start = ((bf16[16,32,2048]{2,1,0:T(8,128)(2,1)}), bf16[16,32,2048]{2,1,0:T(8,128)(2,1)S(1)}, u32[]{:S(2)}, u32[]{:S(2)}) async-start(bf16[16,32,2048]{2,1,0:T(8,128)(2,1)} %bitcast.28), calls=%async_computation | async-start | bytes 4194304 | tf_op jit(solution)/shard_map/all_to_all | solution.py:398
  100.5 15.5 %copy-start.3 = (bf16[4096,2,1,768]{3,0,1,2:T(8,128)(2,1)}, bf16[4096,2,1,768]{3,0,1,2:T(8,128)(2,1)S(1)}, u32[]{:S(2)}) copy-start(bf16[4096,2,1,768]{3,0,1,2:T(8,128)(2,1)S(1)} %copy.14) | copy-start | bytes 37748740
  116.0 11.5 %collective-permute-start = (bf16[512,768]{1,0:T(8,128)(2,1)}, bf16[512,768]{1,0:T(8,128)(2,1)S(1)}, u32[]{:S(2)}, u32[]{:S(2)}) collective-permute-start(bf16[512,768]{1,0:T(8,128)(2,1)} %get-tuple-element.48.refs_8_), channel_id=1, source_target_pairs={{0,16},{16,0},{32,48},{48,32},{64,80},{80,64},{96,112},{112,96},{1... | collective-permute-start | bytes 2359304 | tf_op jit(solution)/shard_map/ppermute | solution.py:402
  127.5 11.2 %copy-start = (bf16[16,32,2048]{2,1,0:T(8,128)(2,1)}, bf16[16,32,2048]{2,1,0:T(8,128)(2,1)S(1)}, u32[]{:S(2)}) copy-start(bf16[16,32,2048]{2,1,0:T(8,128)(2,1)S(1)} %all-to-all-done) | copy-start | bytes 6291460
  127.5 11.2 %copy-start.4 = (bf16[512,768]{1,0:T(8,128)(2,1)}, bf16[512,768]{1,0:T(8,128)(2,1)S(1)}, u32[]{:S(2)}) copy-start(bf16[512,768]{1,0:T(8,128)(2,1)S(1)} %collective-permute-done.refs_9_) | copy-start | bytes 2359300
  127.5 11.1 %collective-permute-start.2 = (bf16[512,2048]{1,0:T(8,128)(2,1)S(1)}, bf16[512,2048]{1,0:T(8,128)(2,1)S(1)}, u32[]{:S(2)}, u32[]{:S(2)}) collective-permute-start(bf16[512,2048]{1,0:T(8,128)(2,1)S(1)} %bitcast.19), channel_id=1, source_target_pairs={{0,16},{16,0},{32,48},{48,32},{64,80},{80,64},{96,112},{112,96},{1... | collective-permute-start | bytes 6291464 | tf_op jit(solution)/shard_map/ppermute | solution.py:402
  135.0 3.7 %collective-permute-start.3 = (bf16[2,512,768]{2,1,0:T(8,128)(2,1)}, bf16[2,512,768]{2,1,0:T(8,128)(2,1)S(1)}, u32[]{:S(2)}, u32[]{:S(2)}) collective-permute-start(bf16[2,512,768]{2,1,0:T(8,128)(2,1)} %get-tuple-element.67.refs_6_.h_ref), channel_id=1, source_target_pairs={{0,16},{16,0},{32,48},{48,32},{64,80},{80,64},{96,112},{112,96},{1... | collective-permute-start | bytes 4718600 | tf_op jit(solution)/shard_map/ppermute | solution.py:402
  138.7 7.7 %copy-start.2 = (bf16[2,512,768]{2,1,0:T(8,128)(2,1)}, bf16[2,512,768]{2,1,0:T(8,128)(2,1)S(1)}, u32[]{:S(2)}) copy-start(bf16[2,512,768]{2,1,0:T(8,128)(2,1)S(1)} %collective-permute-done.3.refs_7_) | copy-start | bytes 4718596
  138.7 7.7 %copy-start.1 = (bf16[512,2048]{1,0:T(8,128)(2,1)}, bf16[512,2048]{1,0:T(8,128)(2,1)S(1)}, u32[]{:S(2)}) copy-start(bf16[512,2048]{1,0:T(8,128)(2,1)S(1)} %collective-permute-done.2.refs_5_) | copy-start | bytes 6291460
  146.4 30.6 %collective-permute-start.4 = (bf16[384,1536]{1,0:T(8,128)(2,1)}, bf16[384,1536]{1,0:T(8,128)(2,1)S(1)}, u32[]{:S(2)}, u32[]{:S(2)}) collective-permute-start(bf16[384,1536]{1,0:T(8,128)(2,1)} %get-tuple-element.62), channel_id=1, source_target_pairs={{0,32},{16,48},{32,64},{48,80},{64,96},{80,112},{96,0},{112,16},{1... | collective-permute-start | bytes 3538952 | tf_op jit(solution)/shard_map/ppermute | solution.py:379
  148.4 30.2 %collective-permute-start.5 = (bf16[384,1536]{1,0:T(8,128)(2,1)}, bf16[384,1536]{1,0:T(8,128)(2,1)S(1)}, u32[]{:S(2)}, u32[]{:S(2)}) collective-permute-start(bf16[384,1536]{1,0:T(8,128)(2,1)} %get-tuple-element.64), channel_id=1, source_target_pairs={{0,96},{16,112},{32,0},{48,16},{64,32},{80,48},{96,64},{112,80},{1... | collective-permute-start | bytes 3538952 | tf_op jit(solution)/shard_map/ppermute | solution.py:379
  162.0 69.9 %all-to-all-start.2 = ((bf16[16,32,4224]{2,1,0:T(8,128)(2,1)}), bf16[16,32,4224]{2,1,0:T(8,128)(2,1)}, u32[]{:S(2)}, u32[]{:S(2)}) async-start(bf16[16,32,4224]{2,1,0:T(8,128)(2,1)} %bitcast.27), calls=%async_computation.2 | async-start | bytes 8650752 | tf_op jit(solution)/shard_map/all_to_all | solution.py:398
  177.0 1.7 copy-start.8
  178.9 28.9 %collective-permute-start.6 = (bf16[384,1536]{1,0:T(8,128)(2,1)S(1)}, bf16[384,1536]{1,0:T(8,128)(2,1)S(1)}, u32[]{:S(2)}, u32[]{:S(2)}) collective-permute-start(bf16[384,1536]{1,0:T(8,128)(2,1)S(1)} %add_convert_fusion.5), channel_id=1, source_target_pairs={{0,32},{16,48},{32,64},{48,80},{64,96},{80,112},{96,0},{112,16},{1... | collective-permute-start | bytes 3538952 | tf_op jit(solution)/shard_map/ppermute | solution.py:379
  179.0 30.5 %collective-permute-start.8 = (bf16[384,1536]{1,0:T(8,128)(2,1)S(1)}, bf16[384,1536]{1,0:T(8,128)(2,1)S(1)}, u32[]{:S(2)}, u32[]{:S(2)}) collective-permute-start(bf16[384,1536]{1,0:T(8,128)(2,1)S(1)} %add_convert_fusion.4), channel_id=1, source_target_pairs={{0,96},{16,112},{32,0},{48,16},{64,32},{80,48},{96,64},{112,80},{1... | collective-permute-start | bytes 3538952 | tf_op jit(solution)/shard_map/ppermute | solution.py:379
  207.8 1.8 copy-start.7
  209.5 28.1 %collective-permute-start.7 = (bf16[384,1536]{1,0:T(8,128)(2,1)S(1)}, bf16[384,1536]{1,0:T(8,128)(2,1)S(1)}, u32[]{:S(2)}, u32[]{:S(2)}) collective-permute-start(bf16[384,1536]{1,0:T(8,128)(2,1)S(1)} %add_convert_fusion.3), channel_id=1, source_target_pairs={{0,32},{16,48},{32,64},{48,80},{64,96},{80,112},{96,0},{112,16},{1... | collective-permute-start | bytes 3538952 | tf_op jit(solution)/shard_map/ppermute | solution.py:379
  210.9 27.6 %collective-permute-start.9 = (bf16[384,1536]{1,0:T(8,128)(2,1)}, bf16[384,1536]{1,0:T(8,128)(2,1)S(1)}, u32[]{:S(2)}, u32[]{:S(2)}) collective-permute-start(bf16[384,1536]{1,0:T(8,128)(2,1)} %add_convert_fusion.2), channel_id=1, source_target_pairs={{0,96},{16,112},{32,0},{48,16},{64,32},{80,48},{96,64},{112,80},{1... | collective-permute-start | bytes 3538952 | tf_op jit(solution)/shard_map/ppermute | solution.py:379
  231.9 6.6 %copy-start.5 = (bf16[384,1536]{1,0:T(8,128)(2,1)S(1)}, bf16[384,1536]{1,0:T(8,128)(2,1)}, u32[]{:S(2)}) copy-start(bf16[384,1536]{1,0:T(8,128)(2,1)} %get-tuple-element.77) | copy-start | bytes 3538948
  231.9 6.6 %copy-start.6 = (bf16[384,1536]{1,0:T(8,128)(2,1)S(1)}, bf16[384,1536]{1,0:T(8,128)(2,1)}, u32[]{:S(2)}) copy-start(bf16[384,1536]{1,0:T(8,128)(2,1)} %get-tuple-element.79) | copy-start | bytes 3538948

commit v8 on v7

--- a/solution.py
+++ b/solution.py
@@ -19,7 +19,7 @@
 LANES = 128
 PACK_STEPS = 2
 PRE_PER = 2
-INPUT_BLOCK = 1024
+INPUT_BLOCK = 2048
 
 
 def params(mib):
@@ -207,7 +207,7 @@
     u_acc[...] += dot_nn(dy[:, depth:], wd[half:].reshape(depth, wd.shape[2]))
     for copy in copies[4:]:
         copy.wait()
-    chunk = 32
+    chunk = 64
 
     def one(i, carry):
         at = pl.ds(pl.multiple_of(i * chunk, chunk), chunk)

time: 242 us -> 242 us (level)
  no operation moved by 1% of the time
where the time goes in v8:
time: 242 us
  blocking collectives  82 us (34%)
  Pallas kernels  72.6 us (30%)
  waiting for transfers between devices  50.5 us (21%)
  starting transfers between devices  19.9 us (8%)
  local copies, waits for them, and re-layouts  9.21 us (4%)
  other arithmetic  6.52 us (3%)
    all_to_all x1, blocking collectives, exchange(): lax.all_to_all(rows.reshape(owners, CAP, wide), 'expert', split_axis=0, c...  82 us
    all_to_all x2, waiting for transfers between devices, exchange(): lax.all_to_all(rows.reshape(owners, CAP, wide), 'expert', split_axis=0, c...  29 us
    pallas_call x3, Pallas kernels, units(): pl.pallas_call(units_kernel, grid_spec=pltpu.PrefetchScalarGridSpec(num_s...  26.7 us
    ppermute x6, waiting for transfers between devices, pass_on(): return (lax.ppermute(up, 'dp', UP), lax.ppermute(dn, 'dp', DOWN))  18 us
    pallas_call x1, Pallas kernels, pre(): pl.pallas_call(functools.partial(pre_kernel, per=per), grid=(SLICES // pe...  15.5 us
    pallas_call x1, Pallas kernels, input_rows(): pl.pallas_call(input_kernel, grid=(cols // blk,), in_specs=[held((2, slot...  11.5 us
    ppermute x6, starting transfers between devices, pass_on(): return (lax.ppermute(up, 'dp', UP), lax.ppermute(dn, 'dp', DOWN))  10.9 us
    all_to_all x2, starting transfers between devices, exchange(): lax.all_to_all(rows.reshape(owners, CAP, wide), 'expert', split_axis=0, c...  8.25 us
  transfers between devices with their start and end apart: 12, of which 7 were waited for; matrix products, arithmetic and copies ran while one was open for 5% of the time, Pallas kernels for 24%

profile of v8, /device:TPU:0, one launch (start us, length us, event | category | flops | bytes accessed | tf_op | source)
XLA Modules:
  0.0 241.6 jit_solution(12325451569569784753)
XLA Ops:
  0.6 6.5 %pack.1 = (bf16[512,6272]{1,0:T(8,128)(2,1)}, bf16[512,2048]{1,0:T(8,128)(2,1)}, bf16[512,128]{1,0:T(8,128)(2,1)}) custom-call(s32[2,128]{1,0:T(2,128)} %bitcast.30, bf16[2,128]{1,0:T(2,128)(2,1)} %bitcast.34, bf16[128,4096]{1,0:T(8,128)(2,1)} %tok_ref.1, bf16[128,4096]{1,0:T(8,128)(2,1)} %dy_ref.1), custom_call_target="tpu_custom_call" | custom-call | flops 3000000000 | bytes 14000000 | tf_op jit(solution)/shard_map/pack/pallas_call | solution.py:95
  7.1 82.0 %all_to_all.15 = bf16[16,32,6272]{2,1,0:T(8,128)(2,1)} all-to-all(bf16[16,32,6272]{2,1,0:T(8,128)(2,1)} %bitcast.26), channel_id=1, replica_groups=mesh['dp'=8,'expert'=16] {'expert'}, dimensions={0} | all-to-all | bytes 12845056 | tf_op jit(solution)/shard_map/all_to_all | solution.py:398
  89.1 0.0 collective-permute-start.1
  89.1 3.7 %all-to-all-start = ((bf16[16,32,2048]{2,1,0:T(8,128)(2,1)}), bf16[16,32,2048]{2,1,0:T(8,128)(2,1)S(1)}, u32[]{:S(2)}, u32[]{:S(2)}) async-start(bf16[16,32,2048]{2,1,0:T(8,128)(2,1)} %bitcast.28), calls=%async_computation | async-start | bytes 4194304 | tf_op jit(solution)/shard_map/all_to_all | solution.py:398
  92.8 7.7 %copy.14 = bf16[4096,2,1,768]{3,0,1,2:T(8,128)(2,1)S(1)} copy(bf16[4096,2,1,768]{3,1,2,0:T(2,128)(2,1)} %param.10) | data formatting | bytes 25165824 | tf_op jit(solution)/shard_map/optimization_barrier | solution.py:406
  100.5 0.0 copy-start.3
  100.5 15.5 %pre.1 = (f32[512,768]{1,0:T(8,128)}, f32[512,768]{1,0:T(8,128)}, f32[512,768]{1,0:T(8,128)}, bf16[512,768]{1,0:T(8,128)(2,1)}, bf16[512,768]{1,0:T(8,128)(2,1)}) custom-call(bf16[512,6272]{1,0:T(8,128)(2,1)} %bitcast.6.rows_ref.dy_ref.gate_ref.refs_0_.refs_2_, bf16[512,6272]{1,0:T(8,128)(2,1)} %bitcast.6.rows_ref.dy_ref.gate_ref.refs_0_.refs_2_, ...), custom_call_target="tpu_custom_call" | custom-call | flops 16999999488 | bytes 40000000 | tf_op jit(solution)/shard_map/pre/pallas_call | solution.py:166
  116.0 0.0 copy-done.3
  116.0 0.6 collective-permute-start
  116.6 10.9 %all-to-all-done = bf16[16,32,2048]{2,1,0:T(8,128)(2,1)S(1)} async-done(((bf16[16,32,2048]{2,1,0:T(8,128)(2,1)}), bf16[16,32,2048]{2,1,0:T(8,128)(2,1)S(1)}, u32[]{:S(2)}, u32[]{:S(2)}) %all-to-all-start) | async-done | bytes 2097184 | tf_op jit(solution)/shard_map/all_to_all | solution.py:398
  127.5 0.0 collective-permute-done.refs_9_
  127.5 0.1 collective-permute-start.2
  127.6 7.3 %hidden.1 = (bf16[2,512,768]{2,1,0:T(8,128)(2,1)}, bf16[512,4224]{1,0:T(8,128)(2,1)}) custom-call(bf16[512,2048]{1,0:T(8,128)(2,1)S(1)} %bitcast.20, bf16[8,2,256,768]{3,2,1,0:T(8,128)(2,1)} %bitcast.33, f32[512,768]{1,0:T(8,128)} %get-tuple-element.50.u_hbm, f32[512,768]{1,0:T(8,128)} %get-tuple-element.51.c1_hbm, f32[512,768]{1,0:T(8,128)} %get-tuple-element.52.c2_hbm, ...), custom_call_target="tpu_custom_call" | custom-call | flops 4000000000 | bytes 14000000 | tf_op jit(solution)/shard_map/hidden/pallas_call | solution.py:231
  134.9 0.1 collective-permute-start.3
  135.0 3.6 %collective-permute-done.3.refs_7_ = bf16[2,512,768]{2,1,0:T(8,128)(2,1)S(1)} collective-permute-done((bf16[2,512,768]{2,1,0:T(8,128)(2,1)}, bf16[2,512,768]{2,1,0:T(8,128)(2,1)S(1)}, u32[]{:S(2)}, u32[]{:S(2)}) %collective-permute-start.3) | collective-permute-done | bytes 1572896 | tf_op jit(solution)/shard_map/ppermute | solution.py:402
  138.6 0.0 collective-permute-done.2.refs_5_
  138.6 0.0 collective-permute-done.1.refs_1_.refs_3_
  138.7 7.7 %units.3 = (bf16[384,1536]{1,0:T(8,128)(2,1)}, bf16[384,1536]{1,0:T(8,128)(2,1)}) custom-call(s32[1]{0:T(128)} %bitcast.4.me_ref, bf16[512,6272]{1,0:T(8,128)(2,1)} %bitcast.6.rows_ref.dy_ref.gate_ref.refs_0_.refs_2_, bf16[512,6272]{1,0:T(8,128)(2,1)} %collective-permute-done.1.refs_1_.refs_3_, ...), custom_call_target="tpu_custom_call" | custom-call | flops 4000000000 | bytes 12000000 | tf_op jit(solution)/shard_map/units/pallas_call | solution.py:315
  146.3 2.0 collective-permute-start.4
  148.3 2.4 collective-permute-start.5
  150.7 11.5 %input_rows.1 = bf16[512,4224]{1,0:T(8,128)(2,1)} custom-call(bf16[2,512,768]{2,1,0:T(8,128)(2,1)} %get-tuple-element.67.refs_6_.h_ref, bf16[2,4096,768]{2,1,0:T(8,128)(2,1)} %bitcast.25, bf16[512,4224]{1,0:T(8,128)(2,1)} %get-tuple-element.60.into_ref), custom_call_target="tpu_custom_call", output_to_operand_aliasing={{}: (2, {})} | custom-call | flops 12999999488 | bytes 24000000 | tf_op jit(solution)/shard_map/input_rows/pallas_call | solution.py:262
  162.2 4.5 %all-to-all-start.2 = ((bf16[16,32,4224]{2,1,0:T(8,128)(2,1)}), bf16[16,32,4224]{2,1,0:T(8,128)(2,1)}, u32[]{:S(2)}, u32[]{:S(2)}) async-start(bf16[16,32,4224]{2,1,0:T(8,128)(2,1)} %bitcast.27), calls=%async_computation.2 | async-start | bytes 8650752 | tf_op jit(solution)/shard_map/all_to_all | solution.py:398
  166.8 7.5 %units.4 = (bf16[384,1536]{1,0:T(8,128)(2,1)}, bf16[384,1536]{1,0:T(8,128)(2,1)}) custom-call(s32[1]{0:T(128)} %bitcast.4.me_ref, bf16[512,6272]{1,0:T(8,128)(2,1)} %bitcast.6.rows_ref.dy_ref.gate_ref.refs_0_.refs_2_, bf16[512,6272]{1,0:T(8,128)(2,1)} %collective-permute-done.1.refs_1_.refs_3_, ...), custom_call_target="tpu_custom_call" | custom-call | flops 4000000000 | bytes 12000000 | tf_op jit(solution)/shard_map/units/pallas_call | solution.py:315
  174.3 2.7 %collective-permute-done.4 = bf16[384,1536]{1,0:T(8,128)(2,1)S(1)} collective-permute-done((bf16[384,1536]{1,0:T(8,128)(2,1)}, bf16[384,1536]{1,0:T(8,128)(2,1)S(1)}, u32[]{:S(2)}, u32[]{:S(2)}) %collective-permute-start.4) | collective-permute-done | bytes 1179680 | tf_op jit(solution)/shard_map/ppermute | solution.py:379
  176.9 1.6 add_convert_fusion.5
  178.6 0.0 collective-permute-done.5
  178.6 0.0 copy-done.8
  178.6 0.3 add_convert_fusion.4
  178.9 0.1 collective-permute-start.6
  179.0 3.2 %collective-permute-start.8 = (bf16[384,1536]{1,0:T(8,128)(2,1)S(1)}, bf16[384,1536]{1,0:T(8,128)(2,1)S(1)}, u32[]{:S(2)}, u32[]{:S(2)}) collective-permute-start(bf16[384,1536]{1,0:T(8,128)(2,1)S(1)} %add_convert_fusion.4), channel_id=1, source_target_pairs={{0,96},{16,112},{32,0},{48,16},{64,32},{80,48},{96,64},{112,80},{1... | collective-permute-start | bytes 3538952 | tf_op jit(solution)/shard_map/ppermute | solution.py:379
  182.2 11.5 %units.5 = (bf16[384,1536]{1,0:T(8,128)(2,1)}, bf16[384,1536]{1,0:T(8,128)(2,1)}, bf16[384,1536]{1,0:T(8,128)(2,1)}, bf16[384,1536]{1,0:T(8,128)(2,1)}) custom-call(s32[1]{0:T(128)} %bitcast.4.me_ref, bf16[512,6272]{1,0:T(8,128)(2,1)} %bitcast.6.rows_ref.dy_ref.gate_ref.refs_0_.refs_2_, bf16[512,6272]{1,0:T(8,128)(2,1)} %collective-permute-done.1.refs_1_.refs_3_, ...), custom_call_target="tpu_custom_call" | custom-call | flops 4000000000 | bytes 12000000 | tf_op jit(solution)/shard_map/units/pallas_call | solution.py:315
  193.7 14.1 %collective-permute-done.6 = bf16[384,1536]{1,0:T(8,128)(2,1)S(1)} collective-permute-done((bf16[384,1536]{1,0:T(8,128)(2,1)S(1)}, bf16[384,1536]{1,0:T(8,128)(2,1)S(1)}, u32[]{:S(2)}, u32[]{:S(2)}) %collective-permute-start.6) | collective-permute-done | bytes 1179680 | tf_op jit(solution)/shard_map/ppermute | solution.py:379
  207.8 1.6 add_convert_fusion.3
  209.4 0.1 collective-permute-start.7
  209.5 0.0 collective-permute-done.8
  209.5 1.3 add_convert_fusion.2
  210.8 3.2 %collective-permute-start.9 = (bf16[384,1536]{1,0:T(8,128)(2,1)}, bf16[384,1536]{1,0:T(8,128)(2,1)S(1)}, u32[]{:S(2)}, u32[]{:S(2)}) collective-permute-start(bf16[384,1536]{1,0:T(8,128)(2,1)} %add_convert_fusion.2), channel_id=1, source_target_pairs={{0,96},{16,112},{32,0},{48,16},{64,32},{80,48},{96,64},{112,80},{1... | collective-permute-start | bytes 3538952 | tf_op jit(solution)/shard_map/ppermute | solution.py:379
  214.0 18.1 %all-to-all-done.2 = bf16[16,32,4224]{2,1,0:T(8,128)(2,1)} async-done(((bf16[16,32,4224]{2,1,0:T(8,128)(2,1)}), bf16[16,32,4224]{2,1,0:T(8,128)(2,1)}, u32[]{:S(2)}, u32[]{:S(2)}) %all-to-all-start.2) | async-done | bytes 4325408 | tf_op jit(solution)/shard_map/all_to_all | solution.py:398
  232.1 5.1 %unpack.1 = (bf16[128,4096]{1,0:T(8,128)(2,1)}, bf16[2,128]{1,0:T(2,128)(2,1)}) custom-call(bf16[512,128]{1,0:T(8,128)(2,1)} %get-tuple-element.71.hot_ref, bf16[512,4224]{1,0:T(8,128)(2,1)} %bitcast.12.rows_ref.gates_ref, s32[2,128]{1,0:T(2,128)} %bitcast.31, bf16[512,4224]{1,0:T(8,128)(2,1)} %bitcast.12.rows_ref.gates_ref), custom_call_target="tpu_custom_call" | custom-call | flops 1000000000 | bytes 10000000 | tf_op jit(solution)/shard_map/unpack/pallas_call | solution.py:356
  237.2 0.3 collective-permute-done.7
  237.5 0.9 collective-permute-done.9
  238.4 0.0 copy-done.5
  238.4 0.6 add_convert_fusion
  239.1 0.1 slice.25
  239.2 0.1 slice.24
  239.2 0.1 pad_maximum_fusion
  239.3 1.3 reshape.43
  240.7 0.9 maximum_bitcast_fusion
  (16 shorter events, 0.1 us)
Async XLA Ops:
  89.1 49.5 %collective-permute-start.1 = (bf16[512,6272]{1,0:T(8,128)(2,1)}, bf16[512,6272]{1,0:T(8,128)(2,1)}, u32[]{:S(2)}, u32[]{:S(2)}) collective-permute-start(bf16[512,6272]{1,0:T(8,128)(2,1)} %bitcast.6.rows_ref.dy_ref.gate_ref.refs_0_.refs_2_), channel_id=1, source_target_pairs={{0,16},{16,0},{32,48},{48,32},{64,80},{80,64},{96,112},{112,96},{1... | collective-permute-start | bytes 19267592 | tf_op jit(solution)/shard_map/ppermute | solution.py:402
  89.1 38.4 %all-to-all-start = ((bf16[16,32,2048]{2,1,0:T(8,128)(2,1)}), bf16[16,32,2048]{2,1,0:T(8,128)(2,1)S(1)}, u32[]{:S(2)}, u32[]{:S(2)}) async-start(bf16[16,32,2048]{2,1,0:T(8,128)(2,1)} %bitcast.28), calls=%async_computation | async-start | bytes 4194304 | tf_op jit(solution)/shard_map/all_to_all | solution.py:398
  100.5 15.5 %copy-start.3 = (bf16[4096,2,1,768]{3,0,1,2:T(8,128)(2,1)}, bf16[4096,2,1,768]{3,0,1,2:T(8,128)(2,1)S(1)}, u32[]{:S(2)}) copy-start(bf16[4096,2,1,768]{3,0,1,2:T(8,128)(2,1)S(1)} %copy.14) | copy-start | bytes 37748740
  116.0 11.5 %collective-permute-start = (bf16[512,768]{1,0:T(8,128)(2,1)}, bf16[512,768]{1,0:T(8,128)(2,1)S(1)}, u32[]{:S(2)}, u32[]{:S(2)}) collective-permute-start(bf16[512,768]{1,0:T(8,128)(2,1)} %get-tuple-element.48.refs_8_), channel_id=1, source_target_pairs={{0,16},{16,0},{32,48},{48,32},{64,80},{80,64},{96,112},{112,96},{1... | collective-permute-start | bytes 2359304 | tf_op jit(solution)/shard_map/ppermute | solution.py:402
  127.5 11.1 %copy-start = (bf16[16,32,2048]{2,1,0:T(8,128)(2,1)}, bf16[16,32,2048]{2,1,0:T(8,128)(2,1)S(1)}, u32[]{:S(2)}) copy-start(bf16[16,32,2048]{2,1,0:T(8,128)(2,1)S(1)} %all-to-all-done) | copy-start | bytes 6291460
  127.5 11.1 %copy-start.4 = (bf16[512,768]{1,0:T(8,128)(2,1)}, bf16[512,768]{1,0:T(8,128)(2,1)S(1)}, u32[]{:S(2)}) copy-start(bf16[512,768]{1,0:T(8,128)(2,1)S(1)} %collective-permute-done.refs_9_) | copy-start | bytes 2359300
  127.5 11.1 %collective-permute-start.2 = (bf16[512,2048]{1,0:T(8,128)(2,1)S(1)}, bf16[512,2048]{1,0:T(8,128)(2,1)S(1)}, u32[]{:S(2)}, u32[]{:S(2)}) collective-permute-start(bf16[512,2048]{1,0:T(8,128)(2,1)S(1)} %bitcast.19), channel_id=1, source_target_pairs={{0,16},{16,0},{32,48},{48,32},{64,80},{80,64},{96,112},{112,96},{1... | collective-permute-start | bytes 6291464 | tf_op jit(solution)/shard_map/ppermute | solution.py:402
  134.9 3.7 %collective-permute-start.3 = (bf16[2,512,768]{2,1,0:T(8,128)(2,1)}, bf16[2,512,768]{2,1,0:T(8,128)(2,1)S(1)}, u32[]{:S(2)}, u32[]{:S(2)}) collective-permute-start(bf16[2,512,768]{2,1,0:T(8,128)(2,1)} %get-tuple-element.67.refs_6_.h_ref), channel_id=1, source_target_pairs={{0,16},{16,0},{32,48},{48,32},{64,80},{80,64},{96,112},{112,96},{1... | collective-permute-start | bytes 4718600 | tf_op jit(solution)/shard_map/ppermute | solution.py:402
  138.6 7.7 %copy-start.2 = (bf16[2,512,768]{2,1,0:T(8,128)(2,1)}, bf16[2,512,768]{2,1,0:T(8,128)(2,1)S(1)}, u32[]{:S(2)}) copy-start(bf16[2,512,768]{2,1,0:T(8,128)(2,1)S(1)} %collective-permute-done.3.refs_7_) | copy-start | bytes 4718596
  138.6 7.7 %copy-start.1 = (bf16[512,2048]{1,0:T(8,128)(2,1)}, bf16[512,2048]{1,0:T(8,128)(2,1)S(1)}, u32[]{:S(2)}) copy-start(bf16[512,2048]{1,0:T(8,128)(2,1)S(1)} %collective-permute-done.2.refs_5_) | copy-start | bytes 6291460
  146.3 30.6 %collective-permute-start.4 = (bf16[384,1536]{1,0:T(8,128)(2,1)}, bf16[384,1536]{1,0:T(8,128)(2,1)S(1)}, u32[]{:S(2)}, u32[]{:S(2)}) collective-permute-start(bf16[384,1536]{1,0:T(8,128)(2,1)} %get-tuple-element.62), channel_id=1, source_target_pairs={{0,32},{16,48},{32,64},{48,80},{64,96},{80,112},{96,0},{112,16},{1... | collective-permute-start | bytes 3538952 | tf_op jit(solution)/shard_map/ppermute | solution.py:379
  148.3 30.2 %collective-permute-start.5 = (bf16[384,1536]{1,0:T(8,128)(2,1)}, bf16[384,1536]{1,0:T(8,128)(2,1)S(1)}, u32[]{:S(2)}, u32[]{:S(2)}) collective-permute-start(bf16[384,1536]{1,0:T(8,128)(2,1)} %get-tuple-element.64), channel_id=1, source_target_pairs={{0,96},{16,112},{32,0},{48,16},{64,32},{80,48},{96,64},{112,80},{1... | collective-permute-start | bytes 3538952 | tf_op jit(solution)/shard_map/ppermute | solution.py:379
  162.2 69.9 %all-to-all-start.2 = ((bf16[16,32,4224]{2,1,0:T(8,128)(2,1)}), bf16[16,32,4224]{2,1,0:T(8,128)(2,1)}, u32[]{:S(2)}, u32[]{:S(2)}) async-start(bf16[16,32,4224]{2,1,0:T(8,128)(2,1)} %bitcast.27), calls=%async_computation.2 | async-start | bytes 8650752 | tf_op jit(solution)/shard_map/all_to_all | solution.py:398
  176.9 1.7 copy-start.8
  178.9 28.9 %collective-permute-start.6 = (bf16[384,1536]{1,0:T(8,128)(2,1)S(1)}, bf16[384,1536]{1,0:T(8,128)(2,1)S(1)}, u32[]{:S(2)}, u32[]{:S(2)}) collective-permute-start(bf16[384,1536]{1,0:T(8,128)(2,1)S(1)} %add_convert_fusion.5), channel_id=1, source_target_pairs={{0,32},{16,48},{32,64},{48,80},{64,96},{80,112},{96,0},{112,16},{1... | collective-permute-start | bytes 3538952 | tf_op jit(solution)/shard_map/ppermute | solution.py:379
  179.0 30.5 %collective-permute-start.8 = (bf16[384,1536]{1,0:T(8,128)(2,1)S(1)}, bf16[384,1536]{1,0:T(8,128)(2,1)S(1)}, u32[]{:S(2)}, u32[]{:S(2)}) collective-permute-start(bf16[384,1536]{1,0:T(8,128)(2,1)S(1)} %add_convert_fusion.4), channel_id=1, source_target_pairs={{0,96},{16,112},{32,0},{48,16},{64,32},{80,48},{96,64},{112,80},{1... | collective-permute-start | bytes 3538952 | tf_op jit(solution)/shard_map/ppermute | solution.py:379
  207.8 1.8 copy-start.7
  209.4 28.1 %collective-permute-start.7 = (bf16[384,1536]{1,0:T(8,128)(2,1)S(1)}, bf16[384,1536]{1,0:T(8,128)(2,1)S(1)}, u32[]{:S(2)}, u32[]{:S(2)}) collective-permute-start(bf16[384,1536]{1,0:T(8,128)(2,1)S(1)} %add_convert_fusion.3), channel_id=1, source_target_pairs={{0,32},{16,48},{32,64},{48,80},{64,96},{80,112},{96,0},{112,16},{1... | collective-permute-start | bytes 3538952 | tf_op jit(solution)/shard_map/ppermute | solution.py:379
  210.8 27.6 %collective-permute-start.9 = (bf16[384,1536]{1,0:T(8,128)(2,1)}, bf16[384,1536]{1,0:T(8,128)(2,1)S(1)}, u32[]{:S(2)}, u32[]{:S(2)}) collective-permute-start(bf16[384,1536]{1,0:T(8,128)(2,1)} %add_convert_fusion.2), channel_id=1, source_target_pairs={{0,96},{16,112},{32,0},{48,16},{64,32},{80,48},{96,64},{112,80},{1... | collective-permute-start | bytes 3538952 | tf_op jit(solution)/shard_map/ppermute | solution.py:379
  232.1 6.3 %copy-start.5 = (bf16[384,1536]{1,0:T(8,128)(2,1)S(1)}, bf16[384,1536]{1,0:T(8,128)(2,1)}, u32[]{:S(2)}) copy-start(bf16[384,1536]{1,0:T(8,128)(2,1)} %get-tuple-element.77) | copy-start | bytes 3538948
  232.1 6.3 %copy-start.6 = (bf16[384,1536]{1,0:T(8,128)(2,1)S(1)}, bf16[384,1536]{1,0:T(8,128)(2,1)}, u32[]{:S(2)}) copy-start(bf16[384,1536]{1,0:T(8,128)(2,1)} %get-tuple-element.79) | copy-start | bytes 3538948
